TPU v7x, 32 devices: a whole 2x2x4 slice. The times are simulated.
32 devices in a mesh: series: 2 (over y), ta: 4 (over z), pb: 4 (over x, core).
Axes of the slice: x: 2, y: 2, z: 4, core: 2. Of those that a mesh axis runs over, the one named last changes fastest.
Arguments:
- blocks: bfloat16 [8, 4, 4, 32, 128, 128], P(('series', 'ta'), 'pb'), parts along dimension 0, may hold values from -6 to 6
- qz_factor: bfloat16 [2048, 256], P(('series', 'ta')), parts along dimension 0, may hold values from -0.5 to 0.5
- qy_factor: bfloat16 [2048, 256], P(('series', 'ta')), parts along dimension 0, may hold values from -0.5 to 0.5
- block_owner: int32 [8, 4, 4], P(('series', 'ta'), 'pb'), parts along dimension 0, may hold values from -1 to 3, as said below
- block_cells: int32 [8, 4, 4, 2], P(('series', 'ta'), 'pb'), parts along dimension 0, may hold values from 0 to 7, as said below
Outputs:
- frame_factor: float32 [1024, 256], P(('series', 'ta', 'pb')), parts along dimension 0
- slot_misfit: float32 [8, 4, 4], P(('series', 'ta'), 'pb'), parts along dimension 0
There are 2 independent parts, one for each index of `series`. A program takes and returns all parts, laid end to end along the dimension named above; each array names one. Nothing has to cross between parts.
Inputs may be any that keep to these rules, and one draw needn't show every extreme that they name: `block_owner`: the slots of device index p along pb hold only frame blocks u * 4 + p. No two live slots of one frame block share the same pair of cells. Every frame block has at least one live slot, and some slot is empty. `block_cells`: each entry is a block index below 8.
All inputs are finite; a program needn't handle non-finite values.
Results may differ from a plain program's by a relative error of at most 0.0003.
Values may be sent and summed in bfloat16 or wider, within the bound.
No kernel may reach another device: no remote copies, remote signals or barrier semaphores. Data moves between devices by JAX's collectives and lax.ppermute only.
A program may use at most 64 MiB of HBM per device.

v0:
```python
import jax
import jax.numpy as jnp
from jax import lax
from jax.sharding import PartitionSpec as P

ridge_weight = 0.1
top_precision = lax.Precision.HIGHEST


def solve_rows(rhs_rows, system):
    lower_factor = jnp.linalg.cholesky(system)
    halfway = lax.linalg.triangular_solve(
        lower_factor, rhs_rows, left_side=False, lower=True, transpose_a=True
    )
    return lax.linalg.triangular_solve(
        lower_factor, halfway, left_side=False, lower=True, transpose_a=False
    )


def body(blocks, qz_factor, qy_factor, block_owner, block_cells):
    ta_count = lax.axis_size("ta")
    slot_total = blocks.shape[2]
    frames = blocks.shape[3]
    block_edge = blocks.shape[4]
    rank_cols = qz_factor.shape[1]
    block_data = blocks.reshape(slot_total, frames, block_edge, block_edge)
    slot_owner = block_owner.reshape(slot_total)
    slot_cells = block_cells.reshape(slot_total, 2)
    full_z, full_y = (
        lax.all_gather(qz_factor, "ta", axis=0, tiled=True),
        lax.all_gather(qy_factor, "ta", axis=0, tiled=True),
    )
    grid_side = full_z.shape[0] // block_edge
    cell_total = grid_side * grid_side
    qz_panels = full_z.reshape(grid_side, block_edge, rank_cols)
    qy_panels = full_y.reshape(grid_side, block_edge, rank_cols)
    gram_z = jnp.einsum("azr,azs->ars", qz_panels, qz_panels, preferred_element_type=jnp.float32)
    gram_y = jnp.einsum("azr,azs->ars", qy_panels, qy_panels, preferred_element_type=jnp.float32)
    live_flag = (slot_owner >= 0).astype(jnp.float32)
    slot_z = qz_panels[slot_cells[:, 0]]
    slot_y = qy_panels[slot_cells[:, 1]]

    def slot_term(slot_item):
        cube_one, panel_z, panel_y = slot_item
        inner_sum = jnp.einsum("fzy,yr->fzr", cube_one, panel_y, preferred_element_type=jnp.float32)
        return jnp.sum(inner_sum * panel_z.astype(jnp.float32)[None], axis=1)

    contributions = lax.map(slot_term, (block_data, slot_z, slot_y))
    cell_index = slot_cells[:, 0] * grid_side + slot_cells[:, 1]
    cell_iota = jnp.arange(cell_total, dtype=jnp.int32)
    owner_hot = (slot_owner[:, None] == jnp.arange(ta_count, dtype=jnp.int32)[None]).astype(
        jnp.float32
    )
    cell_hot = (cell_index[:, None] == cell_iota[None]).astype(jnp.float32)
    spread = jnp.einsum("nu,nfr->ufr", owner_hot, contributions, precision=top_precision).reshape(
        ta_count * frames, rank_cols
    )
    tallies = jnp.einsum("nu,nk->uk", owner_hot, cell_hot, precision=top_precision)
    arrived_terms, arrived_counts = (
        lax.all_to_all(spread, "ta", split_axis=0, concat_axis=0, tiled=True),
        lax.all_to_all(tallies, "ta", split_axis=0, concat_axis=0, tiled=True),
    )
    owned = jnp.sum(arrived_terms.reshape(ta_count, frames, rank_cols), axis=0)
    counts = jnp.sum(arrived_counts, axis=0)
    weights = counts.reshape(grid_side, grid_side)
    mixture = jnp.einsum("ab,brs->ars", weights, gram_y, precision=top_precision)
    system = jnp.sum(gram_z * mixture, axis=0) + ridge_weight * jnp.eye(
        rank_cols, dtype=jnp.float32
    )
    new_rows = solve_rows(owned, system)
    every_row = lax.all_gather(new_rows.astype(jnp.bfloat16), "ta", axis=0, tiled=True)
    safe_owner = jnp.maximum(slot_owner, 0)
    slot_rows = every_row.reshape(ta_count, frames, rank_cols)[safe_owner]

    def misfit_one(slot_item):
        cube_one, panel_z, panel_y, rows_low = slot_item
        outer_prod = (
            rows_low.astype(jnp.float32)[:, None, :] * panel_z.astype(jnp.float32)[None]
        ).astype(jnp.bfloat16)
        model = jnp.einsum("fzr,yr->fzy", outer_prod, panel_y, preferred_element_type=jnp.float32)
        deviation = cube_one.astype(jnp.float32) - model
        return jnp.sum(deviation * deviation) / (frames * block_edge * block_edge)

    misfit = lax.map(misfit_one, (block_data, slot_z, slot_y, slot_rows)) * live_flag
    return (new_rows, misfit.reshape(1, 1, slot_total))


def solution(mesh):
    placed = (
        P(("series", "ta"), "pb", None, None, None, None),
        P(("series", "ta"), None),
        P(("series", "ta"), None),
        P(("series", "ta"), "pb", None),
        P(("series", "ta"), "pb", None, None),
    )
    return jax.shard_map(
        body,
        mesh=mesh,
        in_specs=placed,
        out_specs=(P(("series", "ta", "pb"), None), P(("series", "ta"), "pb", None)),
        check_vma=False,
    )
```

profile of v0, /device:TPU:0, one launch (start us, length us, event | category | flops | bytes accessed | tf_op | source)
XLA Modules:
  0.0 154.2 jit_solution(10912656116232131528)
XLA Ops:
  0.6 0.8 fusion.35
  1.4 1.4 fusion.26
  2.8 6.3 %all-to-all-start.1 = ((f32[4,1,64]{2,1,0:T(1,128)}), f32[4,1,64]{2,1,0:T(1,128)S(1)}, u32[]{:S(2)}, u32[]{:S(2)}) async-start(f32[4,1,64]{2,1,0:T(1,128)} %bitcast.21), calls=%async_computation.1 | async-start | bytes 4096 | tf_op jit(solution)/shard_map/all_to_all | solution.py:61
  9.2 0.7 maximum_bitcast_fusion
  9.8 15.9 %all_gather.9 = bf16[1024,256]{1,0:T(8,128)(2,1)S(1)} all-gather(bf16[256,256]{1,0:T(8,128)(2,1)} %param.11), channel_id=1, replica_groups=mesh['series'=2,'ta'=4,'pb'=4] {'ta'}, dimensions={0}, use_global_device_ids=true | all-gather | bytes 655360 | tf_op jit(solution)/shard_map/all_gather | solution.py:31
  26.2 16.1 %all_gather.10 = bf16[1024,256]{1,0:T(8,128)(2,1)S(1)} all-gather(bf16[256,256]{1,0:T(8,128)(2,1)S(1)} %copy-done), channel_id=1, replica_groups=mesh['series'=2,'ta'=4,'pb'=4] {'ta'}, dimensions={0}, use_global_device_ids=true | all-gather | bytes 655360 | tf_op jit(solution)/shard_map/all_gather | solution.py:30
  43.5 8.8 %while.24 = (s32[]{:T(128)}, f32[4,32,256]{2,0,1:T(4,128)S(1)}, bf16[4,32,128,128]{3,2,1,0:T(8,128)(2,1)}, bf16[4,128,256]{2,1,0:T(8,128)(2,1)S(1)}, bf16[4,128,256]{2,1,0:T(8,128)(2,1)S(1)}) while((s32[]{:T(128)}, f32[4,32,256]{2,0,1:T(4,128)S(1)}, bf16[4,32,128,128]{3,2,1,0:T(8,128)(2,1)}, bf16[4,128,256]{2,1,0:T(8,128)(2,1)S(1)}, ...), condition=%wide.region_2.3_spmd.clone, body=%wide.region_0.2_spmd.sunk.clone | while | flops 270557184 | bytes 1606725 | solution.py:48
  43.5 1.9 %multiply_reduce_fusion.3 = f32[32,256]{1,0:T(8,128)S(1)} fusion(f32[128,256]{1,0:T(8,128)S(1)} %bitcast_convert_fusion.9, bf16[4,32,128,128]{3,2,1,0:T(8,128)(2,1)} %get-tuple-element.279, s32[]{:T(128)} %get-tuple-element.272, bf16[4,128,256]{2,1,0:T(8,128)(2,1)S(1)} %get-tuple-element.280), kind=kOutput, calls=%fused_computation.3.clone.1.clone | convolution fusion | flops 270524416 | bytes 1278976 | tf_op jit(solution)/shard_map/while/body/eval_jaxpr/fzy,yr->fzr/dot_general | solution.py:45
  45.7 1.9 %multiply_reduce_fusion.3 = f32[32,256]{1,0:T(8,128)S(1)} fusion(f32[128,256]{1,0:T(8,128)S(1)} %bitcast_convert_fusion.9, bf16[4,32,128,128]{3,2,1,0:T(8,128)(2,1)} %get-tuple-element.279, s32[]{:T(128)} %get-tuple-element.272, bf16[4,128,256]{2,1,0:T(8,128)(2,1)S(1)} %get-tuple-element.280), kind=kOutput, calls=%fused_computation.3.clone.1.clone | convolution fusion | flops 270524416 | bytes 1278976 | tf_op jit(solution)/shard_map/while/body/eval_jaxpr/fzy,yr->fzr/dot_general | solution.py:45
  47.9 1.9 %multiply_reduce_fusion.3 = f32[32,256]{1,0:T(8,128)S(1)} fusion(f32[128,256]{1,0:T(8,128)S(1)} %bitcast_convert_fusion.9, bf16[4,32,128,128]{3,2,1,0:T(8,128)(2,1)} %get-tuple-element.279, s32[]{:T(128)} %get-tuple-element.272, bf16[4,128,256]{2,1,0:T(8,128)(2,1)S(1)} %get-tuple-element.280), kind=kOutput, calls=%fused_computation.3.clone.1.clone | convolution fusion | flops 270524416 | bytes 1278976 | tf_op jit(solution)/shard_map/while/body/eval_jaxpr/fzy,yr->fzr/dot_general | solution.py:45
  50.1 1.9 %multiply_reduce_fusion.3 = f32[32,256]{1,0:T(8,128)S(1)} fusion(f32[128,256]{1,0:T(8,128)S(1)} %bitcast_convert_fusion.9, bf16[4,32,128,128]{3,2,1,0:T(8,128)(2,1)} %get-tuple-element.279, s32[]{:T(128)} %get-tuple-element.272, bf16[4,128,256]{2,1,0:T(8,128)(2,1)S(1)} %get-tuple-element.280), kind=kOutput, calls=%fused_computation.3.clone.1.clone | convolution fusion | flops 270524416 | bytes 1278976 | tf_op jit(solution)/shard_map/while/body/eval_jaxpr/fzy,yr->fzr/dot_general | solution.py:45
  52.6 0.7 copy.12
  53.2 5.4 %all-to-all-start = ((f32[4,32,256]{2,1,0:T(8,128)}), f32[4,32,256]{2,1,0:T(8,128)S(1)}, u32[]{:S(2)}, u32[]{:S(2)}) async-start(f32[4,32,256]{2,1,0:T(8,128)} %copy.12), calls=%async_computation | async-start | bytes 262144 | tf_op jit(solution)/shard_map/all_to_all | solution.py:60
  58.7 2.9 %fusion.13 = f32[8,256,256]{2,0,1:T(8,128)S(1)} fusion(f32[8,8,1]{1,0,2:T(8,128)S(1)} %reshape.135, f32[8,256,256]{2,1,0:T(8,128)S(1)} %fusion.38), kind=kOutput, calls=%fused_computation.24 | convolution fusion | flops 50331648 | bytes 4194560 | tf_op jit(solution)/shard_map/ab,brs->ars/dot_general | solution.py:66
  61.6 0.9 fusion.15
  62.8 11.7 %cholesky.49 = f32[128,128]{1,0:T(8,128)S(1)} custom-call(f32[128,128]{1,0:T(8,128)S(1)} %cholesky.115), custom_call_target="Cholesky" | custom-call | tf_op jit(solution)/shard_map/jit(cholesky)/cholesky | solution.py:11
  74.6 9.8 %custom-call.16 = f32[1,128,128]{1,2,0:T(8,128)S(1)} custom-call(f32[1,128,128]{2,1,0:T(8,128)S(1)} %get-tuple-element.108), custom_call_target="InvertDiagBlocksLowerTriangular" | custom-call | tf_op jit(solution)/shard_map/jit(cholesky)/cholesky | solution.py:11
  84.8 11.9 %cholesky.103 = f32[128,128]{1,0:T(8,128)S(1)} custom-call(f32[128,128]{1,0:T(8,128)S(1)} %convolution_subtract_fusion), custom_call_target="Cholesky" | custom-call | tf_op jit(solution)/shard_map/jit(cholesky)/cholesky | solution.py:11
  96.7 0.7 compare_reduce_fusion
  98.9 4.1 %while.26 = (s32[]{:T(128)}, f32[256,256]{1,0:T(8,128)S(1)}, s32[2,2]{1,0:T(2,128)S(1)}, f32[2,128,128]{2,1,0:T(8,128)S(1)}) while((s32[]{:T(128)}, f32[256,256]{1,0:T(8,128)S(1)}, s32[2,2]{1,0:T(2,128)S(1)}, f32[2,128,128]{2,1,0:T(8,128)S(1)}) %tuple.67), condition=%wide.while_cond.clone, body=%wide.while_body.sunk.clone | while | flops 2 | bytes 131173 | solution.py:12
  98.9 0.6 fusion.66
  99.5 1.4 bitcast_dynamic-update-slice_fusion.3
  100.9 0.6 fusion.66
  101.5 1.4 bitcast_dynamic-update-slice_fusion.3
  103.0 19.7 %custom-call.17 = f32[2,128,128]{1,2,0:T(8,128)S(1)} custom-call(f32[2,128,128]{2,1,0:T(8,128)S(1)} %get-tuple-element.70), custom_call_target="InvertDiagBlocksLowerTriangular" | custom-call | tf_op jit(solution)/shard_map/triangular_solve | solution.py:12
  123.8 0.7 fusion.36
  124.5 13.7 %all_gather.11 = bf16[128,256]{1,0:T(8,128)(2,1)S(1)} all-gather(bf16[32,256]{1,0:T(8,128)(2,1)S(1)} %get-tuple-element.101), channel_id=1, replica_groups=mesh['series'=2,'ta'=4,'pb'=4] {'ta'}, dimensions={0}, use_global_device_ids=true | all-gather | bytes 81920 | tf_op jit(solution)/shard_map/all_gather | solution.py:71
  138.7 14.9 %while.25 = (s32[]{:T(128)}, f32[4]{0:T(128)S(1)}, bf16[4,32,128,128]{3,2,1,0:T(8,128)(2,1)}, bf16[4,32,256]{2,1,0:T(8,128)(2,1)S(1)}, bf16[4,128,256]{2,1,0:T(8,128)(2,1)S(1)}, /*index=5*/bf16[4,128,256]{2,1,0:T(8,128)(2,1)S(1)}) while((s32[]{:T(128)}, f32[4]{0:T(128)S(1)}, bf16[4,32,128,128]{3,2,1,0:T(8,128)(2,1)}, ...), condition=%wide.region_12.13_spmd.clone, body=%wide.region_10.12_spmd.sunk.clone | while | flops 272670720 | bytes 1524841 | solution.py:84
  138.8 2.9 %fusion.65 = f32[]{:T(128)} fusion(f32[128,256]{1,0:T(8,128)S(1)} %bitcast_convert_fusion.10, f32[32,256]{1,0:T(8,128)S(1)} %bitcast_convert_fusion.11, bf16[4,32,128,128]{3,2,1,0:T(8,128)(2,1)} %get-tuple-element.296, s32[]{:T(128)} %get-tuple-element.288, bf16[4,128,256]{2,1,0:T(8,128)(2,1)S(1)} %get-tuple-element.299), kind=kOutput, calls=%fused_computation.14.clone.1.clone | convolution fusion | flops 272629760 | bytes 1278980 | tf_op jit(solution)/shard_map/while/body/eval_jaxpr/fzr,yr->fzy/dot_general | solution.py:80
  142.5 2.9 %fusion.65 = f32[]{:T(128)} fusion(f32[128,256]{1,0:T(8,128)S(1)} %bitcast_convert_fusion.10, f32[32,256]{1,0:T(8,128)S(1)} %bitcast_convert_fusion.11, bf16[4,32,128,128]{3,2,1,0:T(8,128)(2,1)} %get-tuple-element.296, s32[]{:T(128)} %get-tuple-element.288, bf16[4,128,256]{2,1,0:T(8,128)(2,1)S(1)} %get-tuple-element.299), kind=kOutput, calls=%fused_computation.14.clone.1.clone | convolution fusion | flops 272629760 | bytes 1278980 | tf_op jit(solution)/shard_map/while/body/eval_jaxpr/fzr,yr->fzy/dot_general | solution.py:80
  146.3 2.9 %fusion.65 = f32[]{:T(128)} fusion(f32[128,256]{1,0:T(8,128)S(1)} %bitcast_convert_fusion.10, f32[32,256]{1,0:T(8,128)S(1)} %bitcast_convert_fusion.11, bf16[4,32,128,128]{3,2,1,0:T(8,128)(2,1)} %get-tuple-element.296, s32[]{:T(128)} %get-tuple-element.288, bf16[4,128,256]{2,1,0:T(8,128)(2,1)S(1)} %get-tuple-element.299), kind=kOutput, calls=%fused_computation.14.clone.1.clone | convolution fusion | flops 272629760 | bytes 1278980 | tf_op jit(solution)/shard_map/while/body/eval_jaxpr/fzr,yr->fzy/dot_general | solution.py:80
  150.0 2.9 %fusion.65 = f32[]{:T(128)} fusion(f32[128,256]{1,0:T(8,128)S(1)} %bitcast_convert_fusion.10, f32[32,256]{1,0:T(8,128)S(1)} %bitcast_convert_fusion.11, bf16[4,32,128,128]{3,2,1,0:T(8,128)(2,1)} %get-tuple-element.296, s32[]{:T(128)} %get-tuple-element.288, bf16[4,128,256]{2,1,0:T(8,128)(2,1)S(1)} %get-tuple-element.299), kind=kOutput, calls=%fused_computation.14.clone.1.clone | convolution fusion | flops 272629760 | bytes 1278980 | tf_op jit(solution)/shard_map/while/body/eval_jaxpr/fzr,yr->fzy/dot_general | solution.py:80
  (63 shorter events, 6.5 us)
Async XLA Ops:
  0.6 25.6 %copy-start = (bf16[256,256]{1,0:T(8,128)(2,1)S(1)}, bf16[256,256]{1,0:T(8,128)(2,1)}, u32[]{:S(2)}) copy-start(bf16[256,256]{1,0:T(8,128)(2,1)} %param.10) | copy-start | bytes 393220
  2.8 50.4 %all-to-all-start.1 = ((f32[4,1,64]{2,1,0:T(1,128)}), f32[4,1,64]{2,1,0:T(1,128)S(1)}, u32[]{:S(2)}, u32[]{:S(2)}) async-start(f32[4,1,64]{2,1,0:T(1,128)} %bitcast.21), calls=%async_computation.1 | async-start | bytes 4096 | tf_op jit(solution)/shard_map/all_to_all | solution.py:61
  43.5 8.8 %copy-start.1 = (s32[1,1,4]{2,1,0:T(1,128)S(1)}, s32[1,1,4]{2,1,0:T(1,128)}, u32[]{:S(2)}) copy-start(s32[1,1,4]{2,1,0:T(1,128)} %param.12) | copy-start | bytes 52
  53.2 69.4 %all-to-all-start = ((f32[4,32,256]{2,1,0:T(8,128)}), f32[4,32,256]{2,1,0:T(8,128)S(1)}, u32[]{:S(2)}, u32[]{:S(2)}) async-start(f32[4,32,256]{2,1,0:T(8,128)} %copy.12), calls=%async_computation | async-start | bytes 262144 | tf_op jit(solution)/shard_map/all_to_all | solution.py:60
where the time goes:
time: 155 us; the launch traced here: 154 us
  other arithmetic  56.7 us (37%)
  blocking collectives  45.7 us (29%)
  matrix products  26.8 us (17%)
  starting transfers between devices  11.7 us (8%)
  local copies, waits for them, and re-layouts  7.96 us (5%)
  loops' own time  3.05 us (2%)
  between operations  2.23 us (1%)
    another operation x6, other arithmetic, solve_rows(): lower_factor = jnp.linalg.cholesky(system)  34.2 us
    another operation x3, other arithmetic, solve_rows(): lax.linalg.triangular_solve(lower_factor, rhs_rows, left_side=False, lowe...  19.7 us
    all_gather x1, blocking collectives, body(): lax.all_gather(qz_factor, 'ta', axis=0, tiled=True)  16.1 us
    all_gather x1, blocking collectives, body(): lax.all_gather(qy_factor, 'ta', axis=0, tiled=True)  15.9 us
    all_gather x1, blocking collectives, body(): lax.all_gather(new_rows.astype(jnp.bfloat16), 'ta', axis=0, tiled=True)  13.7 us
    dot_general x4, matrix products, misfit_one(): jnp.einsum('fzr,yr->fzy', outer_prod, panel_y, preferred_element_type=jnp...  11.5 us
    dot_general x4, matrix products, slot_term(): jnp.einsum('fzy,yr->fzr', cube_one, panel_y, preferred_element_type=jnp.f...  7.7 us
    all_to_all x1, starting transfers between devices, body(): lax.all_to_all(tallies, 'ta', split_axis=0, concat_axis=0, tiled=True)  6.35 us
  transfers between devices with their start and end apart: 2, of which 0 were waited for; matrix products, arithmetic and copies ran while one was open for 48% of the time, Pallas kernels for 0%

commit v1 on v0

v1 whole, which is shorter than its diff:
```python
import functools

import jax
import jax.numpy as jnp
from jax import lax
from jax.experimental import pallas as pl
from jax.experimental.pallas import tpu as pltpu
from jax.sharding import PartitionSpec as P

ridge_weight = 0.1
info_rows = 16
ring_limit = 8
newton_steps = 10
newton_goal = 4e-4
top = lax.Precision.HIGHEST
f32 = jnp.float32
bf16 = jnp.bfloat16

vmem_spec = pl.BlockSpec(memory_space=pltpu.VMEM)
smem_spec = pl.BlockSpec(memory_space=pltpu.SMEM)
any_spec = pl.BlockSpec(memory_space=pl.ANY)


def params(mib):
    return pltpu.CompilerParams(vmem_limit_bytes=mib * 1024 * 1024)


def pack_kernel(place, owner, cells, z_ref, y_ref, out_ref):
    half = z_ref.shape[0] // 2
    slots = owner.shape[0]
    start = pl.multiple_of(place[2] * half, half)
    out_ref[0:half, :] = z_ref[pl.ds(start, half), :]
    out_ref[half : 2 * half, :] = y_ref[pl.ds(start, half), :]
    shape = (info_rows, z_ref.shape[1])
    row = lax.broadcasted_iota(jnp.int32, shape, 0)
    lane = lax.broadcasted_iota(jnp.int32, shape, 1)
    table = jnp.zeros(shape, jnp.int32)
    for s in range(slots):
        for r, value in enumerate((owner[s] + 1, cells[2 * s], cells[2 * s + 1])):
            table = jnp.where((row == r) & (lane == s), value, table)
    out_ref[2 * half :, :] = table.astype(f32).astype(bf16)


def term_kernel(
    ta_count, edge, place, owner, cells, x_ref, z_ref, y_ref, far_ref, pair_ref, blocks,
    terms, full_z, full_y, info, cube, sems,
):
    slots, frames = cube.shape[0], cube.shape[1]
    rows = z_ref.shape[0]
    half = rows // 2
    piece = 2 * half + info_rows
    copies = [pltpu.make_async_copy(blocks.at[0, 0, s], cube.at[s], sems.at[s]) for s in range(slots)]
    for copy in copies:
        copy.start()
    me, parity = place[0], place[2]
    mine = pl.multiple_of(me * rows, rows)
    full_z[pl.ds(mine, rows), :] = z_ref[...]
    full_y[pl.ds(mine, rows), :] = y_ref[...]
    info[0:info_rows, :] = x_ref[2 * half :, :]
    for k in range(1, ta_count):
        base = (k - 1) * piece
        source = lax.rem(me + (ta_count - k), ta_count) * rows
        here = pl.multiple_of(source + parity * half, half)
        there = pl.multiple_of(source + (1 - parity) * half, half)
        full_z[pl.ds(here, half), :] = far_ref[base : base + half, :]
        full_y[pl.ds(here, half), :] = far_ref[base + half : base + 2 * half, :]
        full_z[pl.ds(there, half), :] = pair_ref[base : base + half, :]
        full_y[pl.ds(there, half), :] = pair_ref[base + half : base + 2 * half, :]
        info[k * info_rows : (k + 1) * info_rows, :] = far_ref[base + 2 * half : base + piece, :]
    terms[...] = jnp.zeros_like(terms)
    chunk = 8
    rank = full_z.shape[1]
    for s in range(slots):
        copies[s].wait()
        panel_z = full_z[pl.ds(pl.multiple_of(cells[2 * s] * edge, edge), edge), :].astype(f32)
        panel_y = full_y[pl.ds(pl.multiple_of(cells[2 * s + 1] * edge, edge), edge), :]
        u = owner[s]
        live = u >= 0
        k = lax.rem(jnp.maximum(u, 0) + (ta_count - me), ta_count)
        for f in range(0, frames, chunk):
            part = cube[s, f : f + chunk].reshape(chunk * edge, edge)
            inner = jnp.dot(part, panel_y, preferred_element_type=f32)
            summed = jnp.sum(inner.reshape(chunk, edge, rank) * panel_z[None], axis=1)
            at = pl.ds(pl.multiple_of(k * frames + f, chunk), chunk)
            terms[at, :] += jnp.where(live, summed, 0.0)


def system_kernel(ta_count, slots, edge, place, info, full_z, full_y, system, inverse, codes):
    rank = full_z.shape[1]
    grid = full_z.shape[0] // edge
    me = place[0]
    lane = lax.broadcasted_iota(jnp.int32, (1, rank), 1)
    for k in range(ta_count):
        table = info[k * info_rows : (k + 1) * info_rows, :].astype(f32)
        cell = (table[1:2, :] * grid + table[2:3, :]).astype(jnp.int32)
        wanted = table[0:1, :].astype(jnp.int32) == me + 1
        code = jnp.where(wanted, cell, -1)
        for s in range(slots):
            codes[k * slots + s] = jnp.max(jnp.where(lane == s, code, -1))
    eye = lax.broadcasted_iota(jnp.int32, (rank, rank), 0) == lax.broadcasted_iota(
        jnp.int32, (rank, rank), 1
    )
    system[...] = jnp.where(eye, ridge_weight, 0.0).astype(f32)

    @pl.loop(0, ta_count * slots)
    def _(i):
        code = codes[i]

        @pl.when(code >= 0)
        def _():
            at = pl.multiple_of(lax.div(code, grid) * edge, edge)
            panel_z = full_z[pl.ds(at, edge), :]
            at = pl.multiple_of(lax.rem(code, grid) * edge, edge)
            panel_y = full_y[pl.ds(at, edge), :]
            over = (((0,), (0,)), ((), ()))
            gram_z = lax.dot_general(panel_z, panel_z, over, preferred_element_type=f32)
            gram_y = lax.dot_general(panel_y, panel_y, over, preferred_element_type=f32)
            system[...] += gram_z * gram_y

    matrix = system[...]
    down = 1.0 / jnp.sum(jnp.where(eye, matrix, 0.0), axis=1, keepdims=True)
    across = 1.0 / jnp.sum(jnp.where(eye, matrix, 0.0), axis=0, keepdims=True)
    inverse[...] = jnp.where(eye, 2.0 * across, 0.0) - down * matrix * across

    def going(state):
        step, error = state
        return (step < newton_steps) & jnp.logical_not(error <= newton_goal)

    def newton(state):
        guess = inverse[...]
        miss = jnp.where(eye, 1.0, 0.0) - jnp.dot(
            system[...], guess, precision=top, preferred_element_type=f32
        )
        inverse[...] = guess + jnp.dot(guess, miss, precision=top, preferred_element_type=f32)
        return state[0] + 1, jnp.sum(miss * miss)

    _, error = lax.while_loop(going, newton, (jnp.int32(0), jnp.float32(jnp.inf)))

    @pl.when(jnp.logical_not(error <= newton_goal))
    def _():
        inverse[...] = system[...]
        lanes = lax.broadcasted_iota(jnp.int32, (1, rank), 1)
        subs = lax.broadcasted_iota(jnp.int32, (rank, 1), 0)

        @pl.loop(0, rank)
        def _(k):
            whole = inverse[...]
            row = inverse[pl.ds(k, 1), :]
            column = jnp.sum(jnp.where(lanes == k, whole, 0.0), axis=1, keepdims=True)
            pivot = 1.0 / jnp.sum(jnp.where(lanes == k, row, 0.0), axis=1, keepdims=True)
            scaled = jnp.where(lanes == k, 1.0, row) * pivot
            rest = jnp.where(lanes == k, 0.0, whole) - column * scaled
            inverse[...] = jnp.where(subs == k, scaled, rest)


def solve_kernel(ta_count, own, far, system, inverse, rows_out, low_out):
    frames = rows_out.shape[0]
    rhs = own[0:frames, :]
    for k in range(1, ta_count):
        rhs = rhs + far[(k - 1) * frames : k * frames, :]
    dot = functools.partial(jnp.dot, precision=top, preferred_element_type=f32)
    rows = dot(rhs, inverse[...])
    rest = rhs - dot(rows, system[...])
    rows = rows + dot(rest, inverse[...])
    rows_out[...] = rows
    low_out[...] = rows.astype(bf16)


def misfit_kernel(
    ta_count, edge, place, owner, cells, low, far, full_z, full_y, blocks, out, cube, every, sems
):
    slots, frames = cube.shape[0], cube.shape[1]
    copies = [pltpu.make_async_copy(blocks.at[0, 0, s], cube.at[s], sems.at[s]) for s in range(slots)]
    for copy in copies:
        copy.start()
    every[0] = low[...].astype(f32)
    for k in range(1, ta_count):
        every[k] = far[(k - 1) * frames : k * frames, :].astype(f32)
    me = place[0]
    chunk = 8
    rank = full_z.shape[1]
    lane = lax.broadcasted_iota(jnp.int32, out.shape, 1)
    answer = jnp.zeros(out.shape, f32)
    over = (((1,), (1,)), ((), ()))
    for s in range(slots):
        copies[s].wait()
        panel_z = full_z[pl.ds(pl.multiple_of(cells[2 * s] * edge, edge), edge), :].astype(f32)
        panel_y = full_y[pl.ds(pl.multiple_of(cells[2 * s + 1] * edge, edge), edge), :]
        u = owner[s]
        k = lax.rem(me + (ta_count - jnp.maximum(u, 0)), ta_count)
        total = jnp.zeros((8, edge), f32)
        for f in range(0, frames, chunk):
            rows = every[k, f : f + chunk, :]
            outer = (rows[:, None, :] * panel_z[None]).astype(bf16).reshape(chunk * edge, rank)
            model = lax.dot_general(outer, panel_y, over, preferred_element_type=f32)
            off = cube[s, f : f + chunk].reshape(chunk * edge, edge).astype(f32) - model
            total = total + jnp.sum((off * off).reshape(chunk * edge // 8, 8, edge), axis=0)
        mean = jnp.sum(total) * (1.0 / (frames * edge * edge))
        answer = jnp.where((lane == s) & (u >= 0), mean, answer)
    out[...] = answer


def around(x, axis, count):
    if count <= ring_limit:
        turns = [
            lax.ppermute(x, axis, [(i, (i + k) % count) for i in range(count)])
            for k in range(1, count)
        ]
        return jnp.concatenate(turns, axis=0)
    every = lax.all_gather(x, axis, axis=0)
    order = (lax.axis_index(axis) - jnp.arange(1, count)) % count
    return every[order].reshape((count - 1) * x.shape[0], x.shape[1])


def deliver(terms, axis, count):
    frames = terms.shape[0] // count
    if count <= ring_limit:
        turns = [
            lax.ppermute(
                terms[k * frames : (k + 1) * frames],
                axis,
                [(i, (i + k) % count) for i in range(count)],
            )
            for k in range(1, count)
        ]
        return jnp.concatenate(turns, axis=0)
    me = lax.axis_index(axis)
    split = terms.reshape(count, frames, terms.shape[1])
    arrived = lax.all_to_all(
        split[(jnp.arange(count) - me) % count], axis, split_axis=0, concat_axis=0
    )
    order = (me - jnp.arange(1, count)) % count
    return arrived[order].reshape((count - 1) * frames, terms.shape[1])


def body(blocks, qz_factor, qy_factor, block_owner, block_cells):
    ta_count, pb_count = lax.axis_size("ta"), lax.axis_size("pb")
    slots, frames, edge = blocks.shape[2], blocks.shape[3], blocks.shape[4]
    rows, rank = qz_factor.shape
    half = rows // 2
    piece = 2 * half + info_rows
    me, column = lax.axis_index("ta"), lax.axis_index("pb")
    place = jnp.stack([me, column, column % 2]).astype(jnp.int32)
    owner = block_owner.reshape(slots)
    cells = block_cells.reshape(slots * 2)
    shape = jax.ShapeDtypeStruct
    packed = pl.pallas_call(
        pack_kernel,
        out_shape=shape((piece, rank), bf16),
        in_specs=[smem_spec] * 3 + [vmem_spec] * 2,
        out_specs=vmem_spec,
        compiler_params=params(4),
        name="pack",
    )(place, owner, cells, qz_factor, qy_factor)
    far = around(packed, "ta", ta_count)
    pair = lax.ppermute(far, "pb", [(i, i ^ 1) for i in range(pb_count)])
    terms, full_z, full_y, info = pl.pallas_call(
        functools.partial(term_kernel, ta_count, edge),
        out_shape=[
            shape((ta_count * frames, rank), f32),
            shape((ta_count * rows, rank), bf16),
            shape((ta_count * rows, rank), bf16),
            shape((ta_count * info_rows, rank), bf16),
        ],
        in_specs=[smem_spec] * 3 + [vmem_spec] * 5 + [any_spec],
        out_specs=[vmem_spec] * 4,
        scratch_shapes=[
            pltpu.VMEM((slots, frames, edge, edge), bf16),
            pltpu.SemaphoreType.DMA((slots,)),
        ],
        compiler_params=params(24),
        name="terms",
    )(place, owner, cells, packed, qz_factor, qy_factor, far, pair, blocks)
    arrived = deliver(terms, "ta", ta_count)
    system, inverse = pl.pallas_call(
        functools.partial(system_kernel, ta_count, slots, edge),
        out_shape=[shape((rank, rank), f32)] * 2,
        in_specs=[smem_spec] + [vmem_spec] * 3,
        out_specs=[vmem_spec] * 2,
        scratch_shapes=[pltpu.SMEM((ta_count * slots,), jnp.int32)],
        compiler_params=params(16),
        name="system",
    )(place, info, full_z, full_y)
    new_rows, low = pl.pallas_call(
        functools.partial(solve_kernel, ta_count),
        out_shape=[shape((frames, rank), f32), shape((frames, rank), bf16)],
        in_specs=[vmem_spec] * 4,
        out_specs=[vmem_spec] * 2,
        compiler_params=params(8),
        name="solve",
    )(terms, arrived, system, inverse)
    others = around(low, "ta", ta_count)
    misfit = pl.pallas_call(
        functools.partial(misfit_kernel, ta_count, edge),
        out_shape=shape((1, slots), f32),
        in_specs=[smem_spec] * 3 + [vmem_spec] * 4 + [any_spec],
        out_specs=vmem_spec,
        scratch_shapes=[
            pltpu.VMEM((slots, frames, edge, edge), bf16),
            pltpu.VMEM((ta_count, frames, rank), f32),
            pltpu.SemaphoreType.DMA((slots,)),
        ],
        compiler_params=params(24),
        name="misfit",
    )(place, owner, cells, low, others, full_z, full_y, blocks)
    return (new_rows, misfit.reshape(1, 1, slots))


def solution(mesh):
    placed = (
        P(("series", "ta"), "pb", None, None, None, None),
        P(("series", "ta"), None),
        P(("series", "ta"), None),
        P(("series", "ta"), "pb", None),
        P(("series", "ta"), "pb", None, None),
    )
    return jax.shard_map(
        body,
        mesh=mesh,
        in_specs=placed,
        out_specs=(P(("series", "ta", "pb"), None), P(("series", "ta"), "pb", None)),
        check_vma=False,
    )
```

time: 155 us -> 54.6 us (0.35)
  other arithmetic: 56.7 us -> 0.09 us
  blocking collectives: 45.7 us -> 0 us
  matrix products: 26.8 us -> 0 us
  Pallas kernels: 0 us -> 14.4 us
  waiting for transfers between devices: 0.01 us -> 14.3 us
  starting transfers between devices: 11.7 us -> 16.8 us
  loops' own time: 3.05 us -> 0 us
    another operation x10 -> x1, other arithmetic: 53.9 us -> 0.08 us  [body(): place = jnp.stack([me, column, column % 2]).astype(jnp.int32)]
    all_gather x3 -> x0, blocking collectives: 45.7 us -> none  [the longest x1 16.1 us: body(): lax.all_gather(qz_factor, 'ta', axis=0, tiled=True)]
    dot_general x13 -> x0, matrix products: 25.2 us -> none  [the longest x4 11.5 us: misfit_one(): jnp.einsum('fzr,yr->fzy', outer_prod, panel_y, preferred_element_type=jnp...]
    ppermute x0 -> x10, starting transfers between devices: none -> 16.8 us  [the longest x6 11.6 us: around(): lax.ppermute(x, axis, [(i, (i + k) % count) for i in range(count)])]
    pallas_call x0 -> x5, Pallas kernels: none -> 14.4 us  [the longest x1 4.72 us: body(): pl.pallas_call(functools.partial(misfit_kernel, ta_count, edge), out_shap...]
    ppermute x0 -> x10, waiting for transfers between devices: none -> 14.3 us  [the longest x6 12.1 us: around(): lax.ppermute(x, axis, [(i, (i + k) % count) for i in range(count)])]
    all_to_all x2 -> x0, starting transfers between devices: 11.7 us -> none  [the longest x1 6.35 us: body(): lax.all_to_all(tallies, 'ta', split_axis=0, concat_axis=0, tiled=True)]
    unnamed x4 -> x19, local copies, waits for them, and re-layouts: 0.01 us -> 7.9 us
  transfers between devices with their start and end apart: 2 -> 10, of which waited for: 0 -> 6; matrix products, arithmetic and copies ran while one was open for 48% -> 0% of each run, Pallas kernels for 0% -> 7%
where the time goes in v1:
time: 54.6 us; the launch traced here: 54.3 us
  starting transfers between devices  16.8 us (31%)
  Pallas kernels  14.4 us (26%)
  waiting for transfers between devices  14.3 us (26%)
  local copies, waits for them, and re-layouts  8.01 us (15%)
  between operations  0.74 us (1%)
    ppermute x6, waiting for transfers between devices, around(): lax.ppermute(x, axis, [(i, (i + k) % count) for i in range(count)])  12.1 us
    ppermute x6, starting transfers between devices, around(): lax.ppermute(x, axis, [(i, (i + k) % count) for i in range(count)])  11.6 us
    unnamed x19, local copies, waits for them, and re-layouts  7.9 us
    ppermute x3, starting transfers between devices, deliver(): lax.ppermute(terms[k * frames:(k + 1) * frames], axis, [(i, (i + k) % cou...  5.13 us
    pallas_call x1, Pallas kernels, body(): pl.pallas_call(functools.partial(misfit_kernel, ta_count, edge), out_shap...  4.72 us
    pallas_call x1, Pallas kernels, body(): pl.pallas_call(functools.partial(system_kernel, ta_count, slots, edge), o...  3.86 us
    pallas_call x1, Pallas kernels, body(): pl.pallas_call(functools.partial(term_kernel, ta_count, edge), out_shape=...  3.78 us
    ppermute x1, waiting for transfers between devices, body(): pair = lax.ppermute(far, 'pb', [(i, i ^ 1) for i in range(pb_count)])  1.74 us
  transfers between devices with their start and end apart: 10, of which 6 were waited for; matrix products, arithmetic and copies ran while one was open for 0% of the time, Pallas kernels for 7%

profile of v1, /device:TPU:0, one launch (start us, length us, event | category | flops | bytes accessed | tf_op | source)
XLA Modules:
  0.0 54.3 jit_solution(1005190584584018731)
XLA Ops:
  0.6 0.8 %copy.8 = s32[1,1,4,2]{3,2,1,0:T(4,128)S(1)} copy(s32[1,1,4,2]{2,3,1,0:T(2,128)} %param.9) | data formatting | bytes 64 | tf_op args[4]
  1.4 0.1 reshape.14.cells
  1.5 0.1 pad_add_fusion.place
  1.6 0.9 %copy-done.2 = bf16[256,256]{1,0:T(8,128)(2,1)S(1)} copy-done((bf16[256,256]{1,0:T(8,128)(2,1)S(1)}, bf16[256,256]{1,0:T(8,128)(2,1)}, u32[]{:S(2)}) %copy-start.2) | copy-done | bytes 131096
  2.5 0.9 %copy-done.4 = bf16[256,256]{1,0:T(8,128)(2,1)S(1)} copy-done((bf16[256,256]{1,0:T(8,128)(2,1)S(1)}, bf16[256,256]{1,0:T(8,128)(2,1)}, u32[]{:S(2)}) %copy-start.4) | copy-done | bytes 131096
  3.4 0.7 %copy-done.6 = s32[1,1,4]{2,1,0:T(1,128)S(1)} copy-done((s32[1,1,4]{2,1,0:T(1,128)S(1)}, s32[1,1,4]{2,1,0:T(1,128)}, u32[]{:S(2)}) %copy-start.6) | copy-done | bytes 40
  4.0 0.6 %pack.1.x_ref = bf16[272,256]{1,0:T(8,128)(2,1)S(1)} custom-call(s32[3]{0:T(128)S(1)} %pad_add_fusion.place, s32[4]{0:T(128)S(1)} %bitcast.5, s32[8]{0:T(128)S(1)} %reshape.14.cells, bf16[256,256]{1,0:T(8,128)(2,1)S(1)} %copy-done.2, bf16[256,256]{1,0:T(8,128)(2,1)S(1)} %copy-done.4), custom_call_target="tpu_custom_call" | custom-call | tf_op jit(solution)/shard_map/pack/pallas_call | solution.py:247
  4.6 3.1 %collective-permute-start = (bf16[272,256]{1,0:T(8,128)(2,1)S(1)}, bf16[272,256]{1,0:T(8,128)(2,1)S(1)}, u32[]{:S(2)}, u32[]{:S(2)}) collective-permute-start(bf16[272,256]{1,0:T(8,128)(2,1)S(1)} %pack.1.x_ref), channel_id=1, source_target_pairs={{0,4},{4,8},{8,12},{12,0},{1,5},{5,9},{9,13},{13,1},{2,6},{6,10},{... | collective-permute-start | bytes 417800 | tf_op jit(solution)/shard_map/ppermute | solution.py:206
  7.7 2.6 %collective-permute-start.1 = (bf16[272,256]{1,0:T(8,128)(2,1)S(1)}, bf16[272,256]{1,0:T(8,128)(2,1)S(1)}, u32[]{:S(2)}, u32[]{:S(2)}) collective-permute-start(bf16[272,256]{1,0:T(8,128)(2,1)S(1)} %pack.1.x_ref), channel_id=1, source_target_pairs={{0,8},{4,12},{8,0},{12,4},{1,9},{5,13},{9,1},{13,5},{2,10},{6,14},... | collective-permute-start | bytes 417800 | tf_op jit(solution)/shard_map/ppermute | solution.py:206
  10.3 1.3 %collective-permute-start.2 = (bf16[272,256]{1,0:T(8,128)(2,1)S(1)}, bf16[272,256]{1,0:T(8,128)(2,1)S(1)}, u32[]{:S(2)}, u32[]{:S(2)}) collective-permute-start(bf16[272,256]{1,0:T(8,128)(2,1)S(1)} %pack.1.x_ref), channel_id=1, source_target_pairs={{0,12},{4,0},{8,4},{12,8},{1,13},{5,1},{9,5},{13,9},{2,14},{6,2},{... | collective-permute-start | bytes 417800 | tf_op jit(solution)/shard_map/ppermute | solution.py:206
  11.7 2.7 %collective-permute-done = bf16[272,256]{1,0:T(8,128)(2,1)S(1)} collective-permute-done((bf16[272,256]{1,0:T(8,128)(2,1)S(1)}, bf16[272,256]{1,0:T(8,128)(2,1)S(1)}, u32[]{:S(2)}, u32[]{:S(2)}) %collective-permute-start) | collective-permute-done | bytes 139296 | tf_op jit(solution)/shard_map/ppermute | solution.py:206
  14.4 5.1 %collective-permute-done.1 = bf16[272,256]{1,0:T(8,128)(2,1)S(1)} collective-permute-done((bf16[272,256]{1,0:T(8,128)(2,1)S(1)}, bf16[272,256]{1,0:T(8,128)(2,1)S(1)}, u32[]{:S(2)}, u32[]{:S(2)}) %collective-permute-start.1) | collective-permute-done | bytes 139296 | tf_op jit(solution)/shard_map/ppermute | solution.py:206
  19.5 0.0 collective-permute-done.2
  19.5 0.1 collective-permute-start.3
  19.6 1.7 %collective-permute-done.3.pair_ref = bf16[816,256]{1,0:T(8,128)(2,1)S(1)} collective-permute-done((bf16[816,256]{1,0:T(8,128)(2,1)S(1)}, bf16[816,256]{1,0:T(8,128)(2,1)S(1)}, u32[]{:S(2)}, u32[]{:S(2)}) %collective-permute-start.3) | collective-permute-done | bytes 417824 | tf_op jit(solution)/shard_map/ppermute | solution.py:256
  21.3 2.2 %copy-done = bf16[1,1,4,32,128,128]{5,4,3,2,1,0:T(8,128)(2,1)S(1)} copy-done((bf16[1,1,4,32,128,128]{5,4,3,2,1,0:T(8,128)(2,1)S(1)}, bf16[1,1,4,32,128,128]{5,4,3,2,1,0:T(8,128)(2,1)}, u32[]{:S(2)}) %copy-start) | copy-done | bytes 4194328
  23.5 0.9 %copy-done.3 = bf16[256,256]{1,0:T(8,128)(2,1)S(1)} copy-done((bf16[256,256]{1,0:T(8,128)(2,1)S(1)}, bf16[256,256]{1,0:T(8,128)(2,1)}, u32[]{:S(2)}) %copy-start.3) | copy-done | bytes 131096
  24.4 0.9 %copy-done.5 = bf16[256,256]{1,0:T(8,128)(2,1)S(1)} copy-done((bf16[256,256]{1,0:T(8,128)(2,1)S(1)}, bf16[256,256]{1,0:T(8,128)(2,1)}, u32[]{:S(2)}) %copy-start.5) | copy-done | bytes 131096
  25.3 0.7 %copy-done.7 = s32[1,1,4]{2,1,0:T(1,128)S(1)} copy-done((s32[1,1,4]{2,1,0:T(1,128)S(1)}, s32[1,1,4]{2,1,0:T(1,128)}, u32[]{:S(2)}) %copy-start.7) | copy-done | bytes 40
  26.0 3.8 %terms.1 = (f32[128,256]{1,0:T(8,128)S(1)}, bf16[1024,256]{1,0:T(8,128)(2,1)S(1)}, bf16[1024,256]{1,0:T(8,128)(2,1)S(1)}, bf16[64,256]{1,0:T(8,128)(2,1)S(1)}) custom-call(s32[3]{0:T(128)S(1)} %pad_add_fusion.place, s32[4]{0:T(128)S(1)} %bitcast.6, s32[8]{0:T(128)S(1)} %reshape.14.cells, bf16[272,256]{1,0:T(8,128)(2,1)S(1)} %pack.1.x_ref, ...), custom_call_target="tpu_custom_call" | custom-call | tf_op jit(solution)/shard_map/terms/pallas_call | solution.py:257
  29.8 3.5 %collective-permute-start.4 = (f32[32,256]{1,0:T(8,128)S(1)}, f32[32,256]{1,0:T(8,128)S(1)}, u32[]{:S(2)}, u32[]{:S(2)}) collective-permute-start(f32[32,256]{1,0:T(8,128)S(1)} %get-tuple-element.18), channel_id=1, source_target_pairs={{0,4},{4,8},{8,12},{12,0},{1,5},{5,9},{9,13},{13,1},{2,6},{6,10},{... | collective-permute-start | bytes 98312 | tf_op jit(solution)/shard_map/ppermute | solution.py:219
  33.3 1.2 %collective-permute-start.6 = (f32[32,256]{1,0:T(8,128)S(1)}, f32[32,256]{1,0:T(8,128)S(1)}, u32[]{:S(2)}, u32[]{:S(2)}) collective-permute-start(f32[32,256]{1,0:T(8,128)S(1)} %get-tuple-element.19), channel_id=1, source_target_pairs={{0,12},{4,0},{8,4},{12,8},{1,13},{5,1},{9,5},{13,9},{2,14},{6,2},{... | collective-permute-start | bytes 98312 | tf_op jit(solution)/shard_map/ppermute | solution.py:219
  34.4 0.5 collective-permute-start.5
  34.9 3.9 %system.1 = (f32[256,256]{1,0:T(8,128)S(1)}, f32[256,256]{1,0:T(8,128)S(1)}) custom-call(s32[3]{0:T(128)S(1)} %pad_add_fusion.place, bf16[64,256]{1,0:T(8,128)(2,1)S(1)} %get-tuple-element.11.info, bf16[1024,256]{1,0:T(8,128)(2,1)S(1)} %get-tuple-element.12.full_z, bf16[1024,256]{1,0:T(8,128)(2,1)S(1)} %get-tuple-element.13.full_y), custom_call_target="tpu_custom_call" | custom-call | tf_op jit(solution)/shard_map/system/pallas_call | solution.py:275
  38.8 0.4 collective-permute-done.5
  39.3 1.4 %solve.1 = (f32[32,256]{1,0:T(8,128)}, bf16[32,256]{1,0:T(8,128)(2,1)S(1)}) custom-call(f32[128,256]{1,0:T(8,128)S(1)} %get-tuple-element.10.own, f32[96,256]{1,0:T(8,128)S(1)} %pad_maximum_fusion.far, f32[256,256]{1,0:T(8,128)S(1)} %get-tuple-element.14.system, f32[256,256]{1,0:T(8,128)S(1)} %get-tuple-element.15.inverse), custom_call_target="tpu_custom_call" | custom-call | tf_op jit(solution)/shard_map/solve/pallas_call | solution.py:284
  40.7 2.6 %collective-permute-start.9 = (bf16[32,256]{1,0:T(8,128)(2,1)S(1)}, bf16[32,256]{1,0:T(8,128)(2,1)S(1)}, u32[]{:S(2)}, u32[]{:S(2)}) collective-permute-start(bf16[32,256]{1,0:T(8,128)(2,1)S(1)} %get-tuple-element.17.low), channel_id=1, source_target_pairs={{0,12},{4,0},{8,4},{12,8},{1,13},{5,1},{9,5},{13,9},{2,14},{6,2},{... | collective-permute-start | bytes 49160 | tf_op jit(solution)/shard_map/ppermute | solution.py:206
  43.3 0.8 %collective-permute-start.8 = (bf16[32,256]{1,0:T(8,128)(2,1)S(1)}, bf16[32,256]{1,0:T(8,128)(2,1)S(1)}, u32[]{:S(2)}, u32[]{:S(2)}) collective-permute-start(bf16[32,256]{1,0:T(8,128)(2,1)S(1)} %get-tuple-element.17.low), channel_id=1, source_target_pairs={{0,8},{4,12},{8,0},{12,4},{1,9},{5,13},{9,1},{13,5},{2,10},{6,14},... | collective-permute-start | bytes 49160 | tf_op jit(solution)/shard_map/ppermute | solution.py:206
  44.0 1.2 %collective-permute-start.7 = (bf16[32,256]{1,0:T(8,128)(2,1)S(1)}, bf16[32,256]{1,0:T(8,128)(2,1)S(1)}, u32[]{:S(2)}, u32[]{:S(2)}) collective-permute-start(bf16[32,256]{1,0:T(8,128)(2,1)S(1)} %get-tuple-element.17.low), channel_id=1, source_target_pairs={{0,4},{4,8},{8,12},{12,0},{1,5},{5,9},{9,13},{13,1},{2,6},{6,10},{... | collective-permute-start | bytes 49160 | tf_op jit(solution)/shard_map/ppermute | solution.py:206
  45.3 2.7 %collective-permute-done.8 = bf16[32,256]{1,0:T(8,128)(2,1)S(1)} collective-permute-done((bf16[32,256]{1,0:T(8,128)(2,1)S(1)}, bf16[32,256]{1,0:T(8,128)(2,1)S(1)}, u32[]{:S(2)}, u32[]{:S(2)}) %collective-permute-start.8) | collective-permute-done | bytes 16416 | tf_op jit(solution)/shard_map/ppermute | solution.py:206
  47.9 1.7 %collective-permute-done.7 = bf16[32,256]{1,0:T(8,128)(2,1)S(1)} collective-permute-done((bf16[32,256]{1,0:T(8,128)(2,1)S(1)}, bf16[32,256]{1,0:T(8,128)(2,1)S(1)}, u32[]{:S(2)}, u32[]{:S(2)}) %collective-permute-start.7) | collective-permute-done | bytes 16416 | tf_op jit(solution)/shard_map/ppermute | solution.py:206
  49.6 4.7 %misfit.1 = f32[1,4]{1,0:T(1,128)} custom-call(s32[3]{0:T(128)S(1)} %pad_add_fusion.place, s32[4]{0:T(128)S(1)} %bitcast.7, s32[8]{0:T(128)S(1)} %reshape.14.cells, bf16[32,256]{1,0:T(8,128)(2,1)S(1)} %get-tuple-element.17.low, bf16[96,256]{1,0:T(8,128)(2,1)S(1)} %pad_maximum_fusion.1.far, bf16[1024,256]{1,0:T(8,128)(2,1)S(1)} %get-tuple-element.12.full_z, ...), custom_call_target="tpu_custom_call" | custom-call | tf_op jit(solution)/shard_map/misfit/pallas_call | solution.py:293
  (18 shorter events, 0.1 us)
Async XLA Ops:
  1.6 0.9 %copy-start.2 = (bf16[256,256]{1,0:T(8,128)(2,1)S(1)}, bf16[256,256]{1,0:T(8,128)(2,1)}, u32[]{:S(2)}) copy-start(bf16[256,256]{1,0:T(8,128)(2,1)} %z_ref.3) | copy-start | bytes 393220
  2.5 0.9 %copy-start.4 = (bf16[256,256]{1,0:T(8,128)(2,1)S(1)}, bf16[256,256]{1,0:T(8,128)(2,1)}, u32[]{:S(2)}) copy-start(bf16[256,256]{1,0:T(8,128)(2,1)} %y_ref.3) | copy-start | bytes 393220
  3.4 0.7 %copy-start.6 = (s32[1,1,4]{2,1,0:T(1,128)S(1)}, s32[1,1,4]{2,1,0:T(1,128)}, u32[]{:S(2)}) copy-start(s32[1,1,4]{2,1,0:T(1,128)} %param.8) | copy-start | bytes 52
  4.6 9.8 %collective-permute-start = (bf16[272,256]{1,0:T(8,128)(2,1)S(1)}, bf16[272,256]{1,0:T(8,128)(2,1)S(1)}, u32[]{:S(2)}, u32[]{:S(2)}) collective-permute-start(bf16[272,256]{1,0:T(8,128)(2,1)S(1)} %pack.1.x_ref), channel_id=1, source_target_pairs={{0,4},{4,8},{8,12},{12,0},{1,5},{5,9},{9,13},{13,1},{2,6},{6,10},{... | collective-permute-start | bytes 417800 | tf_op jit(solution)/shard_map/ppermute | solution.py:206
  7.7 11.8 %collective-permute-start.1 = (bf16[272,256]{1,0:T(8,128)(2,1)S(1)}, bf16[272,256]{1,0:T(8,128)(2,1)S(1)}, u32[]{:S(2)}, u32[]{:S(2)}) collective-permute-start(bf16[272,256]{1,0:T(8,128)(2,1)S(1)} %pack.1.x_ref), channel_id=1, source_target_pairs={{0,8},{4,12},{8,0},{12,4},{1,9},{5,13},{9,1},{13,5},{2,10},{6,14},... | collective-permute-start | bytes 417800 | tf_op jit(solution)/shard_map/ppermute | solution.py:206
  10.3 9.2 %collective-permute-start.2 = (bf16[272,256]{1,0:T(8,128)(2,1)S(1)}, bf16[272,256]{1,0:T(8,128)(2,1)S(1)}, u32[]{:S(2)}, u32[]{:S(2)}) collective-permute-start(bf16[272,256]{1,0:T(8,128)(2,1)S(1)} %pack.1.x_ref), channel_id=1, source_target_pairs={{0,12},{4,0},{8,4},{12,8},{1,13},{5,1},{9,5},{13,9},{2,14},{6,2},{... | collective-permute-start | bytes 417800 | tf_op jit(solution)/shard_map/ppermute | solution.py:206
  19.5 1.8 %collective-permute-start.3 = (bf16[816,256]{1,0:T(8,128)(2,1)S(1)}, bf16[816,256]{1,0:T(8,128)(2,1)S(1)}, u32[]{:S(2)}, u32[]{:S(2)}) collective-permute-start(bf16[816,256]{1,0:T(8,128)(2,1)S(1)} %constant_dynamic-update-slice_fusion.far_ref), channel_id=1, source_target_pairs={{0,1},{1,0},{2,3},{3,2},{4,5},{5,4},{6,7},{7,6},{8,9},{9,8},{10,11... | collective-permute-start | bytes 1253384 | tf_op jit(solution)/shard_map/ppermute | solution.py:256
  21.3 2.2 %copy-start = (bf16[1,1,4,32,128,128]{5,4,3,2,1,0:T(8,128)(2,1)S(1)}, bf16[1,1,4,32,128,128]{5,4,3,2,1,0:T(8,128)(2,1)}, u32[]{:S(2)}) copy-start(bf16[1,1,4,32,128,128]{5,4,3,2,1,0:T(8,128)(2,1)} %blocks.3) | copy-start | bytes 12582916
  23.5 0.9 %copy-start.3 = (bf16[256,256]{1,0:T(8,128)(2,1)S(1)}, bf16[256,256]{1,0:T(8,128)(2,1)}, u32[]{:S(2)}) copy-start(bf16[256,256]{1,0:T(8,128)(2,1)} %z_ref.3) | copy-start | bytes 393220
  24.4 0.9 %copy-start.5 = (bf16[256,256]{1,0:T(8,128)(2,1)S(1)}, bf16[256,256]{1,0:T(8,128)(2,1)}, u32[]{:S(2)}) copy-start(bf16[256,256]{1,0:T(8,128)(2,1)} %y_ref.3) | copy-start | bytes 393220
  25.3 0.7 %copy-start.7 = (s32[1,1,4]{2,1,0:T(1,128)S(1)}, s32[1,1,4]{2,1,0:T(1,128)}, u32[]{:S(2)}) copy-start(s32[1,1,4]{2,1,0:T(1,128)} %param.8) | copy-start | bytes 52
  26.0 23.6 %copy-start.1 = (bf16[1,1,4,32,128,128]{5,4,3,2,1,0:T(8,128)(2,1)S(1)}, bf16[1,1,4,32,128,128]{5,4,3,2,1,0:T(8,128)(2,1)}, u32[]{:S(2)}) copy-start(bf16[1,1,4,32,128,128]{5,4,3,2,1,0:T(8,128)(2,1)} %blocks.3) | copy-start | bytes 12582916
  29.8 9.0 %collective-permute-start.4 = (f32[32,256]{1,0:T(8,128)S(1)}, f32[32,256]{1,0:T(8,128)S(1)}, u32[]{:S(2)}, u32[]{:S(2)}) collective-permute-start(f32[32,256]{1,0:T(8,128)S(1)} %get-tuple-element.18), channel_id=1, source_target_pairs={{0,4},{4,8},{8,12},{12,0},{1,5},{5,9},{9,13},{13,1},{2,6},{6,10},{... | collective-permute-start | bytes 98312 | tf_op jit(solution)/shard_map/ppermute | solution.py:219
  33.3 5.5 %collective-permute-start.6 = (f32[32,256]{1,0:T(8,128)S(1)}, f32[32,256]{1,0:T(8,128)S(1)}, u32[]{:S(2)}, u32[]{:S(2)}) collective-permute-start(f32[32,256]{1,0:T(8,128)S(1)} %get-tuple-element.19), channel_id=1, source_target_pairs={{0,12},{4,0},{8,4},{12,8},{1,13},{5,1},{9,5},{13,9},{2,14},{6,2},{... | collective-permute-start | bytes 98312 | tf_op jit(solution)/shard_map/ppermute | solution.py:219
  34.4 4.8 %collective-permute-start.5 = (f32[32,256]{1,0:T(8,128)S(1)}, f32[32,256]{1,0:T(8,128)S(1)}, u32[]{:S(2)}, u32[]{:S(2)}) collective-permute-start(f32[32,256]{1,0:T(8,128)S(1)} %get-tuple-element.20), channel_id=1, source_target_pairs={{0,8},{4,12},{8,0},{12,4},{1,9},{5,13},{9,1},{13,5},{2,10},{6,14},... | collective-permute-start | bytes 98312 | tf_op jit(solution)/shard_map/ppermute | solution.py:219
  40.7 4.5 %collective-permute-start.9 = (bf16[32,256]{1,0:T(8,128)(2,1)S(1)}, bf16[32,256]{1,0:T(8,128)(2,1)S(1)}, u32[]{:S(2)}, u32[]{:S(2)}) collective-permute-start(bf16[32,256]{1,0:T(8,128)(2,1)S(1)} %get-tuple-element.17.low), channel_id=1, source_target_pairs={{0,12},{4,0},{8,4},{12,8},{1,13},{5,1},{9,5},{13,9},{2,14},{6,2},{... | collective-permute-start | bytes 49160 | tf_op jit(solution)/shard_map/ppermute | solution.py:206
  43.3 4.6 %collective-permute-start.8 = (bf16[32,256]{1,0:T(8,128)(2,1)S(1)}, bf16[32,256]{1,0:T(8,128)(2,1)S(1)}, u32[]{:S(2)}, u32[]{:S(2)}) collective-permute-start(bf16[32,256]{1,0:T(8,128)(2,1)S(1)} %get-tuple-element.17.low), channel_id=1, source_target_pairs={{0,8},{4,12},{8,0},{12,4},{1,9},{5,13},{9,1},{13,5},{2,10},{6,14},... | collective-permute-start | bytes 49160 | tf_op jit(solution)/shard_map/ppermute | solution.py:206
  44.0 5.5 %collective-permute-start.7 = (bf16[32,256]{1,0:T(8,128)(2,1)S(1)}, bf16[32,256]{1,0:T(8,128)(2,1)S(1)}, u32[]{:S(2)}, u32[]{:S(2)}) collective-permute-start(bf16[32,256]{1,0:T(8,128)(2,1)S(1)} %get-tuple-element.17.low), channel_id=1, source_target_pairs={{0,4},{4,8},{8,12},{12,0},{1,5},{5,9},{9,13},{13,1},{2,6},{6,10},{... | collective-permute-start | bytes 49160 | tf_op jit(solution)/shard_map/ppermute | solution.py:206

commit v2 on v1

--- a/solution.py
+++ b/solution.py
@@ -18,63 +18,88 @@
 
 vmem_spec = pl.BlockSpec(memory_space=pltpu.VMEM)
 smem_spec = pl.BlockSpec(memory_space=pltpu.SMEM)
-any_spec = pl.BlockSpec(memory_space=pl.ANY)
+hbm_spec = pl.BlockSpec(memory_space=pltpu.HBM)
+
+
+def held(x):
+    return pltpu.with_memory_space_constraint(x, pltpu.HBM)
 
 
 def params(mib):
     return pltpu.CompilerParams(vmem_limit_bytes=mib * 1024 * 1024)
 
 
-def pack_kernel(place, owner, cells, z_ref, y_ref, out_ref):
-    half = z_ref.shape[0] // 2
-    slots = owner.shape[0]
-    start = pl.multiple_of(place[2] * half, half)
-    out_ref[0:half, :] = z_ref[pl.ds(start, half), :]
-    out_ref[half : 2 * half, :] = y_ref[pl.ds(start, half), :]
-    shape = (info_rows, z_ref.shape[1])
+def pack_kernel(owner, cells, z_hbm, y_hbm, out_ref, rest_ref, table_ref, sems):
+    half = z_hbm.shape[0] // 2
+    rank = z_hbm.shape[1]
+    slots = owner.shape[2]
+    parity = lax.rem(lax.axis_index("pb"), 2)
+    copies = []
+    for i, source in enumerate((z_hbm, y_hbm)):
+        for j, target in enumerate((out_ref, rest_ref)):
+            at = pl.multiple_of((parity if j == 0 else 1 - parity) * half, half)
+            copies.append(
+                pltpu.make_async_copy(
+                    source.at[pl.ds(at, half), :],
+                    target.at[i * half : (i + 1) * half, :],
+                    sems.at[2 * i + j],
+                )
+            )
+    for copy in copies:
+        copy.start()
+    shape = (info_rows, rank)
     row = lax.broadcasted_iota(jnp.int32, shape, 0)
     lane = lax.broadcasted_iota(jnp.int32, shape, 1)
     table = jnp.zeros(shape, jnp.int32)
     for s in range(slots):
-        for r, value in enumerate((owner[s] + 1, cells[2 * s], cells[2 * s + 1])):
-            table = jnp.where((row == r) & (lane == s), value, table)
+        values = (owner[0, 0, s], cells[0, 0, 0, s], cells[0, 0, 1, s])
+        for r, value in enumerate(values):
+            table_ref[r * slots + s] = value
+            shown = value + 1 if r == 0 else value
+            table = jnp.where((row == r) & (lane == s), shown, table)
     out_ref[2 * half :, :] = table.astype(f32).astype(bf16)
-
-
-def term_kernel(
-    ta_count, edge, place, owner, cells, x_ref, z_ref, y_ref, far_ref, pair_ref, blocks,
-    terms, full_z, full_y, info, cube, sems,
-):
-    slots, frames = cube.shape[0], cube.shape[1]
-    rows = z_ref.shape[0]
-    half = rows // 2
-    piece = 2 * half + info_rows
+    for copy in copies:
+        copy.wait()
+
+
+def load_kernel(blocks, cube, sems):
+    slots = cube.shape[0]
     copies = [pltpu.make_async_copy(blocks.at[0, 0, s], cube.at[s], sems.at[s]) for s in range(slots)]
     for copy in copies:
         copy.start()
-    me, parity = place[0], place[2]
-    mine = pl.multiple_of(me * rows, rows)
-    full_z[pl.ds(mine, rows), :] = z_ref[...]
-    full_y[pl.ds(mine, rows), :] = y_ref[...]
-    info[0:info_rows, :] = x_ref[2 * half :, :]
-    for k in range(1, ta_count):
+    for copy in copies:
+        copy.wait()
+
+
+def term_kernel(
+    ta_count, edge, table, near_ref, rest_ref, far_ref, pair_ref, cube, terms, full_z, full_y, info
+):
+    slots, frames = cube.shape[0], cube.shape[1]
+    half = rest_ref.shape[0] // 2
+    piece = 2 * half + info_rows
+    me = lax.axis_index("ta")
+    parity = lax.rem(lax.axis_index("pb"), 2)
+    for k in range(ta_count):
         base = (k - 1) * piece
-        source = lax.rem(me + (ta_count - k), ta_count) * rows
+        source = lax.rem(me + (ta_count - k), ta_count) * (2 * half)
         here = pl.multiple_of(source + parity * half, half)
         there = pl.multiple_of(source + (1 - parity) * half, half)
-        full_z[pl.ds(here, half), :] = far_ref[base : base + half, :]
-        full_y[pl.ds(here, half), :] = far_ref[base + half : base + 2 * half, :]
-        full_z[pl.ds(there, half), :] = pair_ref[base : base + half, :]
-        full_y[pl.ds(there, half), :] = pair_ref[base + half : base + 2 * half, :]
-        info[k * info_rows : (k + 1) * info_rows, :] = far_ref[base + 2 * half : base + piece, :]
+        one = near_ref if k == 0 else far_ref.at[base : base + piece, :]
+        two = rest_ref if k == 0 else pair_ref.at[base : base + piece, :]
+        full_z[pl.ds(here, half), :] = one[0:half, :]
+        full_y[pl.ds(here, half), :] = one[half : 2 * half, :]
+        full_z[pl.ds(there, half), :] = two[0:half, :]
+        full_y[pl.ds(there, half), :] = two[half : 2 * half, :]
+        info[k * info_rows : (k + 1) * info_rows, :] = one[2 * half : piece, :]
     terms[...] = jnp.zeros_like(terms)
     chunk = 8
     rank = full_z.shape[1]
     for s in range(slots):
-        copies[s].wait()
-        panel_z = full_z[pl.ds(pl.multiple_of(cells[2 * s] * edge, edge), edge), :].astype(f32)
-        panel_y = full_y[pl.ds(pl.multiple_of(cells[2 * s + 1] * edge, edge), edge), :]
-        u = owner[s]
+        at = pl.multiple_of(table[slots + s] * edge, edge)
+        panel_z = full_z[pl.ds(at, edge), :].astype(f32)
+        at = pl.multiple_of(table[2 * slots + s] * edge, edge)
+        panel_y = full_y[pl.ds(at, edge), :]
+        u = table[s]
         live = u >= 0
         k = lax.rem(jnp.maximum(u, 0) + (ta_count - me), ta_count)
         for f in range(0, frames, chunk):
@@ -85,10 +110,10 @@
             terms[at, :] += jnp.where(live, summed, 0.0)
 
 
-def system_kernel(ta_count, slots, edge, place, info, full_z, full_y, system, inverse, codes):
+def system_kernel(ta_count, slots, edge, info, full_z, full_y, system, inverse, codes):
     rank = full_z.shape[1]
     grid = full_z.shape[0] // edge
-    me = place[0]
+    me = lax.axis_index("ta")
     lane = lax.broadcasted_iota(jnp.int32, (1, rank), 1)
     for k in range(ta_count):
         table = info[k * info_rows : (k + 1) * info_rows, :].astype(f32)
@@ -166,27 +191,23 @@
     low_out[...] = rows.astype(bf16)
 
 
-def misfit_kernel(
-    ta_count, edge, place, owner, cells, low, far, full_z, full_y, blocks, out, cube, every, sems
-):
+def misfit_kernel(ta_count, edge, table, low, far, full_z, full_y, cube, out, every):
     slots, frames = cube.shape[0], cube.shape[1]
-    copies = [pltpu.make_async_copy(blocks.at[0, 0, s], cube.at[s], sems.at[s]) for s in range(slots)]
-    for copy in copies:
-        copy.start()
     every[0] = low[...].astype(f32)
     for k in range(1, ta_count):
         every[k] = far[(k - 1) * frames : k * frames, :].astype(f32)
-    me = place[0]
+    me = lax.axis_index("ta")
     chunk = 8
     rank = full_z.shape[1]
     lane = lax.broadcasted_iota(jnp.int32, out.shape, 1)
     answer = jnp.zeros(out.shape, f32)
     over = (((1,), (1,)), ((), ()))
     for s in range(slots):
-        copies[s].wait()
-        panel_z = full_z[pl.ds(pl.multiple_of(cells[2 * s] * edge, edge), edge), :].astype(f32)
-        panel_y = full_y[pl.ds(pl.multiple_of(cells[2 * s + 1] * edge, edge), edge), :]
-        u = owner[s]
+        at = pl.multiple_of(table[slots + s] * edge, edge)
+        panel_z = full_z[pl.ds(at, edge), :].astype(f32)
+        at = pl.multiple_of(table[2 * slots + s] * edge, edge)
+        panel_y = full_y[pl.ds(at, edge), :]
+        u = table[s]
         k = lax.rem(me + (ta_count - jnp.maximum(u, 0)), ta_count)
         total = jnp.zeros((8, edge), f32)
         for f in range(0, frames, chunk):
@@ -239,20 +260,33 @@
     rows, rank = qz_factor.shape
     half = rows // 2
     piece = 2 * half + info_rows
-    me, column = lax.axis_index("ta"), lax.axis_index("pb")
-    place = jnp.stack([me, column, column % 2]).astype(jnp.int32)
-    owner = block_owner.reshape(slots)
-    cells = block_cells.reshape(slots * 2)
     shape = jax.ShapeDtypeStruct
-    packed = pl.pallas_call(
+    packed, rest, table = pl.pallas_call(
         pack_kernel,
-        out_shape=shape((piece, rank), bf16),
-        in_specs=[smem_spec] * 3 + [vmem_spec] * 2,
-        out_specs=vmem_spec,
+        out_shape=[
+            shape((piece, rank), bf16),
+            shape((2 * half, rank), bf16),
+            shape((3 * slots,), jnp.int32),
+        ],
+        in_specs=[smem_spec] * 2 + [hbm_spec] * 2,
+        out_specs=[vmem_spec] * 2 + [smem_spec],
+        scratch_shapes=[pltpu.SemaphoreType.DMA((4,))],
         compiler_params=params(4),
         name="pack",
-    )(place, owner, cells, qz_factor, qy_factor)
-    far = around(packed, "ta", ta_count)
+    )(*(held(x) for x in (block_owner, jnp.swapaxes(block_cells, 2, 3), qz_factor, qy_factor)))
+    cube = pl.pallas_call(
+        load_kernel,
+        out_shape=shape((slots, frames, edge, edge), bf16),
+        in_specs=[hbm_spec],
+        out_specs=vmem_spec,
+        scratch_shapes=[pltpu.SemaphoreType.DMA((slots,))],
+        compiler_params=params(8),
+        cost_estimate=pl.CostEstimate(
+            flops=0, transcendentals=0, bytes_accessed=4 * slots * frames * edge * edge
+        ),
+        name="load",
+    )(held(blocks))
+    far, cube = lax.optimization_barrier((around(packed, "ta", ta_count), cube))
     pair = lax.ppermute(far, "pb", [(i, i ^ 1) for i in range(pb_count)])
     terms, full_z, full_y, info = pl.pallas_call(
         functools.partial(term_kernel, ta_count, edge),
@@ -262,25 +296,21 @@
             shape((ta_count * rows, rank), bf16),
             shape((ta_count * info_rows, rank), bf16),
         ],
-        in_specs=[smem_spec] * 3 + [vmem_spec] * 5 + [any_spec],
+        in_specs=[smem_spec] + [vmem_spec] * 5,
         out_specs=[vmem_spec] * 4,
-        scratch_shapes=[
-            pltpu.VMEM((slots, frames, edge, edge), bf16),
-            pltpu.SemaphoreType.DMA((slots,)),
-        ],
-        compiler_params=params(24),
+        compiler_params=params(16),
         name="terms",
-    )(place, owner, cells, packed, qz_factor, qy_factor, far, pair, blocks)
+    )(table, packed, rest, far, pair, cube)
     arrived = deliver(terms, "ta", ta_count)
     system, inverse = pl.pallas_call(
         functools.partial(system_kernel, ta_count, slots, edge),
         out_shape=[shape((rank, rank), f32)] * 2,
-        in_specs=[smem_spec] + [vmem_spec] * 3,
+        in_specs=[vmem_spec] * 3,
         out_specs=[vmem_spec] * 2,
         scratch_shapes=[pltpu.SMEM((ta_count * slots,), jnp.int32)],
         compiler_params=params(16),
         name="system",
-    )(place, info, full_z, full_y)
+    )(info, full_z, full_y)
     new_rows, low = pl.pallas_call(
         functools.partial(solve_kernel, ta_count),
         out_shape=[shape((frames, rank), f32), shape((frames, rank), bf16)],
@@ -293,16 +323,12 @@
     misfit = pl.pallas_call(
         functools.partial(misfit_kernel, ta_count, edge),
         out_shape=shape((1, slots), f32),
-        in_specs=[smem_spec] * 3 + [vmem_spec] * 4 + [any_spec],
+        in_specs=[smem_spec] + [vmem_spec] * 5,
         out_specs=vmem_spec,
-        scratch_shapes=[
-            pltpu.VMEM((slots, frames, edge, edge), bf16),
-            pltpu.VMEM((ta_count, frames, rank), f32),
-            pltpu.SemaphoreType.DMA((slots,)),
-        ],
-        compiler_params=params(24),
+        scratch_shapes=[pltpu.VMEM((ta_count, frames, rank), f32)],
+        compiler_params=params(16),
         name="misfit",
-    )(place, owner, cells, low, others, full_z, full_y, blocks)
+    )(table, low, others, full_z, full_y, cube)
     return (new_rows, misfit.reshape(1, 1, slots))
 
 

time: 54.6 us -> 46 us (0.84)
  local copies, waits for them, and re-layouts: 8.01 us -> 0.01 us
  starting transfers between devices: 16.8 us -> 15 us
  Pallas kernels: 14.4 us -> 15.7 us
    unnamed x19 -> x0, local copies, waits for them, and re-layouts: 7.9 us -> none
    pallas_call x1 -> x2, Pallas kernels: 0.57 us -> 4.47 us  [the longest x1 2.27 us: body(): pl.pallas_call(pack_kernel, out_shape=[shape((piece, rank), bf16), shape(...]
    ppermute x6, starting transfers between devices: 11.6 us -> 10.1 us  [around(): lax.ppermute(x, axis, [(i, (i + k) % count) for i in range(count)])]
    pallas_call x1, Pallas kernels: 4.72 us -> 3.54 us  [body(): pl.pallas_call(functools.partial(misfit_kernel, ta_count, edge), out_shap...]
    pallas_call x1, Pallas kernels: 3.78 us -> 2.95 us  [body(): pl.pallas_call(functools.partial(term_kernel, ta_count, edge), out_shape=...]
    pallas_call x1, Pallas kernels: 3.86 us -> 3.31 us  [body(): pl.pallas_call(functools.partial(system_kernel, ta_count, slots, edge), o...]
  transfers between devices with their start and end apart: 10 -> 10, of which waited for: 6 -> 6; matrix products, arithmetic and copies ran while one was open for 0% -> 0% of each run, Pallas kernels for 7% -> 12%
where the time goes in v2:
time: 46 us; the launch traced here: 45.9 us
  Pallas kernels  15.7 us (34%)
  starting transfers between devices  15 us (33%)
  waiting for transfers between devices  14.4 us (31%)
  between operations  0.71 us (2%)
    ppermute x6, waiting for transfers between devices, around(): lax.ppermute(x, axis, [(i, (i + k) % count) for i in range(count)])  12.1 us
    ppermute x6, starting transfers between devices, around(): lax.ppermute(x, axis, [(i, (i + k) % count) for i in range(count)])  10.1 us
    ppermute x3, starting transfers between devices, deliver(): lax.ppermute(terms[k * frames:(k + 1) * frames], axis, [(i, (i + k) % cou...  4.81 us
    pallas_call x1, Pallas kernels, body(): pl.pallas_call(functools.partial(misfit_kernel, ta_count, edge), out_shap...  3.54 us
    pallas_call x1, Pallas kernels, body(): pl.pallas_call(functools.partial(system_kernel, ta_count, slots, edge), o...  3.31 us
    pallas_call x1, Pallas kernels, body(): pl.pallas_call(functools.partial(term_kernel, ta_count, edge), out_shape=...  2.95 us
    pallas_call x1, Pallas kernels, body(): pl.pallas_call(pack_kernel, out_shape=[shape((piece, rank), bf16), shape(...  2.27 us
    pallas_call x1, Pallas kernels, body(): pl.pallas_call(load_kernel, out_shape=shape((slots, frames, edge, edge),...  2.2 us
  transfers between devices with their start and end apart: 10, of which 6 were waited for; matrix products, arithmetic and copies ran while one was open for 0% of the time, Pallas kernels for 12%

profile of v2, /device:TPU:0, one launch (start us, length us, event | category | flops | bytes accessed | tf_op | source)
XLA Modules:
  0.0 45.9 jit_solution(9215591056571816756)
XLA Ops:
  0.6 2.3 %pack.1 = (bf16[272,256]{1,0:T(8,128)(2,1)S(1)}, bf16[256,256]{1,0:T(8,128)(2,1)S(1)}, s32[12]{0:T(128)S(1)}) custom-call(s32[1,1,4]{2,1,0:T(1,128)} %owner.1, s32[1,1,2,4]{3,2,1,0:T(2,128)} %bitcast.2, bf16[256,256]{1,0:T(8,128)(2,1)} %z_hbm.1, bf16[256,256]{1,0:T(8,128)(2,1)} %y_hbm.1), custom_call_target="tpu_custom_call" | custom-call | tf_op jit(solution)/shard_map/pack/pallas_call | solution.py:264
  2.9 5.1 %collective-permute-start.2 = (bf16[272,256]{1,0:T(8,128)(2,1)S(1)}, bf16[272,256]{1,0:T(8,128)(2,1)S(1)}, u32[]{:S(2)}, u32[]{:S(2)}) collective-permute-start(bf16[272,256]{1,0:T(8,128)(2,1)S(1)} %get-tuple-element.16.near_ref), channel_id=1, source_target_pairs={{0,12},{4,0},{8,4},{12,8},{1,13},{5,1},{9,5},{13,9},{2,14},{6,2},{... | collective-permute-start | bytes 417800 | tf_op jit(solution)/shard_map/ppermute | solution.py:227
  8.0 0.0 collective-permute-start.1
  8.0 1.0 %collective-permute-start = (bf16[272,256]{1,0:T(8,128)(2,1)S(1)}, bf16[272,256]{1,0:T(8,128)(2,1)S(1)}, u32[]{:S(2)}, u32[]{:S(2)}) collective-permute-start(bf16[272,256]{1,0:T(8,128)(2,1)S(1)} %get-tuple-element.16.near_ref), channel_id=1, source_target_pairs={{0,4},{4,8},{8,12},{12,0},{1,5},{5,9},{9,13},{13,1},{2,6},{6,10},{... | collective-permute-start | bytes 417800 | tf_op jit(solution)/shard_map/ppermute | solution.py:227
  9.1 2.2 %load.1.cube = bf16[4,32,128,128]{3,2,1,0:T(8,128)(2,1)S(1)} custom-call(bf16[1,1,4,32,128,128]{5,4,3,2,1,0:T(8,128)(2,1)} %blocks.1), custom_call_target="tpu_custom_call" | custom-call | bytes 8388608 | tf_op jit(solution)/shard_map/load/pallas_call | solution.py:277
  11.3 0.9 %collective-permute-done.2 = bf16[272,256]{1,0:T(8,128)(2,1)S(1)} collective-permute-done((bf16[272,256]{1,0:T(8,128)(2,1)S(1)}, bf16[272,256]{1,0:T(8,128)(2,1)S(1)}, u32[]{:S(2)}, u32[]{:S(2)}) %collective-permute-start.2) | collective-permute-done | bytes 139296 | tf_op jit(solution)/shard_map/ppermute | solution.py:227
  12.1 7.7 %collective-permute-done.1 = bf16[272,256]{1,0:T(8,128)(2,1)S(1)} collective-permute-done((bf16[272,256]{1,0:T(8,128)(2,1)S(1)}, bf16[272,256]{1,0:T(8,128)(2,1)S(1)}, u32[]{:S(2)}, u32[]{:S(2)}) %collective-permute-start.1) | collective-permute-done | bytes 139296 | tf_op jit(solution)/shard_map/ppermute | solution.py:227
  19.9 0.0 collective-permute-done
  19.9 0.1 collective-permute-start.3
  20.0 1.7 %collective-permute-done.3.pair_ref = bf16[816,256]{1,0:T(8,128)(2,1)S(1)} collective-permute-done((bf16[816,256]{1,0:T(8,128)(2,1)S(1)}, bf16[816,256]{1,0:T(8,128)(2,1)S(1)}, u32[]{:S(2)}, u32[]{:S(2)}) %collective-permute-start.3) | collective-permute-done | bytes 417824 | tf_op jit(solution)/shard_map/ppermute | solution.py:290
  21.7 2.9 %terms.1 = (f32[128,256]{1,0:T(8,128)S(1)}, bf16[1024,256]{1,0:T(8,128)(2,1)S(1)}, bf16[1024,256]{1,0:T(8,128)(2,1)S(1)}, bf16[64,256]{1,0:T(8,128)(2,1)S(1)}) custom-call(s32[12]{0:T(128)S(1)} %get-tuple-element.15.table, bf16[272,256]{1,0:T(8,128)(2,1)S(1)} %get-tuple-element.16.near_ref, bf16[256,256]{1,0:T(8,128)(2,1)S(1)} %get-tuple-element.17.rest_ref, ...), custom_call_target="tpu_custom_call" | custom-call | tf_op jit(solution)/shard_map/terms/pallas_call | solution.py:291
  24.7 0.9 %collective-permute-start.4 = (f32[32,256]{1,0:T(8,128)S(1)}, f32[32,256]{1,0:T(8,128)S(1)}, u32[]{:S(2)}, u32[]{:S(2)}) collective-permute-start(f32[32,256]{1,0:T(8,128)S(1)} %get-tuple-element.28), channel_id=1, source_target_pairs={{0,4},{4,8},{8,12},{12,0},{1,5},{5,9},{9,13},{13,1},{2,6},{6,10},{... | collective-permute-start | bytes 98312 | tf_op jit(solution)/shard_map/ppermute | solution.py:240
  25.6 3.0 %collective-permute-start.6 = (f32[32,256]{1,0:T(8,128)S(1)}, f32[32,256]{1,0:T(8,128)S(1)}, u32[]{:S(2)}, u32[]{:S(2)}) collective-permute-start(f32[32,256]{1,0:T(8,128)S(1)} %get-tuple-element.29), channel_id=1, source_target_pairs={{0,12},{4,0},{8,4},{12,8},{1,13},{5,1},{9,5},{13,9},{2,14},{6,2},{... | collective-permute-start | bytes 98312 | tf_op jit(solution)/shard_map/ppermute | solution.py:240
  28.6 0.9 %collective-permute-start.5 = (f32[32,256]{1,0:T(8,128)S(1)}, f32[32,256]{1,0:T(8,128)S(1)}, u32[]{:S(2)}, u32[]{:S(2)}) collective-permute-start(f32[32,256]{1,0:T(8,128)S(1)} %get-tuple-element.30), channel_id=1, source_target_pairs={{0,8},{4,12},{8,0},{12,4},{1,9},{5,13},{9,1},{13,5},{2,10},{6,14},... | collective-permute-start | bytes 98312 | tf_op jit(solution)/shard_map/ppermute | solution.py:240
  29.5 3.3 %system.1 = (f32[256,256]{1,0:T(8,128)S(1)}, f32[256,256]{1,0:T(8,128)S(1)}) custom-call(bf16[64,256]{1,0:T(8,128)(2,1)S(1)} %get-tuple-element.21.info, bf16[1024,256]{1,0:T(8,128)(2,1)S(1)} %get-tuple-element.22.full_z, bf16[1024,256]{1,0:T(8,128)(2,1)S(1)} %get-tuple-element.23.full_y), custom_call_target="tpu_custom_call" | custom-call | tf_op jit(solution)/shard_map/system/pallas_call | solution.py:305
  32.8 0.0 collective-permute-done.4
  32.8 0.0 collective-permute-done.6
  32.8 0.5 %collective-permute-done.5 = f32[32,256]{1,0:T(8,128)S(1)} collective-permute-done((f32[32,256]{1,0:T(8,128)S(1)}, f32[32,256]{1,0:T(8,128)S(1)}, u32[]{:S(2)}, u32[]{:S(2)}) %collective-permute-start.5) | collective-permute-done | bytes 32800 | tf_op jit(solution)/shard_map/ppermute | solution.py:240
  33.4 1.4 %solve.1 = (f32[32,256]{1,0:T(8,128)}, bf16[32,256]{1,0:T(8,128)(2,1)S(1)}) custom-call(f32[128,256]{1,0:T(8,128)S(1)} %get-tuple-element.20.own, f32[96,256]{1,0:T(8,128)S(1)} %pad_maximum_fusion.1.far, f32[256,256]{1,0:T(8,128)S(1)} %get-tuple-element.24.system, f32[256,256]{1,0:T(8,128)S(1)} %get-tuple-element.25.inverse), custom_call_target="tpu_custom_call" | custom-call | tf_op jit(solution)/shard_map/solve/pallas_call | solution.py:314
  34.8 1.1 %collective-permute-start.9 = (bf16[32,256]{1,0:T(8,128)(2,1)S(1)}, bf16[32,256]{1,0:T(8,128)(2,1)S(1)}, u32[]{:S(2)}, u32[]{:S(2)}) collective-permute-start(bf16[32,256]{1,0:T(8,128)(2,1)S(1)} %get-tuple-element.27.low), channel_id=1, source_target_pairs={{0,12},{4,0},{8,4},{12,8},{1,13},{5,1},{9,5},{13,9},{2,14},{6,2},{... | collective-permute-start | bytes 49160 | tf_op jit(solution)/shard_map/ppermute | solution.py:227
  36.0 0.8 %collective-permute-start.8 = (bf16[32,256]{1,0:T(8,128)(2,1)S(1)}, bf16[32,256]{1,0:T(8,128)(2,1)S(1)}, u32[]{:S(2)}, u32[]{:S(2)}) collective-permute-start(bf16[32,256]{1,0:T(8,128)(2,1)S(1)} %get-tuple-element.27.low), channel_id=1, source_target_pairs={{0,8},{4,12},{8,0},{12,4},{1,9},{5,13},{9,1},{13,5},{2,10},{6,14},... | collective-permute-start | bytes 49160 | tf_op jit(solution)/shard_map/ppermute | solution.py:227
  36.8 2.0 %collective-permute-start.7 = (bf16[32,256]{1,0:T(8,128)(2,1)S(1)}, bf16[32,256]{1,0:T(8,128)(2,1)S(1)}, u32[]{:S(2)}, u32[]{:S(2)}) collective-permute-start(bf16[32,256]{1,0:T(8,128)(2,1)S(1)} %get-tuple-element.27.low), channel_id=1, source_target_pairs={{0,4},{4,8},{8,12},{12,0},{1,5},{5,9},{9,13},{13,1},{2,6},{6,10},{... | collective-permute-start | bytes 49160 | tf_op jit(solution)/shard_map/ppermute | solution.py:227
  38.8 0.0 collective-permute-done.9
  38.8 1.8 %collective-permute-done.8 = bf16[32,256]{1,0:T(8,128)(2,1)S(1)} collective-permute-done((bf16[32,256]{1,0:T(8,128)(2,1)S(1)}, bf16[32,256]{1,0:T(8,128)(2,1)S(1)}, u32[]{:S(2)}, u32[]{:S(2)}) %collective-permute-start.8) | collective-permute-done | bytes 16416 | tf_op jit(solution)/shard_map/ppermute | solution.py:227
  40.6 1.7 %collective-permute-done.7 = bf16[32,256]{1,0:T(8,128)(2,1)S(1)} collective-permute-done((bf16[32,256]{1,0:T(8,128)(2,1)S(1)}, bf16[32,256]{1,0:T(8,128)(2,1)S(1)}, u32[]{:S(2)}, u32[]{:S(2)}) %collective-permute-start.7) | collective-permute-done | bytes 16416 | tf_op jit(solution)/shard_map/ppermute | solution.py:227
  42.4 3.5 %misfit.1 = f32[1,4]{1,0:T(1,128)} custom-call(s32[12]{0:T(128)S(1)} %get-tuple-element.15.table, bf16[32,256]{1,0:T(8,128)(2,1)S(1)} %get-tuple-element.27.low, bf16[96,256]{1,0:T(8,128)(2,1)S(1)} %pad_maximum_fusion.2.far, bf16[1024,256]{1,0:T(8,128)(2,1)S(1)} %get-tuple-element.22.full_z, bf16[1024,256]{1,0:T(8,128)(2,1)S(1)} %get-tuple-element.23.full_y, ...), custom_call_target="tpu_custom_call" | custom-call | tf_op jit(solution)/shard_map/misfit/pallas_call | solution.py:323
  (4 shorter events, 0.0 us)
Async XLA Ops:
  2.9 9.2 %collective-permute-start.2 = (bf16[272,256]{1,0:T(8,128)(2,1)S(1)}, bf16[272,256]{1,0:T(8,128)(2,1)S(1)}, u32[]{:S(2)}, u32[]{:S(2)}) collective-permute-start(bf16[272,256]{1,0:T(8,128)(2,1)S(1)} %get-tuple-element.16.near_ref), channel_id=1, source_target_pairs={{0,12},{4,0},{8,4},{12,8},{1,13},{5,1},{9,5},{13,9},{2,14},{6,2},{... | collective-permute-start | bytes 417800 | tf_op jit(solution)/shard_map/ppermute | solution.py:227
  8.0 11.8 %collective-permute-start.1 = (bf16[272,256]{1,0:T(8,128)(2,1)S(1)}, bf16[272,256]{1,0:T(8,128)(2,1)S(1)}, u32[]{:S(2)}, u32[]{:S(2)}) collective-permute-start(bf16[272,256]{1,0:T(8,128)(2,1)S(1)} %get-tuple-element.16.near_ref), channel_id=1, source_target_pairs={{0,8},{4,12},{8,0},{12,4},{1,9},{5,13},{9,1},{13,5},{2,10},{6,14},... | collective-permute-start | bytes 417800 | tf_op jit(solution)/shard_map/ppermute | solution.py:227
  8.0 11.8 %collective-permute-start = (bf16[272,256]{1,0:T(8,128)(2,1)S(1)}, bf16[272,256]{1,0:T(8,128)(2,1)S(1)}, u32[]{:S(2)}, u32[]{:S(2)}) collective-permute-start(bf16[272,256]{1,0:T(8,128)(2,1)S(1)} %get-tuple-element.16.near_ref), channel_id=1, source_target_pairs={{0,4},{4,8},{8,12},{12,0},{1,5},{5,9},{9,13},{13,1},{2,6},{6,10},{... | collective-permute-start | bytes 417800 | tf_op jit(solution)/shard_map/ppermute | solution.py:227
  19.9 1.8 %collective-permute-start.3 = (bf16[816,256]{1,0:T(8,128)(2,1)S(1)}, bf16[816,256]{1,0:T(8,128)(2,1)S(1)}, u32[]{:S(2)}, u32[]{:S(2)}) collective-permute-start(bf16[816,256]{1,0:T(8,128)(2,1)S(1)} %pad_maximum_fusion.far_ref), channel_id=1, source_target_pairs={{0,1},{1,0},{2,3},{3,2},{4,5},{5,4},{6,7},{7,6},{8,9},{9,8},{10,11... | collective-permute-start | bytes 1253384 | tf_op jit(solution)/shard_map/ppermute | solution.py:290
  24.7 8.1 %collective-permute-start.4 = (f32[32,256]{1,0:T(8,128)S(1)}, f32[32,256]{1,0:T(8,128)S(1)}, u32[]{:S(2)}, u32[]{:S(2)}) collective-permute-start(f32[32,256]{1,0:T(8,128)S(1)} %get-tuple-element.28), channel_id=1, source_target_pairs={{0,4},{4,8},{8,12},{12,0},{1,5},{5,9},{9,13},{13,1},{2,6},{6,10},{... | collective-permute-start | bytes 98312 | tf_op jit(solution)/shard_map/ppermute | solution.py:240
  25.6 7.3 %collective-permute-start.6 = (f32[32,256]{1,0:T(8,128)S(1)}, f32[32,256]{1,0:T(8,128)S(1)}, u32[]{:S(2)}, u32[]{:S(2)}) collective-permute-start(f32[32,256]{1,0:T(8,128)S(1)} %get-tuple-element.29), channel_id=1, source_target_pairs={{0,12},{4,0},{8,4},{12,8},{1,13},{5,1},{9,5},{13,9},{2,14},{6,2},{... | collective-permute-start | bytes 98312 | tf_op jit(solution)/shard_map/ppermute | solution.py:240
  28.6 4.8 %collective-permute-start.5 = (f32[32,256]{1,0:T(8,128)S(1)}, f32[32,256]{1,0:T(8,128)S(1)}, u32[]{:S(2)}, u32[]{:S(2)}) collective-permute-start(f32[32,256]{1,0:T(8,128)S(1)} %get-tuple-element.30), channel_id=1, source_target_pairs={{0,8},{4,12},{8,0},{12,4},{1,9},{5,13},{9,1},{13,5},{2,10},{6,14},... | collective-permute-start | bytes 98312 | tf_op jit(solution)/shard_map/ppermute | solution.py:240
  34.8 4.0 %collective-permute-start.9 = (bf16[32,256]{1,0:T(8,128)(2,1)S(1)}, bf16[32,256]{1,0:T(8,128)(2,1)S(1)}, u32[]{:S(2)}, u32[]{:S(2)}) collective-permute-start(bf16[32,256]{1,0:T(8,128)(2,1)S(1)} %get-tuple-element.27.low), channel_id=1, source_target_pairs={{0,12},{4,0},{8,4},{12,8},{1,13},{5,1},{9,5},{13,9},{2,14},{6,2},{... | collective-permute-start | bytes 49160 | tf_op jit(solution)/shard_map/ppermute | solution.py:227
  36.0 4.6 %collective-permute-start.8 = (bf16[32,256]{1,0:T(8,128)(2,1)S(1)}, bf16[32,256]{1,0:T(8,128)(2,1)S(1)}, u32[]{:S(2)}, u32[]{:S(2)}) collective-permute-start(bf16[32,256]{1,0:T(8,128)(2,1)S(1)} %get-tuple-element.27.low), channel_id=1, source_target_pairs={{0,8},{4,12},{8,0},{12,4},{1,9},{5,13},{9,1},{13,5},{2,10},{6,14},... | collective-permute-start | bytes 49160 | tf_op jit(solution)/shard_map/ppermute | solution.py:227
  36.8 5.5 %collective-permute-start.7 = (bf16[32,256]{1,0:T(8,128)(2,1)S(1)}, bf16[32,256]{1,0:T(8,128)(2,1)S(1)}, u32[]{:S(2)}, u32[]{:S(2)}) collective-permute-start(bf16[32,256]{1,0:T(8,128)(2,1)S(1)} %get-tuple-element.27.low), channel_id=1, source_target_pairs={{0,4},{4,8},{8,12},{12,0},{1,5},{5,9},{9,13},{13,1},{2,6},{6,10},{... | collective-permute-start | bytes 49160 | tf_op jit(solution)/shard_map/ppermute | solution.py:227

commit v3 on v2

--- a/solution.py
+++ b/solution.py
@@ -9,7 +9,7 @@
 
 ridge_weight = 0.1
 info_rows = 16
-ring_limit = 8
+swap_limit = 8
 newton_steps = 10
 newton_goal = 4e-4
 top = lax.Precision.HIGHEST
@@ -29,24 +29,37 @@
     return pltpu.CompilerParams(vmem_limit_bytes=mib * 1024 * 1024)
 
 
-def pack_kernel(owner, cells, z_hbm, y_hbm, out_ref, rest_ref, table_ref, sems):
+def pack_kernel(owner_hbm, cells_hbm, z_hbm, y_hbm, half_ref, part_ref, rest_ref, table_ref, owner, cells, sems):
     half = z_hbm.shape[0] // 2
+    part = half // 2
     rank = z_hbm.shape[1]
     slots = owner.shape[2]
-    parity = lax.rem(lax.axis_index("pb"), 2)
+    column = lax.axis_index("pb")
+    core = lax.rem(column, 2)
+    side = lax.rem(lax.div(column, 2), 2)
+    small = [
+        pltpu.make_async_copy(owner_hbm, owner, sems.at[6]),
+        pltpu.make_async_copy(cells_hbm, cells, sems.at[7]),
+    ]
     copies = []
-    for i, source in enumerate((z_hbm, y_hbm)):
-        for j, target in enumerate((out_ref, rest_ref)):
-            at = pl.multiple_of((parity if j == 0 else 1 - parity) * half, half)
+    pieces = (
+        (half_ref, core * half, half),
+        (part_ref, core * half + side * part, part),
+        (rest_ref, (1 - core) * half, half),
+    )
+    for i, (target, at, count) in enumerate(pieces):
+        for j, source in enumerate((z_hbm, y_hbm)):
             copies.append(
                 pltpu.make_async_copy(
-                    source.at[pl.ds(at, half), :],
-                    target.at[i * half : (i + 1) * half, :],
+                    source.at[pl.ds(pl.multiple_of(at, count), count), :],
+                    target.at[j * count : (j + 1) * count, :],
                     sems.at[2 * i + j],
                 )
             )
-    for copy in copies:
+    for copy in small + copies:
         copy.start()
+    for copy in small:
+        copy.wait()
     shape = (info_rows, rank)
     row = lax.broadcasted_iota(jnp.int32, shape, 0)
     lane = lax.broadcasted_iota(jnp.int32, shape, 1)
@@ -57,9 +70,16 @@
             table_ref[r * slots + s] = value
             shown = value + 1 if r == 0 else value
             table = jnp.where((row == r) & (lane == s), shown, table)
-    out_ref[2 * half :, :] = table.astype(f32).astype(bf16)
+    table = table.astype(f32).astype(bf16)
+    half_ref[2 * half :, :] = table
+    part_ref[2 * part :, :] = table
     for copy in copies:
         copy.wait()
+
+
+def distance(u, me, swaps):
+    u = jnp.maximum(u, 0)
+    return lax.bitwise_xor(u, me) if swaps else u
 
 
 def load_kernel(blocks, cube, sems):
@@ -71,26 +91,51 @@
         copy.wait()
 
 
-def term_kernel(
-    ta_count, edge, table, near_ref, rest_ref, far_ref, pair_ref, cube, terms, full_z, full_y, info
-):
+def assemble(near, part, rest, first, away, side_away, mate, full_z, full_y, info):
+    half = rest.shape[0] // 2
+    quarter = half // 2
+    rows = 2 * half
+    tall = 2 * half + info_rows
+    short = 2 * quarter + info_rows
+    me = lax.axis_index("ta")
+    column = lax.axis_index("pb")
+    core = lax.rem(column, 2)
+    side = lax.rem(lax.div(column, 2), 2)
+
+    def put(ref, base, at, count):
+        at = pl.ds(pl.multiple_of(at, count), count)
+        full_z[at, :] = ref[base : base + count, :]
+        full_y[at, :] = ref[base + count : base + 2 * count, :]
+
+    info[0:info_rows, :] = near[2 * half :, :]
+    put(near, 0, me * rows + core * half, half)
+    put(rest, 0, me * rows + (1 - core) * half, half)
+    info[info_rows : 2 * info_rows, :] = first[2 * half :, :]
+    source = lax.bitwise_xor(me, 1) * rows
+    put(first, 0, source + core * half, half)
+    put(mate, 0, source + (1 - core) * half, half)
+    others = away.shape[0] // short
+    for i in range(others):
+        source = lax.bitwise_xor(me, i + 2) * rows
+        base = i * short
+        info[(i + 2) * info_rows : (i + 3) * info_rows, :] = away[base + 2 * quarter : base + short, :]
+        for ref, start, which, where in (
+            (away, 0, core, side),
+            (side_away, 0, core, 1 - side),
+            (mate, tall, 1 - core, side),
+            (mate, tall + others * short, 1 - core, 1 - side),
+        ):
+            put(ref, start + base, source + which * half + where * quarter, quarter)
+
+
+def term_kernel(ta_count, edge, swaps, table, cube, *refs):
+    if swaps:
+        pieces, (terms, full_z, full_y, info) = refs[:-4], refs[-4:]
+        assemble(*pieces, full_z, full_y, info)
+    else:
+        full_z, full_y, terms = refs
     slots, frames = cube.shape[0], cube.shape[1]
-    half = rest_ref.shape[0] // 2
-    piece = 2 * half + info_rows
     me = lax.axis_index("ta")
-    parity = lax.rem(lax.axis_index("pb"), 2)
-    for k in range(ta_count):
-        base = (k - 1) * piece
-        source = lax.rem(me + (ta_count - k), ta_count) * (2 * half)
-        here = pl.multiple_of(source + parity * half, half)
-        there = pl.multiple_of(source + (1 - parity) * half, half)
-        one = near_ref if k == 0 else far_ref.at[base : base + piece, :]
-        two = rest_ref if k == 0 else pair_ref.at[base : base + piece, :]
-        full_z[pl.ds(here, half), :] = one[0:half, :]
-        full_y[pl.ds(here, half), :] = one[half : 2 * half, :]
-        full_z[pl.ds(there, half), :] = two[0:half, :]
-        full_y[pl.ds(there, half), :] = two[half : 2 * half, :]
-        info[k * info_rows : (k + 1) * info_rows, :] = one[2 * half : piece, :]
     terms[...] = jnp.zeros_like(terms)
     chunk = 8
     rank = full_z.shape[1]
@@ -101,7 +146,7 @@
         panel_y = full_y[pl.ds(at, edge), :]
         u = table[s]
         live = u >= 0
-        k = lax.rem(jnp.maximum(u, 0) + (ta_count - me), ta_count)
+        k = distance(u, me, swaps)
         for f in range(0, frames, chunk):
             part = cube[s, f : f + chunk].reshape(chunk * edge, edge)
             inner = jnp.dot(part, panel_y, preferred_element_type=f32)
@@ -178,11 +223,16 @@
             inverse[...] = jnp.where(subs == k, scaled, rest)
 
 
-def solve_kernel(ta_count, own, far, system, inverse, rows_out, low_out):
+def solve_kernel(ta_count, swaps, own, far, system, inverse, rows_out, low_out):
     frames = rows_out.shape[0]
-    rhs = own[0:frames, :]
-    for k in range(1, ta_count):
-        rhs = rhs + far[(k - 1) * frames : k * frames, :]
+    if swaps:
+        rhs = own[0:frames, :]
+        for k in range(1, ta_count):
+            rhs = rhs + far[(k - 1) * frames : k * frames, :]
+    else:
+        rhs = far[0:frames, :]
+        for k in range(1, ta_count):
+            rhs = rhs + far[k * frames : (k + 1) * frames, :]
     dot = functools.partial(jnp.dot, precision=top, preferred_element_type=f32)
     rows = dot(rhs, inverse[...])
     rest = rhs - dot(rows, system[...])
@@ -191,11 +241,13 @@
     low_out[...] = rows.astype(bf16)
 
 
-def misfit_kernel(ta_count, edge, table, low, far, full_z, full_y, cube, out, every):
+def misfit_kernel(ta_count, edge, swaps, table, low, far, full_z, full_y, cube, out, every):
     slots, frames = cube.shape[0], cube.shape[1]
-    every[0] = low[...].astype(f32)
-    for k in range(1, ta_count):
-        every[k] = far[(k - 1) * frames : k * frames, :].astype(f32)
+    if swaps:
+        every[0] = low[...].astype(f32)
+    first = 1 if swaps else 0
+    for k in range(first, ta_count):
+        every[k] = far[(k - first) * frames : (k + 1 - first) * frames, :].astype(f32)
     me = lax.axis_index("ta")
     chunk = 8
     rank = full_z.shape[1]
@@ -208,7 +260,7 @@
         at = pl.multiple_of(table[2 * slots + s] * edge, edge)
         panel_y = full_y[pl.ds(at, edge), :]
         u = table[s]
-        k = lax.rem(me + (ta_count - jnp.maximum(u, 0)), ta_count)
+        k = distance(u, me, swaps)
         total = jnp.zeros((8, edge), f32)
         for f in range(0, frames, chunk):
             rows = every[k, f : f + chunk, :]
@@ -221,59 +273,21 @@
     out[...] = answer
 
 
-def around(x, axis, count):
-    if count <= ring_limit:
-        turns = [
-            lax.ppermute(x, axis, [(i, (i + k) % count) for i in range(count)])
-            for k in range(1, count)
-        ]
-        return jnp.concatenate(turns, axis=0)
-    every = lax.all_gather(x, axis, axis=0)
-    order = (lax.axis_index(axis) - jnp.arange(1, count)) % count
-    return every[order].reshape((count - 1) * x.shape[0], x.shape[1])
-
-
-def deliver(terms, axis, count):
-    frames = terms.shape[0] // count
-    if count <= ring_limit:
-        turns = [
-            lax.ppermute(
-                terms[k * frames : (k + 1) * frames],
-                axis,
-                [(i, (i + k) % count) for i in range(count)],
-            )
-            for k in range(1, count)
-        ]
-        return jnp.concatenate(turns, axis=0)
-    me = lax.axis_index(axis)
-    split = terms.reshape(count, frames, terms.shape[1])
-    arrived = lax.all_to_all(
-        split[(jnp.arange(count) - me) % count], axis, split_axis=0, concat_axis=0
-    )
-    order = (me - jnp.arange(1, count)) % count
-    return arrived[order].reshape((count - 1) * frames, terms.shape[1])
+def swap(x, axis, count, k):
+    return lax.ppermute(x, axis, [(i, i ^ k) for i in range(count)])
 
 
 def body(blocks, qz_factor, qy_factor, block_owner, block_cells):
     ta_count, pb_count = lax.axis_size("ta"), lax.axis_size("pb")
     slots, frames, edge = blocks.shape[2], blocks.shape[3], blocks.shape[4]
     rows, rank = qz_factor.shape
-    half = rows // 2
-    piece = 2 * half + info_rows
+    half, quarter = rows // 2, rows // 4
+    swaps = (
+        ta_count in (4, swap_limit) and pb_count % 4 == 0 and rows % 64 == 0
+    )
     shape = jax.ShapeDtypeStruct
-    packed, rest, table = pl.pallas_call(
-        pack_kernel,
-        out_shape=[
-            shape((piece, rank), bf16),
-            shape((2 * half, rank), bf16),
-            shape((3 * slots,), jnp.int32),
-        ],
-        in_specs=[smem_spec] * 2 + [hbm_spec] * 2,
-        out_specs=[vmem_spec] * 2 + [smem_spec],
-        scratch_shapes=[pltpu.SemaphoreType.DMA((4,))],
-        compiler_params=params(4),
-        name="pack",
-    )(*(held(x) for x in (block_owner, jnp.swapaxes(block_cells, 2, 3), qz_factor, qy_factor)))
+    cells = jnp.swapaxes(block_cells, 2, 3)
+    full = [shape((ta_count * rows, rank), bf16)] * 2
     cube = pl.pallas_call(
         load_kernel,
         out_shape=shape((slots, frames, edge, edge), bf16),
@@ -286,22 +300,64 @@
         ),
         name="load",
     )(held(blocks))
-    far, cube = lax.optimization_barrier((around(packed, "ta", ta_count), cube))
-    pair = lax.ppermute(far, "pb", [(i, i ^ 1) for i in range(pb_count)])
-    terms, full_z, full_y, info = pl.pallas_call(
-        functools.partial(term_kernel, ta_count, edge),
-        out_shape=[
-            shape((ta_count * frames, rank), f32),
-            shape((ta_count * rows, rank), bf16),
-            shape((ta_count * rows, rank), bf16),
-            shape((ta_count * info_rows, rank), bf16),
-        ],
-        in_specs=[smem_spec] + [vmem_spec] * 5,
-        out_specs=[vmem_spec] * 4,
+    if swaps:
+        near, part, rest, table = pl.pallas_call(
+            pack_kernel,
+            out_shape=[
+                shape((2 * half + info_rows, rank), bf16),
+                shape((2 * quarter + info_rows, rank), bf16),
+                shape((2 * half, rank), bf16),
+                shape((3 * slots,), jnp.int32),
+            ],
+            in_specs=[hbm_spec] * 4,
+            out_specs=[vmem_spec] * 3 + [smem_spec],
+            scratch_shapes=[
+                pltpu.SMEM(block_owner.shape, jnp.int32),
+                pltpu.SMEM(cells.shape, jnp.int32),
+                pltpu.SemaphoreType.DMA((8,)),
+            ],
+            compiler_params=params(4),
+            name="pack",
+        )(*(held(x) for x in (block_owner, cells, qz_factor, qy_factor)))
+        first = swap(near, "ta", ta_count, 1)
+        away = jnp.concatenate([swap(part, "ta", ta_count, k) for k in range(2, ta_count)], axis=0)
+        away, cube = lax.optimization_barrier((away, cube))
+        side_away = swap(away, "pb", pb_count, 2)
+        mate = swap(jnp.concatenate([first, away, side_away], axis=0), "pb", pb_count, 1)
+        pieces = (near, part, rest, first, away, side_away, mate)
+        made = full + [shape((ta_count * info_rows, rank), bf16)]
+    else:
+        table = jnp.concatenate([block_owner.reshape(slots), cells.reshape(2 * slots)])
+        pieces = (
+            lax.all_gather(qz_factor, "ta", axis=0, tiled=True),
+            lax.all_gather(qy_factor, "ta", axis=0, tiled=True),
+        )
+        made = []
+        shown = jnp.zeros((info_rows, rank), jnp.int32)
+        shown = shown.at[0, :slots].set(table[:slots] + 1)
+        shown = shown.at[1:3, :slots].set(table[slots:].reshape(2, slots))
+        info = lax.all_gather(shown.astype(bf16), "ta", axis=0, tiled=True)
+    out = pl.pallas_call(
+        functools.partial(term_kernel, ta_count, edge, swaps),
+        out_shape=[shape((ta_count * frames, rank), f32)] + made,
+        in_specs=[smem_spec] + [vmem_spec] * (1 + len(pieces)),
+        out_specs=[vmem_spec] * (1 + len(made)),
         compiler_params=params(16),
         name="terms",
-    )(table, packed, rest, far, pair, cube)
-    arrived = deliver(terms, "ta", ta_count)
+    )(table, cube, *pieces)
+    terms = out[0]
+    if swaps:
+        full_z, full_y, info = out[1:]
+        arrived = jnp.concatenate(
+            [
+                swap(terms[k * frames : (k + 1) * frames], "ta", ta_count, k)
+                for k in range(1, ta_count)
+            ],
+            axis=0,
+        )
+    else:
+        full_z, full_y = pieces
+        arrived = lax.all_to_all(terms, "ta", split_axis=0, concat_axis=0, tiled=True)
     system, inverse = pl.pallas_call(
         functools.partial(system_kernel, ta_count, slots, edge),
         out_shape=[shape((rank, rank), f32)] * 2,
@@ -312,16 +368,19 @@
         name="system",
     )(info, full_z, full_y)
     new_rows, low = pl.pallas_call(
-        functools.partial(solve_kernel, ta_count),
+        functools.partial(solve_kernel, ta_count, swaps),
         out_shape=[shape((frames, rank), f32), shape((frames, rank), bf16)],
         in_specs=[vmem_spec] * 4,
         out_specs=[vmem_spec] * 2,
         compiler_params=params(8),
         name="solve",
     )(terms, arrived, system, inverse)
-    others = around(low, "ta", ta_count)
+    if swaps:
+        others = jnp.concatenate([swap(low, "ta", ta_count, k) for k in range(1, ta_count)], axis=0)
+    else:
+        others = lax.all_gather(low, "ta", axis=0, tiled=True)
     misfit = pl.pallas_call(
-        functools.partial(misfit_kernel, ta_count, edge),
+        functools.partial(misfit_kernel, ta_count, edge, swaps),
         out_shape=shape((1, slots), f32),
         in_specs=[smem_spec] + [vmem_spec] * 5,
         out_specs=vmem_spec,

time: 46 us -> 44.9 us (0.976)
  Pallas kernels: 15.7 us -> 14.9 us
    pallas_call x4, Pallas kernels: 10.2 us -> 9.6 us  [the longest x1 3.56 us: body(): pl.pallas_call(functools.partial(misfit_kernel, ta_count, edge, swaps), o...]
    ppermute x10 -> x11, starting transfers between devices: 15 us -> 14.7 us  [swap(): return lax.ppermute(x, axis, [(i, i ^ k) for i in range(count)])]
    ppermute x10 -> x11, waiting for transfers between devices: 14.4 us -> 14.3 us  [swap(): return lax.ppermute(x, axis, [(i, i ^ k) for i in range(count)])]
  transfers between devices with their start and end apart: 10 -> 11, of which waited for: 6 -> 7; matrix products, arithmetic and copies ran while one was open for 0% -> 0% of each run, Pallas kernels for 12% -> 12%
where the time goes in v3:
time: 44.9 us; the launch traced here: 44.6 us
  Pallas kernels  14.9 us (33%)
  starting transfers between devices  14.7 us (33%)
  waiting for transfers between devices  14.3 us (32%)
  between operations  0.72 us (2%)
    ppermute x11, starting transfers between devices, swap(): return lax.ppermute(x, axis, [(i, i ^ k) for i in range(count)])  14.7 us
    ppermute x11, waiting for transfers between devices, swap(): return lax.ppermute(x, axis, [(i, i ^ k) for i in range(count)])  14.3 us
    pallas_call x1, Pallas kernels, body(): pl.pallas_call(functools.partial(misfit_kernel, ta_count, edge, swaps), o...  3.56 us
    pallas_call x1, Pallas kernels, body(): pl.pallas_call(functools.partial(system_kernel, ta_count, slots, edge), o...  3.06 us
    pallas_call x1, Pallas kernels, body(): pl.pallas_call(functools.partial(term_kernel, ta_count, edge, swaps), out...  2.95 us
    pallas_call x1, Pallas kernels, body(): pl.pallas_call(load_kernel, out_shape=shape((slots, frames, edge, edge),...  2.21 us
    pallas_call x1, Pallas kernels, body(): pl.pallas_call(pack_kernel, out_shape=[shape((2 * half + info_rows, rank)...  1.64 us
    pallas_call x1, Pallas kernels, body(): pl.pallas_call(functools.partial(solve_kernel, ta_count, swaps), out_shap...  1.44 us
  transfers between devices with their start and end apart: 11, of which 7 were waited for; matrix products, arithmetic and copies ran while one was open for 0% of the time, Pallas kernels for 12%

profile of v3, /device:TPU:0, one launch (start us, length us, event | category | flops | bytes accessed | tf_op | source)
XLA Modules:
  0.0 44.6 jit_solution(13083351597954414542)
XLA Ops:
  0.6 1.6 %pack.1 = (bf16[272,256]{1,0:T(8,128)(2,1)S(1)}, bf16[144,256]{1,0:T(8,128)(2,1)S(1)}, bf16[256,256]{1,0:T(8,128)(2,1)S(1)}, s32[12]{0:T(128)S(1)}) custom-call(s32[1,1,4]{2,1,0:T(1,128)} %owner_hbm.1, s32[1,1,2,4]{3,2,1,0:T(2,128)} %bitcast.2, bf16[256,256]{1,0:T(8,128)(2,1)} %z_hbm.1, bf16[256,256]{1,0:T(8,128)(2,1)} %y_hbm.1), custom_call_target="tpu_custom_call" | custom-call | tf_op jit(solution)/shard_map/pack/pallas_call | solution.py:304
  2.3 5.1 %collective-permute-start.1 = (bf16[144,256]{1,0:T(8,128)(2,1)S(1)}, bf16[144,256]{1,0:T(8,128)(2,1)S(1)}, u32[]{:S(2)}, u32[]{:S(2)}) collective-permute-start(bf16[144,256]{1,0:T(8,128)(2,1)S(1)} %get-tuple-element.17.refs_1_), channel_id=1, source_target_pairs={{0,12},{4,8},{8,4},{12,0},{1,13},{5,9},{9,5},{13,1},{2,14},{6,10},... | collective-permute-start | bytes 221192 | tf_op jit(solution)/shard_map/ppermute | solution.py:277
  7.4 0.0 collective-permute-start
  7.4 2.2 %load.1.cube = bf16[4,32,128,128]{3,2,1,0:T(8,128)(2,1)S(1)} custom-call(bf16[1,1,4,32,128,128]{5,4,3,2,1,0:T(8,128)(2,1)} %blocks.1), custom_call_target="tpu_custom_call" | custom-call | bytes 8388608 | tf_op jit(solution)/shard_map/load/pallas_call | solution.py:291
  9.6 0.4 %collective-permute-done.1 = bf16[144,256]{1,0:T(8,128)(2,1)S(1)} collective-permute-done((bf16[144,256]{1,0:T(8,128)(2,1)S(1)}, bf16[144,256]{1,0:T(8,128)(2,1)S(1)}, u32[]{:S(2)}, u32[]{:S(2)}) %collective-permute-start.1) | collective-permute-done | bytes 73760 | tf_op jit(solution)/shard_map/ppermute | solution.py:277
  10.1 3.6 %collective-permute-done = bf16[144,256]{1,0:T(8,128)(2,1)S(1)} collective-permute-done((bf16[144,256]{1,0:T(8,128)(2,1)S(1)}, bf16[144,256]{1,0:T(8,128)(2,1)S(1)}, u32[]{:S(2)}, u32[]{:S(2)}) %collective-permute-start) | collective-permute-done | bytes 73760 | tf_op jit(solution)/shard_map/ppermute | solution.py:277
  13.7 1.6 %collective-permute-start.3 = (bf16[288,256]{1,0:T(8,128)(2,1)S(1)}, bf16[288,256]{1,0:T(8,128)(2,1)S(1)}, u32[]{:S(2)}, u32[]{:S(2)}) collective-permute-start(bf16[288,256]{1,0:T(8,128)(2,1)S(1)} %pad_maximum_fusion.1.refs_4_), channel_id=1, source_target_pairs={{0,2},{1,3},{2,0},{3,1},{4,6},{5,7},{6,4},{7,5},{8,10},{9,11},{10,... | collective-permute-start | bytes 442376 | tf_op jit(solution)/shard_map/ppermute | solution.py:277
  15.2 0.0 collective-permute-start.2
  15.2 5.1 %collective-permute-done.2.refs_3_ = bf16[272,256]{1,0:T(8,128)(2,1)S(1)} collective-permute-done((bf16[272,256]{1,0:T(8,128)(2,1)S(1)}, bf16[272,256]{1,0:T(8,128)(2,1)S(1)}, u32[]{:S(2)}, u32[]{:S(2)}) %collective-permute-start.2) | collective-permute-done | bytes 139296 | tf_op jit(solution)/shard_map/ppermute | solution.py:277
  20.3 0.0 collective-permute-done.3.refs_5_
  20.3 0.1 collective-permute-start.4
  20.4 1.8 %collective-permute-done.4.refs_6_ = bf16[848,256]{1,0:T(8,128)(2,1)S(1)} collective-permute-done((bf16[848,256]{1,0:T(8,128)(2,1)S(1)}, bf16[848,256]{1,0:T(8,128)(2,1)S(1)}, u32[]{:S(2)}, u32[]{:S(2)}) %collective-permute-start.4) | collective-permute-done | bytes 434208 | tf_op jit(solution)/shard_map/ppermute | solution.py:277
  22.2 2.9 %terms.1 = (f32[128,256]{1,0:T(8,128)S(1)}, bf16[1024,256]{1,0:T(8,128)(2,1)S(1)}, bf16[1024,256]{1,0:T(8,128)(2,1)S(1)}, bf16[64,256]{1,0:T(8,128)(2,1)S(1)}) custom-call(s32[12]{0:T(128)S(1)} %get-tuple-element.16.table, bf16[4,32,128,128]{3,2,1,0:T(8,128)(2,1)S(1)} %load.1.cube, bf16[272,256]{1,0:T(8,128)(2,1)S(1)} %get-tuple-element.19.refs_0_, ...), custom_call_target="tpu_custom_call" | custom-call | tf_op jit(solution)/shard_map/terms/pallas_call | solution.py:340
  25.1 0.2 collective-permute-start.5
  25.3 2.7 %collective-permute-start.7 = (f32[32,256]{1,0:T(8,128)S(1)}, f32[32,256]{1,0:T(8,128)S(1)}, u32[]{:S(2)}, u32[]{:S(2)}) collective-permute-start(f32[32,256]{1,0:T(8,128)S(1)} %get-tuple-element.31), channel_id=1, source_target_pairs={{0,12},{4,8},{8,4},{12,0},{1,13},{5,9},{9,5},{13,1},{2,14},{6,10},... | collective-permute-start | bytes 98312 | tf_op jit(solution)/shard_map/ppermute | solution.py:277
  28.0 0.7 %collective-permute-start.6 = (f32[32,256]{1,0:T(8,128)S(1)}, f32[32,256]{1,0:T(8,128)S(1)}, u32[]{:S(2)}, u32[]{:S(2)}) collective-permute-start(f32[32,256]{1,0:T(8,128)S(1)} %get-tuple-element.32), channel_id=1, source_target_pairs={{0,8},{4,12},{8,0},{12,4},{1,9},{5,13},{9,1},{13,5},{2,10},{6,14},... | collective-permute-start | bytes 98312 | tf_op jit(solution)/shard_map/ppermute | solution.py:277
  28.7 3.1 %system.1 = (f32[256,256]{1,0:T(8,128)S(1)}, f32[256,256]{1,0:T(8,128)S(1)}) custom-call(bf16[64,256]{1,0:T(8,128)(2,1)S(1)} %get-tuple-element.23.info, bf16[1024,256]{1,0:T(8,128)(2,1)S(1)} %get-tuple-element.24.full_z, bf16[1024,256]{1,0:T(8,128)(2,1)S(1)} %get-tuple-element.25.full_y), custom_call_target="tpu_custom_call" | custom-call | tf_op jit(solution)/shard_map/system/pallas_call | solution.py:361
  31.8 0.0 collective-permute-done.5
  31.8 0.0 collective-permute-done.7
  31.8 1.0 %collective-permute-done.6 = f32[32,256]{1,0:T(8,128)S(1)} collective-permute-done((f32[32,256]{1,0:T(8,128)S(1)}, f32[32,256]{1,0:T(8,128)S(1)}, u32[]{:S(2)}, u32[]{:S(2)}) %collective-permute-start.6) | collective-permute-done | bytes 32800 | tf_op jit(solution)/shard_map/ppermute | solution.py:277
  32.8 1.4 %solve.1 = (f32[32,256]{1,0:T(8,128)}, bf16[32,256]{1,0:T(8,128)(2,1)S(1)}) custom-call(f32[128,256]{1,0:T(8,128)S(1)} %get-tuple-element.22.own, f32[96,256]{1,0:T(8,128)S(1)} %pad_maximum_fusion.2.far, f32[256,256]{1,0:T(8,128)S(1)} %get-tuple-element.26.system, f32[256,256]{1,0:T(8,128)S(1)} %get-tuple-element.27.inverse), custom_call_target="tpu_custom_call" | custom-call | tf_op jit(solution)/shard_map/solve/pallas_call | solution.py:370
  34.3 2.1 %collective-permute-start.10 = (bf16[32,256]{1,0:T(8,128)(2,1)S(1)}, bf16[32,256]{1,0:T(8,128)(2,1)S(1)}, u32[]{:S(2)}, u32[]{:S(2)}) collective-permute-start(bf16[32,256]{1,0:T(8,128)(2,1)S(1)} %get-tuple-element.29.low), channel_id=1, source_target_pairs={{0,12},{4,8},{8,4},{12,0},{1,13},{5,9},{9,5},{13,1},{2,14},{6,10},... | collective-permute-start | bytes 49160 | tf_op jit(solution)/shard_map/ppermute | solution.py:277
  36.4 0.4 collective-permute-start.9
  36.8 1.9 %collective-permute-start.8 = (bf16[32,256]{1,0:T(8,128)(2,1)S(1)}, bf16[32,256]{1,0:T(8,128)(2,1)S(1)}, u32[]{:S(2)}, u32[]{:S(2)}) collective-permute-start(bf16[32,256]{1,0:T(8,128)(2,1)S(1)} %get-tuple-element.29.low), channel_id=1, source_target_pairs={{0,4},{4,0},{8,12},{12,8},{1,5},{5,1},{9,13},{13,9},{2,6},{6,2},{1... | collective-permute-start | bytes 49160 | tf_op jit(solution)/shard_map/ppermute | solution.py:277
  38.6 1.1 %collective-permute-done.10 = bf16[32,256]{1,0:T(8,128)(2,1)S(1)} collective-permute-done((bf16[32,256]{1,0:T(8,128)(2,1)S(1)}, bf16[32,256]{1,0:T(8,128)(2,1)S(1)}, u32[]{:S(2)}, u32[]{:S(2)}) %collective-permute-start.10) | collective-permute-done | bytes 16416 | tf_op jit(solution)/shard_map/ppermute | solution.py:277
  39.8 1.2 %collective-permute-done.9 = bf16[32,256]{1,0:T(8,128)(2,1)S(1)} collective-permute-done((bf16[32,256]{1,0:T(8,128)(2,1)S(1)}, bf16[32,256]{1,0:T(8,128)(2,1)S(1)}, u32[]{:S(2)}, u32[]{:S(2)}) %collective-permute-start.9) | collective-permute-done | bytes 16416 | tf_op jit(solution)/shard_map/ppermute | solution.py:277
  41.0 0.0 collective-permute-done.8
  41.0 3.6 %misfit.1 = f32[1,4]{1,0:T(1,128)} custom-call(s32[12]{0:T(128)S(1)} %get-tuple-element.16.table, bf16[32,256]{1,0:T(8,128)(2,1)S(1)} %get-tuple-element.29.low, bf16[96,256]{1,0:T(8,128)(2,1)S(1)} %pad_maximum_fusion.3.far, bf16[1024,256]{1,0:T(8,128)(2,1)S(1)} %get-tuple-element.24.full_z, bf16[1024,256]{1,0:T(8,128)(2,1)S(1)} %get-tuple-element.25.full_y, ...), custom_call_target="tpu_custom_call" | custom-call | tf_op jit(solution)/shard_map/misfit/pallas_call | solution.py:382
  (5 shorter events, 0.1 us)
Async XLA Ops:
  2.3 7.8 %collective-permute-start.1 = (bf16[144,256]{1,0:T(8,128)(2,1)S(1)}, bf16[144,256]{1,0:T(8,128)(2,1)S(1)}, u32[]{:S(2)}, u32[]{:S(2)}) collective-permute-start(bf16[144,256]{1,0:T(8,128)(2,1)S(1)} %get-tuple-element.17.refs_1_), channel_id=1, source_target_pairs={{0,12},{4,8},{8,4},{12,0},{1,13},{5,9},{9,5},{13,1},{2,14},{6,10},... | collective-permute-start | bytes 221192 | tf_op jit(solution)/shard_map/ppermute | solution.py:277
  7.4 6.2 %collective-permute-start = (bf16[144,256]{1,0:T(8,128)(2,1)S(1)}, bf16[144,256]{1,0:T(8,128)(2,1)S(1)}, u32[]{:S(2)}, u32[]{:S(2)}) collective-permute-start(bf16[144,256]{1,0:T(8,128)(2,1)S(1)} %get-tuple-element.17.refs_1_), channel_id=1, source_target_pairs={{0,8},{4,12},{8,0},{12,4},{1,9},{5,13},{9,1},{13,5},{2,10},{6,14},... | collective-permute-start | bytes 221192 | tf_op jit(solution)/shard_map/ppermute | solution.py:277
  13.7 6.6 %collective-permute-start.3 = (bf16[288,256]{1,0:T(8,128)(2,1)S(1)}, bf16[288,256]{1,0:T(8,128)(2,1)S(1)}, u32[]{:S(2)}, u32[]{:S(2)}) collective-permute-start(bf16[288,256]{1,0:T(8,128)(2,1)S(1)} %pad_maximum_fusion.1.refs_4_), channel_id=1, source_target_pairs={{0,2},{1,3},{2,0},{3,1},{4,6},{5,7},{6,4},{7,5},{8,10},{9,11},{10,... | collective-permute-start | bytes 442376 | tf_op jit(solution)/shard_map/ppermute | solution.py:277
  15.2 5.1 %collective-permute-start.2 = (bf16[272,256]{1,0:T(8,128)(2,1)S(1)}, bf16[272,256]{1,0:T(8,128)(2,1)S(1)}, u32[]{:S(2)}, u32[]{:S(2)}) collective-permute-start(bf16[272,256]{1,0:T(8,128)(2,1)S(1)} %get-tuple-element.19.refs_0_), channel_id=1, source_target_pairs={{0,4},{4,0},{8,12},{12,8},{1,5},{5,1},{9,13},{13,9},{2,6},{6,2},{1... | collective-permute-start | bytes 417800 | tf_op jit(solution)/shard_map/ppermute | solution.py:277
  20.3 1.8 %collective-permute-start.4 = (bf16[848,256]{1,0:T(8,128)(2,1)S(1)}, bf16[848,256]{1,0:T(8,128)(2,1)S(1)}, u32[]{:S(2)}, u32[]{:S(2)}) collective-permute-start(bf16[848,256]{1,0:T(8,128)(2,1)S(1)} %pad_maximum_fusion), channel_id=1, source_target_pairs={{0,1},{1,0},{2,3},{3,2},{4,5},{5,4},{6,7},{7,6},{8,9},{9,8},{10,11... | collective-permute-start | bytes 1302536 | tf_op jit(solution)/shard_map/ppermute | solution.py:277
  25.1 6.6 %collective-permute-start.5 = (f32[32,256]{1,0:T(8,128)S(1)}, f32[32,256]{1,0:T(8,128)S(1)}, u32[]{:S(2)}, u32[]{:S(2)}) collective-permute-start(f32[32,256]{1,0:T(8,128)S(1)} %get-tuple-element.30), channel_id=1, source_target_pairs={{0,4},{4,0},{8,12},{12,8},{1,5},{5,1},{9,13},{13,9},{2,6},{6,2},{1... | collective-permute-start | bytes 98312 | tf_op jit(solution)/shard_map/ppermute | solution.py:277
  25.3 6.4 %collective-permute-start.7 = (f32[32,256]{1,0:T(8,128)S(1)}, f32[32,256]{1,0:T(8,128)S(1)}, u32[]{:S(2)}, u32[]{:S(2)}) collective-permute-start(f32[32,256]{1,0:T(8,128)S(1)} %get-tuple-element.31), channel_id=1, source_target_pairs={{0,12},{4,8},{8,4},{12,0},{1,13},{5,9},{9,5},{13,1},{2,14},{6,10},... | collective-permute-start | bytes 98312 | tf_op jit(solution)/shard_map/ppermute | solution.py:277
  28.0 4.8 %collective-permute-start.6 = (f32[32,256]{1,0:T(8,128)S(1)}, f32[32,256]{1,0:T(8,128)S(1)}, u32[]{:S(2)}, u32[]{:S(2)}) collective-permute-start(f32[32,256]{1,0:T(8,128)S(1)} %get-tuple-element.32), channel_id=1, source_target_pairs={{0,8},{4,12},{8,0},{12,4},{1,9},{5,13},{9,1},{13,5},{2,10},{6,14},... | collective-permute-start | bytes 98312 | tf_op jit(solution)/shard_map/ppermute | solution.py:277
  34.3 5.5 %collective-permute-start.10 = (bf16[32,256]{1,0:T(8,128)(2,1)S(1)}, bf16[32,256]{1,0:T(8,128)(2,1)S(1)}, u32[]{:S(2)}, u32[]{:S(2)}) collective-permute-start(bf16[32,256]{1,0:T(8,128)(2,1)S(1)} %get-tuple-element.29.low), channel_id=1, source_target_pairs={{0,12},{4,8},{8,4},{12,0},{1,13},{5,9},{9,5},{13,1},{2,14},{6,10},... | collective-permute-start | bytes 49160 | tf_op jit(solution)/shard_map/ppermute | solution.py:277
  36.4 4.7 %collective-permute-start.9 = (bf16[32,256]{1,0:T(8,128)(2,1)S(1)}, bf16[32,256]{1,0:T(8,128)(2,1)S(1)}, u32[]{:S(2)}, u32[]{:S(2)}) collective-permute-start(bf16[32,256]{1,0:T(8,128)(2,1)S(1)} %get-tuple-element.29.low), channel_id=1, source_target_pairs={{0,8},{4,12},{8,0},{12,4},{1,9},{5,13},{9,1},{13,5},{2,10},{6,14},... | collective-permute-start | bytes 49160 | tf_op jit(solution)/shard_map/ppermute | solution.py:277
  36.8 4.3 %collective-permute-start.8 = (bf16[32,256]{1,0:T(8,128)(2,1)S(1)}, bf16[32,256]{1,0:T(8,128)(2,1)S(1)}, u32[]{:S(2)}, u32[]{:S(2)}) collective-permute-start(bf16[32,256]{1,0:T(8,128)(2,1)S(1)} %get-tuple-element.29.low), channel_id=1, source_target_pairs={{0,4},{4,0},{8,12},{12,8},{1,5},{5,1},{9,13},{13,9},{2,6},{6,2},{1... | collective-permute-start | bytes 49160 | tf_op jit(solution)/shard_map/ppermute | solution.py:277

commit v4 on v3

--- a/solution.py
+++ b/solution.py
@@ -288,7 +288,7 @@
     shape = jax.ShapeDtypeStruct
     cells = jnp.swapaxes(block_cells, 2, 3)
     full = [shape((ta_count * rows, rank), bf16)] * 2
-    cube = pl.pallas_call(
+    load = pl.pallas_call(
         load_kernel,
         out_shape=shape((slots, frames, edge, edge), bf16),
         in_specs=[hbm_spec],
@@ -299,7 +299,7 @@
             flops=0, transcendentals=0, bytes_accessed=4 * slots * frames * edge * edge
         ),
         name="load",
-    )(held(blocks))
+    )
     if swaps:
         near, part, rest, table = pl.pallas_call(
             pack_kernel,
@@ -321,12 +321,15 @@
         )(*(held(x) for x in (block_owner, cells, qz_factor, qy_factor)))
         first = swap(near, "ta", ta_count, 1)
         away = jnp.concatenate([swap(part, "ta", ta_count, k) for k in range(2, ta_count)], axis=0)
-        away, cube = lax.optimization_barrier((away, cube))
-        side_away = swap(away, "pb", pb_count, 2)
+        first, away, blocks = lax.optimization_barrier((first, away, blocks))
+        side_away, cube = lax.optimization_barrier(
+            (swap(away, "pb", pb_count, 2), load(held(blocks)))
+        )
         mate = swap(jnp.concatenate([first, away, side_away], axis=0), "pb", pb_count, 1)
         pieces = (near, part, rest, first, away, side_away, mate)
         made = full + [shape((ta_count * info_rows, rank), bf16)]
     else:
+        cube = load(held(blocks))
         table = jnp.concatenate([block_owner.reshape(slots), cells.reshape(2 * slots)])
         pieces = (
             lax.all_gather(qz_factor, "ta", axis=0, tiled=True),

time: 44.9 us -> 44.7 us (level)
  waiting for transfers between devices: 14.3 us -> 12.7 us
  starting transfers between devices: 14.7 us -> 15.7 us
  Pallas kernels: 14.9 us -> 15.4 us
    ppermute x11, waiting for transfers between devices: 14.3 us -> 12.7 us  [swap(): return lax.ppermute(x, axis, [(i, i ^ k) for i in range(count)])]
    ppermute x11, starting transfers between devices: 14.7 us -> 15.7 us  [swap(): return lax.ppermute(x, axis, [(i, i ^ k) for i in range(count)])]
    pallas_call x1, Pallas kernels: 3.06 us -> 3.56 us  [body(): pl.pallas_call(functools.partial(system_kernel, ta_count, slots, edge), o...]
  transfers between devices with their start and end apart: 11 -> 11, of which waited for: 7 -> 10; matrix products, arithmetic and copies ran while one was open for 0% -> 0% of each run, Pallas kernels for 12% -> 13%
where the time goes in v4:
time: 44.7 us; the launch traced here: 44.6 us
  starting transfers between devices  15.7 us (35%)
  Pallas kernels  15.4 us (34%)
  waiting for transfers between devices  12.7 us (28%)
  between operations  0.71 us (2%)
    ppermute x11, starting transfers between devices, swap(): return lax.ppermute(x, axis, [(i, i ^ k) for i in range(count)])  15.7 us
    ppermute x11, waiting for transfers between devices, swap(): return lax.ppermute(x, axis, [(i, i ^ k) for i in range(count)])  12.7 us
    pallas_call x1, Pallas kernels, body(): pl.pallas_call(functools.partial(misfit_kernel, ta_count, edge, swaps), o...  3.57 us
    pallas_call x1, Pallas kernels, body(): pl.pallas_call(functools.partial(system_kernel, ta_count, slots, edge), o...  3.56 us
    pallas_call x1, Pallas kernels, body(): pl.pallas_call(functools.partial(term_kernel, ta_count, edge, swaps), out...  2.95 us
    pallas_call x1, Pallas kernels, body(): load(held(blocks))  2.2 us
    pallas_call x1, Pallas kernels, body(): pl.pallas_call(pack_kernel, out_shape=[shape((2 * half + info_rows, rank)...  1.64 us
    pallas_call x1, Pallas kernels, body(): pl.pallas_call(functools.partial(solve_kernel, ta_count, swaps), out_shap...  1.44 us
  transfers between devices with their start and end apart: 11, of which 10 were waited for; matrix products, arithmetic and copies ran while one was open for 0% of the time, Pallas kernels for 13%

profile of v4, /device:TPU:0, one launch (start us, length us, event | category | flops | bytes accessed | tf_op | source)
XLA Modules:
  0.0 44.6 jit_solution(13168511776919483330)
XLA Ops:
  0.6 1.6 %pack.1 = (bf16[272,256]{1,0:T(8,128)(2,1)S(1)}, bf16[144,256]{1,0:T(8,128)(2,1)S(1)}, bf16[256,256]{1,0:T(8,128)(2,1)S(1)}, s32[12]{0:T(128)S(1)}) custom-call(s32[1,1,4]{2,1,0:T(1,128)} %owner_hbm.1, s32[1,1,2,4]{3,2,1,0:T(2,128)} %bitcast.2, bf16[256,256]{1,0:T(8,128)(2,1)} %z_hbm.1, bf16[256,256]{1,0:T(8,128)(2,1)} %y_hbm.1), custom_call_target="tpu_custom_call" | custom-call | tf_op jit(solution)/shard_map/pack/pallas_call | solution.py:304
  2.3 5.1 %collective-permute-start.2 = (bf16[144,256]{1,0:T(8,128)(2,1)S(1)}, bf16[144,256]{1,0:T(8,128)(2,1)S(1)}, u32[]{:S(2)}, u32[]{:S(2)}) collective-permute-start(bf16[144,256]{1,0:T(8,128)(2,1)S(1)} %get-tuple-element.21.refs_1_), channel_id=1, source_target_pairs={{0,12},{4,8},{8,4},{12,0},{1,13},{5,9},{9,5},{13,1},{2,14},{6,10},... | collective-permute-start | bytes 221192 | tf_op jit(solution)/shard_map/ppermute | solution.py:277
  7.4 0.0 collective-permute-start.1
  7.4 0.6 %collective-permute-start = (bf16[272,256]{1,0:T(8,128)(2,1)S(1)}, bf16[272,256]{1,0:T(8,128)(2,1)S(1)}, u32[]{:S(2)}, u32[]{:S(2)}) collective-permute-start(bf16[272,256]{1,0:T(8,128)(2,1)S(1)} %get-tuple-element.20.refs_0_), channel_id=1, source_target_pairs={{0,4},{4,0},{8,12},{12,8},{1,5},{5,1},{9,13},{13,9},{2,6},{6,2},{1... | collective-permute-start | bytes 417800 | tf_op jit(solution)/shard_map/ppermute | solution.py:277
  8.1 2.0 %collective-permute-done.2 = bf16[144,256]{1,0:T(8,128)(2,1)S(1)} collective-permute-done((bf16[144,256]{1,0:T(8,128)(2,1)S(1)}, bf16[144,256]{1,0:T(8,128)(2,1)S(1)}, u32[]{:S(2)}, u32[]{:S(2)}) %collective-permute-start.2) | collective-permute-done | bytes 73760 | tf_op jit(solution)/shard_map/ppermute | solution.py:277
  10.1 3.7 %collective-permute-done.1 = bf16[144,256]{1,0:T(8,128)(2,1)S(1)} collective-permute-done((bf16[144,256]{1,0:T(8,128)(2,1)S(1)}, bf16[144,256]{1,0:T(8,128)(2,1)S(1)}, u32[]{:S(2)}, u32[]{:S(2)}) %collective-permute-start.1) | collective-permute-done | bytes 73760 | tf_op jit(solution)/shard_map/ppermute | solution.py:277
  13.8 0.6 %collective-permute-done.refs_3_ = bf16[272,256]{1,0:T(8,128)(2,1)S(1)} collective-permute-done((bf16[272,256]{1,0:T(8,128)(2,1)S(1)}, bf16[272,256]{1,0:T(8,128)(2,1)S(1)}, u32[]{:S(2)}, u32[]{:S(2)}) %collective-permute-start) | collective-permute-done | bytes 139296 | tf_op jit(solution)/shard_map/ppermute | solution.py:277
  14.4 1.7 %collective-permute-start.3 = (bf16[288,256]{1,0:T(8,128)(2,1)S(1)}, bf16[288,256]{1,0:T(8,128)(2,1)S(1)}, u32[]{:S(2)}, u32[]{:S(2)}) collective-permute-start(bf16[288,256]{1,0:T(8,128)(2,1)S(1)} %pad_maximum_fusion.1.refs_4_), channel_id=1, source_target_pairs={{0,2},{1,3},{2,0},{3,1},{4,6},{5,7},{6,4},{7,5},{8,10},{9,11},{10,... | collective-permute-start | bytes 442376 | tf_op jit(solution)/shard_map/ppermute | solution.py:277
  16.1 2.2 %load.1.cube = bf16[4,32,128,128]{3,2,1,0:T(8,128)(2,1)S(1)} custom-call(bf16[1,1,4,32,128,128]{5,4,3,2,1,0:T(8,128)(2,1)} %blocks), custom_call_target="tpu_custom_call" | custom-call | bytes 8388608 | tf_op jit(solution)/shard_map/load/pallas_call | solution.py:326
  18.3 1.2 %collective-permute-done.3.refs_5_ = bf16[288,256]{1,0:T(8,128)(2,1)S(1)} collective-permute-done((bf16[288,256]{1,0:T(8,128)(2,1)S(1)}, bf16[288,256]{1,0:T(8,128)(2,1)S(1)}, u32[]{:S(2)}, u32[]{:S(2)}) %collective-permute-start.3) | collective-permute-done | bytes 147488 | tf_op jit(solution)/shard_map/ppermute | solution.py:277
  19.6 0.1 collective-permute-start.4
  19.7 1.8 %collective-permute-done.4.refs_6_ = bf16[848,256]{1,0:T(8,128)(2,1)S(1)} collective-permute-done((bf16[848,256]{1,0:T(8,128)(2,1)S(1)}, bf16[848,256]{1,0:T(8,128)(2,1)S(1)}, u32[]{:S(2)}, u32[]{:S(2)}) %collective-permute-start.4) | collective-permute-done | bytes 434208 | tf_op jit(solution)/shard_map/ppermute | solution.py:277
  21.4 2.9 %terms.1 = (f32[128,256]{1,0:T(8,128)S(1)}, bf16[1024,256]{1,0:T(8,128)(2,1)S(1)}, bf16[1024,256]{1,0:T(8,128)(2,1)S(1)}, bf16[64,256]{1,0:T(8,128)(2,1)S(1)}) custom-call(s32[12]{0:T(128)S(1)} %get-tuple-element.19.table, bf16[4,32,128,128]{3,2,1,0:T(8,128)(2,1)S(1)} %load.1.cube, bf16[272,256]{1,0:T(8,128)(2,1)S(1)} %get-tuple-element.20.refs_0_, ...), custom_call_target="tpu_custom_call" | custom-call | tf_op jit(solution)/shard_map/terms/pallas_call | solution.py:343
  24.4 1.7 %collective-permute-start.5 = (f32[32,256]{1,0:T(8,128)S(1)}, f32[32,256]{1,0:T(8,128)S(1)}, u32[]{:S(2)}, u32[]{:S(2)}) collective-permute-start(f32[32,256]{1,0:T(8,128)S(1)} %get-tuple-element.36), channel_id=1, source_target_pairs={{0,4},{4,0},{8,12},{12,8},{1,5},{5,1},{9,13},{13,9},{2,6},{6,2},{1... | collective-permute-start | bytes 98312 | tf_op jit(solution)/shard_map/ppermute | solution.py:277
  26.1 1.6 %collective-permute-start.7 = (f32[32,256]{1,0:T(8,128)S(1)}, f32[32,256]{1,0:T(8,128)S(1)}, u32[]{:S(2)}, u32[]{:S(2)}) collective-permute-start(f32[32,256]{1,0:T(8,128)S(1)} %get-tuple-element.37), channel_id=1, source_target_pairs={{0,12},{4,8},{8,4},{12,0},{1,13},{5,9},{9,5},{13,1},{2,14},{6,10},... | collective-permute-start | bytes 98312 | tf_op jit(solution)/shard_map/ppermute | solution.py:277
  27.7 0.5 %collective-permute-start.6 = (f32[32,256]{1,0:T(8,128)S(1)}, f32[32,256]{1,0:T(8,128)S(1)}, u32[]{:S(2)}, u32[]{:S(2)}) collective-permute-start(f32[32,256]{1,0:T(8,128)S(1)} %get-tuple-element.38), channel_id=1, source_target_pairs={{0,8},{4,12},{8,0},{12,4},{1,9},{5,13},{9,1},{13,5},{2,10},{6,14},... | collective-permute-start | bytes 98312 | tf_op jit(solution)/shard_map/ppermute | solution.py:277
  28.2 3.6 %system.1 = (f32[256,256]{1,0:T(8,128)S(1)}, f32[256,256]{1,0:T(8,128)S(1)}) custom-call(bf16[64,256]{1,0:T(8,128)(2,1)S(1)} %get-tuple-element.29.info, bf16[1024,256]{1,0:T(8,128)(2,1)S(1)} %get-tuple-element.30.full_z, bf16[1024,256]{1,0:T(8,128)(2,1)S(1)} %get-tuple-element.31.full_y), custom_call_target="tpu_custom_call" | custom-call | tf_op jit(solution)/shard_map/system/pallas_call | solution.py:364
  31.8 0.0 collective-permute-done.5
  31.8 0.3 collective-permute-done.7
  32.1 0.5 %collective-permute-done.6 = f32[32,256]{1,0:T(8,128)S(1)} collective-permute-done((f32[32,256]{1,0:T(8,128)S(1)}, f32[32,256]{1,0:T(8,128)S(1)}, u32[]{:S(2)}, u32[]{:S(2)}) %collective-permute-start.6) | collective-permute-done | bytes 32800 | tf_op jit(solution)/shard_map/ppermute | solution.py:277
  32.5 1.4 %solve.1 = (f32[32,256]{1,0:T(8,128)}, bf16[32,256]{1,0:T(8,128)(2,1)S(1)}) custom-call(f32[128,256]{1,0:T(8,128)S(1)} %get-tuple-element.28.own, f32[96,256]{1,0:T(8,128)S(1)} %pad_maximum_fusion.2.far, f32[256,256]{1,0:T(8,128)S(1)} %get-tuple-element.32.system, f32[256,256]{1,0:T(8,128)S(1)} %get-tuple-element.33.inverse), custom_call_target="tpu_custom_call" | custom-call | tf_op jit(solution)/shard_map/solve/pallas_call | solution.py:373
  34.0 2.2 %collective-permute-start.10 = (bf16[32,256]{1,0:T(8,128)(2,1)S(1)}, bf16[32,256]{1,0:T(8,128)(2,1)S(1)}, u32[]{:S(2)}, u32[]{:S(2)}) collective-permute-start(bf16[32,256]{1,0:T(8,128)(2,1)S(1)} %get-tuple-element.35.low), channel_id=1, source_target_pairs={{0,12},{4,8},{8,4},{12,0},{1,13},{5,9},{9,5},{13,1},{2,14},{6,10},... | collective-permute-start | bytes 49160 | tf_op jit(solution)/shard_map/ppermute | solution.py:277
  36.2 1.1 %collective-permute-start.9 = (bf16[32,256]{1,0:T(8,128)(2,1)S(1)}, bf16[32,256]{1,0:T(8,128)(2,1)S(1)}, u32[]{:S(2)}, u32[]{:S(2)}) collective-permute-start(bf16[32,256]{1,0:T(8,128)(2,1)S(1)} %get-tuple-element.35.low), channel_id=1, source_target_pairs={{0,8},{4,12},{8,0},{12,4},{1,9},{5,13},{9,1},{13,5},{2,10},{6,14},... | collective-permute-start | bytes 49160 | tf_op jit(solution)/shard_map/ppermute | solution.py:277
  37.3 1.1 %collective-permute-start.8 = (bf16[32,256]{1,0:T(8,128)(2,1)S(1)}, bf16[32,256]{1,0:T(8,128)(2,1)S(1)}, u32[]{:S(2)}, u32[]{:S(2)}) collective-permute-start(bf16[32,256]{1,0:T(8,128)(2,1)S(1)} %get-tuple-element.35.low), channel_id=1, source_target_pairs={{0,4},{4,0},{8,12},{12,8},{1,5},{5,1},{9,13},{13,9},{2,6},{6,2},{1... | collective-permute-start | bytes 49160 | tf_op jit(solution)/shard_map/ppermute | solution.py:277
  38.4 1.1 %collective-permute-done.10 = bf16[32,256]{1,0:T(8,128)(2,1)S(1)} collective-permute-done((bf16[32,256]{1,0:T(8,128)(2,1)S(1)}, bf16[32,256]{1,0:T(8,128)(2,1)S(1)}, u32[]{:S(2)}, u32[]{:S(2)}) %collective-permute-start.10) | collective-permute-done | bytes 16416 | tf_op jit(solution)/shard_map/ppermute | solution.py:277
  39.5 1.3 %collective-permute-done.9 = bf16[32,256]{1,0:T(8,128)(2,1)S(1)} collective-permute-done((bf16[32,256]{1,0:T(8,128)(2,1)S(1)}, bf16[32,256]{1,0:T(8,128)(2,1)S(1)}, u32[]{:S(2)}, u32[]{:S(2)}) %collective-permute-start.9) | collective-permute-done | bytes 16416 | tf_op jit(solution)/shard_map/ppermute | solution.py:277
  40.8 0.2 collective-permute-done.8
  41.0 3.6 %misfit.1 = f32[1,4]{1,0:T(1,128)} custom-call(s32[12]{0:T(128)S(1)} %get-tuple-element.19.table, bf16[32,256]{1,0:T(8,128)(2,1)S(1)} %get-tuple-element.35.low, bf16[96,256]{1,0:T(8,128)(2,1)S(1)} %pad_maximum_fusion.3.far, bf16[1024,256]{1,0:T(8,128)(2,1)S(1)} %get-tuple-element.30.full_z, bf16[1024,256]{1,0:T(8,128)(2,1)S(1)} %get-tuple-element.31.full_y, ...), custom_call_target="tpu_custom_call" | custom-call | tf_op jit(solution)/shard_map/misfit/pallas_call | solution.py:385
  (5 shorter events, 0.1 us)
Async XLA Ops:
  2.3 7.8 %collective-permute-start.2 = (bf16[144,256]{1,0:T(8,128)(2,1)S(1)}, bf16[144,256]{1,0:T(8,128)(2,1)S(1)}, u32[]{:S(2)}, u32[]{:S(2)}) collective-permute-start(bf16[144,256]{1,0:T(8,128)(2,1)S(1)} %get-tuple-element.21.refs_1_), channel_id=1, source_target_pairs={{0,12},{4,8},{8,4},{12,0},{1,13},{5,9},{9,5},{13,1},{2,14},{6,10},... | collective-permute-start | bytes 221192 | tf_op jit(solution)/shard_map/ppermute | solution.py:277
  7.4 6.3 %collective-permute-start.1 = (bf16[144,256]{1,0:T(8,128)(2,1)S(1)}, bf16[144,256]{1,0:T(8,128)(2,1)S(1)}, u32[]{:S(2)}, u32[]{:S(2)}) collective-permute-start(bf16[144,256]{1,0:T(8,128)(2,1)S(1)} %get-tuple-element.21.refs_1_), channel_id=1, source_target_pairs={{0,8},{4,12},{8,0},{12,4},{1,9},{5,13},{9,1},{13,5},{2,10},{6,14},... | collective-permute-start | bytes 221192 | tf_op jit(solution)/shard_map/ppermute | solution.py:277
  7.4 7.0 %collective-permute-start = (bf16[272,256]{1,0:T(8,128)(2,1)S(1)}, bf16[272,256]{1,0:T(8,128)(2,1)S(1)}, u32[]{:S(2)}, u32[]{:S(2)}) collective-permute-start(bf16[272,256]{1,0:T(8,128)(2,1)S(1)} %get-tuple-element.20.refs_0_), channel_id=1, source_target_pairs={{0,4},{4,0},{8,12},{12,8},{1,5},{5,1},{9,13},{13,9},{2,6},{6,2},{1... | collective-permute-start | bytes 417800 | tf_op jit(solution)/shard_map/ppermute | solution.py:277
  14.4 5.1 %collective-permute-start.3 = (bf16[288,256]{1,0:T(8,128)(2,1)S(1)}, bf16[288,256]{1,0:T(8,128)(2,1)S(1)}, u32[]{:S(2)}, u32[]{:S(2)}) collective-permute-start(bf16[288,256]{1,0:T(8,128)(2,1)S(1)} %pad_maximum_fusion.1.refs_4_), channel_id=1, source_target_pairs={{0,2},{1,3},{2,0},{3,1},{4,6},{5,7},{6,4},{7,5},{8,10},{9,11},{10,... | collective-permute-start | bytes 442376 | tf_op jit(solution)/shard_map/ppermute | solution.py:277
  19.6 1.8 %collective-permute-start.4 = (bf16[848,256]{1,0:T(8,128)(2,1)S(1)}, bf16[848,256]{1,0:T(8,128)(2,1)S(1)}, u32[]{:S(2)}, u32[]{:S(2)}) collective-permute-start(bf16[848,256]{1,0:T(8,128)(2,1)S(1)} %pad_maximum_fusion), channel_id=1, source_target_pairs={{0,1},{1,0},{2,3},{3,2},{4,5},{5,4},{6,7},{7,6},{8,9},{9,8},{10,11... | collective-permute-start | bytes 1302536 | tf_op jit(solution)/shard_map/ppermute | solution.py:277
  24.4 7.4 %collective-permute-start.5 = (f32[32,256]{1,0:T(8,128)S(1)}, f32[32,256]{1,0:T(8,128)S(1)}, u32[]{:S(2)}, u32[]{:S(2)}) collective-permute-start(f32[32,256]{1,0:T(8,128)S(1)} %get-tuple-element.36), channel_id=1, source_target_pairs={{0,4},{4,0},{8,12},{12,8},{1,5},{5,1},{9,13},{13,9},{2,6},{6,2},{1... | collective-permute-start | bytes 98312 | tf_op jit(solution)/shard_map/ppermute | solution.py:277
  26.1 6.0 %collective-permute-start.7 = (f32[32,256]{1,0:T(8,128)S(1)}, f32[32,256]{1,0:T(8,128)S(1)}, u32[]{:S(2)}, u32[]{:S(2)}) collective-permute-start(f32[32,256]{1,0:T(8,128)S(1)} %get-tuple-element.37), channel_id=1, source_target_pairs={{0,12},{4,8},{8,4},{12,0},{1,13},{5,9},{9,5},{13,1},{2,14},{6,10},... | collective-permute-start | bytes 98312 | tf_op jit(solution)/shard_map/ppermute | solution.py:277
  27.7 4.8 %collective-permute-start.6 = (f32[32,256]{1,0:T(8,128)S(1)}, f32[32,256]{1,0:T(8,128)S(1)}, u32[]{:S(2)}, u32[]{:S(2)}) collective-permute-start(f32[32,256]{1,0:T(8,128)S(1)} %get-tuple-element.38), channel_id=1, source_target_pairs={{0,8},{4,12},{8,0},{12,4},{1,9},{5,13},{9,1},{13,5},{2,10},{6,14},... | collective-permute-start | bytes 98312 | tf_op jit(solution)/shard_map/ppermute | solution.py:277
  34.0 5.5 %collective-permute-start.10 = (bf16[32,256]{1,0:T(8,128)(2,1)S(1)}, bf16[32,256]{1,0:T(8,128)(2,1)S(1)}, u32[]{:S(2)}, u32[]{:S(2)}) collective-permute-start(bf16[32,256]{1,0:T(8,128)(2,1)S(1)} %get-tuple-element.35.low), channel_id=1, source_target_pairs={{0,12},{4,8},{8,4},{12,0},{1,13},{5,9},{9,5},{13,1},{2,14},{6,10},... | collective-permute-start | bytes 49160 | tf_op jit(solution)/shard_map/ppermute | solution.py:277
  36.2 4.6 %collective-permute-start.9 = (bf16[32,256]{1,0:T(8,128)(2,1)S(1)}, bf16[32,256]{1,0:T(8,128)(2,1)S(1)}, u32[]{:S(2)}, u32[]{:S(2)}) collective-permute-start(bf16[32,256]{1,0:T(8,128)(2,1)S(1)} %get-tuple-element.35.low), channel_id=1, source_target_pairs={{0,8},{4,12},{8,0},{12,4},{1,9},{5,13},{9,1},{13,5},{2,10},{6,14},... | collective-permute-start | bytes 49160 | tf_op jit(solution)/shard_map/ppermute | solution.py:277
  37.3 3.7 %collective-permute-start.8 = (bf16[32,256]{1,0:T(8,128)(2,1)S(1)}, bf16[32,256]{1,0:T(8,128)(2,1)S(1)}, u32[]{:S(2)}, u32[]{:S(2)}) collective-permute-start(bf16[32,256]{1,0:T(8,128)(2,1)S(1)} %get-tuple-element.35.low), channel_id=1, source_target_pairs={{0,4},{4,0},{8,12},{12,8},{1,5},{5,1},{9,13},{13,9},{2,6},{6,2},{1... | collective-permute-start | bytes 49160 | tf_op jit(solution)/shard_map/ppermute | solution.py:277

commit v5 on v4

--- a/solution.py
+++ b/solution.py
@@ -11,7 +11,8 @@
 info_rows = 16
 swap_limit = 8
 newton_steps = 10
-newton_goal = 4e-4
+newton_goal = 0.25
+solve_goal = 2e-6
 top = lax.Precision.HIGHEST
 f32 = jnp.float32
 bf16 = jnp.bfloat16
@@ -82,16 +83,33 @@
     return lax.bitwise_xor(u, me) if swaps else u
 
 
-def load_kernel(blocks, cube, sems):
+def load_kernel(tables, blocks, *refs):
+    infos, (cube, found, sems) = refs[:-3], refs[-3:]
     slots = cube.shape[0]
     copies = [pltpu.make_async_copy(blocks.at[0, 0, s], cube.at[s], sems.at[s]) for s in range(slots)]
     for copy in copies:
         copy.start()
+    rank = infos[0].shape[1]
+    me = lax.axis_index("ta")
+    grid = tables[0]
+    lane = lax.broadcasted_iota(jnp.int32, (1, rank), 1)
+    codes = []
+    for which, base in tables[1:]:
+        table = infos[which][base : base + info_rows, :].astype(f32)
+        cell = (table[1:2, :] * grid + table[2:3, :]).astype(jnp.int32)
+        wanted = table[0:1, :].astype(jnp.int32) == me + 1
+        code = jnp.where(wanted, cell, -1)
+        codes += [jnp.max(jnp.where(lane == s, code, -1)) for s in range(slots)]
+    count = jnp.int32(0)
+    for code in codes:
+        found[1 + count] = code
+        count = count + (code >= 0).astype(jnp.int32)
+    found[0] = count
     for copy in copies:
         copy.wait()
 
 
-def assemble(near, part, rest, first, away, side_away, mate, full_z, full_y, info):
+def assemble(near, rest, first, away, side_away, mate, side_mate, full_z, full_y):
     half = rest.shape[0] // 2
     quarter = half // 2
     rows = 2 * half
@@ -107,10 +125,8 @@
         full_z[at, :] = ref[base : base + count, :]
         full_y[at, :] = ref[base + count : base + 2 * count, :]
 
-    info[0:info_rows, :] = near[2 * half :, :]
     put(near, 0, me * rows + core * half, half)
     put(rest, 0, me * rows + (1 - core) * half, half)
-    info[info_rows : 2 * info_rows, :] = first[2 * half :, :]
     source = lax.bitwise_xor(me, 1) * rows
     put(first, 0, source + core * half, half)
     put(mate, 0, source + (1 - core) * half, half)
@@ -118,20 +134,19 @@
     for i in range(others):
         source = lax.bitwise_xor(me, i + 2) * rows
         base = i * short
-        info[(i + 2) * info_rows : (i + 3) * info_rows, :] = away[base + 2 * quarter : base + short, :]
         for ref, start, which, where in (
             (away, 0, core, side),
             (side_away, 0, core, 1 - side),
             (mate, tall, 1 - core, side),
-            (mate, tall + others * short, 1 - core, 1 - side),
+            (side_mate, 0, 1 - core, 1 - side),
         ):
             put(ref, start + base, source + which * half + where * quarter, quarter)
 
 
 def term_kernel(ta_count, edge, swaps, table, cube, *refs):
     if swaps:
-        pieces, (terms, full_z, full_y, info) = refs[:-4], refs[-4:]
-        assemble(*pieces, full_z, full_y, info)
+        pieces, (terms, full_z, full_y) = refs[:-3], refs[-3:]
+        assemble(*pieces, full_z, full_y)
     else:
         full_z, full_y, terms = refs
     slots, frames = cube.shape[0], cube.shape[1]
@@ -155,76 +170,63 @@
             terms[at, :] += jnp.where(live, summed, 0.0)
 
 
-def system_kernel(ta_count, slots, edge, info, full_z, full_y, system, inverse, codes):
+def system_kernel(edge, found, full_z, full_y, system, high, mid, low, inverse, guess_ref):
     rank = full_z.shape[1]
     grid = full_z.shape[0] // edge
-    me = lax.axis_index("ta")
-    lane = lax.broadcasted_iota(jnp.int32, (1, rank), 1)
-    for k in range(ta_count):
-        table = info[k * info_rows : (k + 1) * info_rows, :].astype(f32)
-        cell = (table[1:2, :] * grid + table[2:3, :]).astype(jnp.int32)
-        wanted = table[0:1, :].astype(jnp.int32) == me + 1
-        code = jnp.where(wanted, cell, -1)
-        for s in range(slots):
-            codes[k * slots + s] = jnp.max(jnp.where(lane == s, code, -1))
+    count = found[0]
     eye = lax.broadcasted_iota(jnp.int32, (rank, rank), 0) == lax.broadcasted_iota(
         jnp.int32, (rank, rank), 1
     )
     system[...] = jnp.where(eye, ridge_weight, 0.0).astype(f32)
 
-    @pl.loop(0, ta_count * slots)
-    def _(i):
-        code = codes[i]
-
-        @pl.when(code >= 0)
-        def _():
-            at = pl.multiple_of(lax.div(code, grid) * edge, edge)
-            panel_z = full_z[pl.ds(at, edge), :]
-            at = pl.multiple_of(lax.rem(code, grid) * edge, edge)
-            panel_y = full_y[pl.ds(at, edge), :]
-            over = (((0,), (0,)), ((), ()))
-            gram_z = lax.dot_general(panel_z, panel_z, over, preferred_element_type=f32)
-            gram_y = lax.dot_general(panel_y, panel_y, over, preferred_element_type=f32)
-            system[...] += gram_z * gram_y
+    def product(code):
+        over = (((0,), (0,)), ((), ()))
+        at = pl.multiple_of(lax.div(code, grid) * edge, edge)
+        panel_z = full_z[pl.ds(at, edge), :]
+        at = pl.multiple_of(lax.rem(code, grid) * edge, edge)
+        panel_y = full_y[pl.ds(at, edge), :]
+        gram_z = lax.dot_general(panel_z, panel_z, over, preferred_element_type=f32)
+        gram_y = lax.dot_general(panel_y, panel_y, over, preferred_element_type=f32)
+        return gram_z * gram_y
+
+    @pl.loop(0, lax.div(count + 1, 2))
+    def _(j):
+        one = found[1 + 2 * j]
+        paired = 2 * j + 1 < count
+        two = jnp.where(paired, found[2 + 2 * j], one)
+        system[...] += product(one) + product(two) * jnp.where(paired, 1.0, 0.0)
 
     matrix = system[...]
+    first = matrix.astype(bf16)
+    rest = matrix - first.astype(f32)
+    second = rest.astype(bf16)
+    high[...] = first
+    mid[...] = second
+    low[...] = (rest - second.astype(f32)).astype(bf16)
     down = 1.0 / jnp.sum(jnp.where(eye, matrix, 0.0), axis=1, keepdims=True)
     across = 1.0 / jnp.sum(jnp.where(eye, matrix, 0.0), axis=0, keepdims=True)
-    inverse[...] = jnp.where(eye, 2.0 * across, 0.0) - down * matrix * across
+    guess_ref[...] = jnp.where(eye, 2.0 * across, 0.0) - down * matrix * across
 
     def going(state):
         step, error = state
         return (step < newton_steps) & jnp.logical_not(error <= newton_goal)
 
     def newton(state):
-        guess = inverse[...]
-        miss = jnp.where(eye, 1.0, 0.0) - jnp.dot(
-            system[...], guess, precision=top, preferred_element_type=f32
-        )
-        inverse[...] = guess + jnp.dot(guess, miss, precision=top, preferred_element_type=f32)
+        guess = guess_ref[...]
+        short = guess.astype(bf16)
+        miss = jnp.where(eye, 1.0, 0.0) - jnp.dot(high[...], short, preferred_element_type=f32)
+        better = guess + jnp.dot(short, miss.astype(bf16), preferred_element_type=f32)
+        guess_ref[...] = better
+        inverse[...] = better.astype(bf16)
         return state[0] + 1, jnp.sum(miss * miss)
 
-    _, error = lax.while_loop(going, newton, (jnp.int32(0), jnp.float32(jnp.inf)))
-
-    @pl.when(jnp.logical_not(error <= newton_goal))
-    def _():
-        inverse[...] = system[...]
-        lanes = lax.broadcasted_iota(jnp.int32, (1, rank), 1)
-        subs = lax.broadcasted_iota(jnp.int32, (rank, 1), 0)
-
-        @pl.loop(0, rank)
-        def _(k):
-            whole = inverse[...]
-            row = inverse[pl.ds(k, 1), :]
-            column = jnp.sum(jnp.where(lanes == k, whole, 0.0), axis=1, keepdims=True)
-            pivot = 1.0 / jnp.sum(jnp.where(lanes == k, row, 0.0), axis=1, keepdims=True)
-            scaled = jnp.where(lanes == k, 1.0, row) * pivot
-            rest = jnp.where(lanes == k, 0.0, whole) - column * scaled
-            inverse[...] = jnp.where(subs == k, scaled, rest)
-
-
-def solve_kernel(ta_count, swaps, own, far, system, inverse, rows_out, low_out):
-    frames = rows_out.shape[0]
+    lax.while_loop(going, newton, newton((jnp.int32(0), jnp.float32(0.0))))
+
+
+def solve_kernel(
+    ta_count, swaps, own, far, system, high, mid, low, inverse, rows_out, low_out, exact
+):
+    frames, rank = rows_out.shape
     if swaps:
         rhs = own[0:frames, :]
         for k in range(1, ta_count):
@@ -233,12 +235,51 @@
         rhs = far[0:frames, :]
         for k in range(1, ta_count):
             rhs = rhs + far[k * frames : (k + 1) * frames, :]
-    dot = functools.partial(jnp.dot, precision=top, preferred_element_type=f32)
-    rows = dot(rhs, inverse[...])
-    rest = rhs - dot(rows, system[...])
-    rows = rows + dot(rest, inverse[...])
+    dot = functools.partial(jnp.dot, preferred_element_type=f32)
+
+    def residual(rows):
+        one = rows.astype(bf16)
+        rest = rows - one.astype(f32)
+        two = rest.astype(bf16)
+        three = (rest - two.astype(f32)).astype(bf16)
+        a = dot(jnp.concatenate([one, two, three], axis=0), high[...])
+        b = dot(jnp.concatenate([one, two], axis=0), mid[...])
+        c = dot(one, low[...])
+        small = (a[2 * frames :] + b[frames:]) + c
+        return ((rhs - a[:frames]) - (a[frames : 2 * frames] + b[:frames])) - small
+
+    rows = dot(rhs.astype(bf16), inverse[...])
+    rest_a = residual(rows)
+    rows = rows + dot(rest_a.astype(bf16), inverse[...])
+    rest_b = residual(rows)
+    rows = rows + dot(rest_b.astype(bf16), inverse[...])
     rows_out[...] = rows
-    low_out[...] = rows.astype(bf16)
+    scale = 1.0 / jnp.maximum(jnp.sum(rhs * rhs), 1e-30)
+    size_a = jnp.sum(rest_a * rest_a) * scale
+    size_b = jnp.sum(rest_b * rest_b) * scale
+
+    @pl.when(jnp.logical_not(size_b * size_b <= solve_goal * solve_goal * size_a))
+    def _():
+        exact[...] = system[...]
+        lanes = lax.broadcasted_iota(jnp.int32, (1, rank), 1)
+        subs = lax.broadcasted_iota(jnp.int32, (rank, 1), 0)
+
+        @pl.loop(0, rank)
+        def _(k):
+            whole = exact[...]
+            row = exact[pl.ds(k, 1), :]
+            column = jnp.sum(jnp.where(lanes == k, whole, 0.0), axis=1, keepdims=True)
+            pivot = 1.0 / jnp.sum(jnp.where(lanes == k, row, 0.0), axis=1, keepdims=True)
+            scaled = jnp.where(lanes == k, 1.0, row) * pivot
+            rest = jnp.where(lanes == k, 0.0, whole) - column * scaled
+            exact[...] = jnp.where(subs == k, scaled, rest)
+
+        full = functools.partial(dot, precision=top)
+        answer = full(rhs, exact[...])
+        miss = rhs - full(answer, system[...])
+        rows_out[...] = answer + full(miss, exact[...])
+
+    low_out[...] = rows_out[...].astype(bf16)
 
 
 def misfit_kernel(ta_count, edge, swaps, table, low, far, full_z, full_y, cube, out, every):
@@ -288,18 +329,25 @@
     shape = jax.ShapeDtypeStruct
     cells = jnp.swapaxes(block_cells, 2, 3)
     full = [shape((ta_count * rows, rank), bf16)] * 2
-    load = pl.pallas_call(
-        load_kernel,
-        out_shape=shape((slots, frames, edge, edge), bf16),
-        in_specs=[hbm_spec],
-        out_specs=vmem_spec,
-        scratch_shapes=[pltpu.SemaphoreType.DMA((slots,))],
-        compiler_params=params(8),
-        cost_estimate=pl.CostEstimate(
-            flops=0, transcendentals=0, bytes_accessed=4 * slots * frames * edge * edge
-        ),
-        name="load",
-    )
+    grid = ta_count * rows // edge
+
+    def load(blocks, tables, infos):
+        return pl.pallas_call(
+            functools.partial(load_kernel, [grid] + tables),
+            out_shape=[
+                shape((slots, frames, edge, edge), bf16),
+                shape((ta_count * slots + 2,), jnp.int32),
+            ],
+            in_specs=[hbm_spec] + [vmem_spec] * len(infos),
+            out_specs=[vmem_spec, smem_spec],
+            scratch_shapes=[pltpu.SemaphoreType.DMA((slots,))],
+            compiler_params=params(8),
+            cost_estimate=pl.CostEstimate(
+                flops=0, transcendentals=0, bytes_accessed=4 * slots * frames * edge * edge
+            ),
+            name="load",
+        )(held(blocks), *infos)
+
     if swaps:
         near, part, rest, table = pl.pallas_call(
             pack_kernel,
@@ -322,14 +370,20 @@
         first = swap(near, "ta", ta_count, 1)
         away = jnp.concatenate([swap(part, "ta", ta_count, k) for k in range(2, ta_count)], axis=0)
         first, away, blocks = lax.optimization_barrier((first, away, blocks))
-        side_away, cube = lax.optimization_barrier(
-            (swap(away, "pb", pb_count, 2), load(held(blocks)))
+        short = 2 * quarter + info_rows
+        tables = [(0, 2 * half), (1, 2 * half)]
+        tables += [(2, i * short + 2 * quarter) for i in range(ta_count - 2)]
+        side_away, mate, (cube, found) = lax.optimization_barrier(
+            (
+                swap(away, "pb", pb_count, 2),
+                swap(jnp.concatenate([first, away], axis=0), "pb", pb_count, 1),
+                load(blocks, tables, (near, first, away)),
+            )
         )
-        mate = swap(jnp.concatenate([first, away, side_away], axis=0), "pb", pb_count, 1)
-        pieces = (near, part, rest, first, away, side_away, mate)
-        made = full + [shape((ta_count * info_rows, rank), bf16)]
+        side_mate = swap(side_away, "pb", pb_count, 1)
+        pieces = (near, rest, first, away, side_away, mate, side_mate)
+        made = full
     else:
-        cube = load(held(blocks))
         table = jnp.concatenate([block_owner.reshape(slots), cells.reshape(2 * slots)])
         pieces = (
             lax.all_gather(qz_factor, "ta", axis=0, tiled=True),
@@ -340,6 +394,7 @@
         shown = shown.at[0, :slots].set(table[:slots] + 1)
         shown = shown.at[1:3, :slots].set(table[slots:].reshape(2, slots))
         info = lax.all_gather(shown.astype(bf16), "ta", axis=0, tiled=True)
+        cube, found = load(blocks, [(0, k * info_rows) for k in range(ta_count)], (info,))
     out = pl.pallas_call(
         functools.partial(term_kernel, ta_count, edge, swaps),
         out_shape=[shape((ta_count * frames, rank), f32)] + made,
@@ -350,7 +405,7 @@
     )(table, cube, *pieces)
     terms = out[0]
     if swaps:
-        full_z, full_y, info = out[1:]
+        full_z, full_y = out[1:]
         arrived = jnp.concatenate(
             [
                 swap(terms[k * frames : (k + 1) * frames], "ta", ta_count, k)
@@ -361,23 +416,25 @@
     else:
         full_z, full_y = pieces
         arrived = lax.all_to_all(terms, "ta", split_axis=0, concat_axis=0, tiled=True)
-    system, inverse = pl.pallas_call(
-        functools.partial(system_kernel, ta_count, slots, edge),
-        out_shape=[shape((rank, rank), f32)] * 2,
-        in_specs=[vmem_spec] * 3,
-        out_specs=[vmem_spec] * 2,
-        scratch_shapes=[pltpu.SMEM((ta_count * slots,), jnp.int32)],
+    square = [shape((rank, rank), f32)] + [shape((rank, rank), bf16)] * 4
+    parts = pl.pallas_call(
+        functools.partial(system_kernel, edge),
+        out_shape=square,
+        in_specs=[smem_spec] + [vmem_spec] * 2,
+        out_specs=[vmem_spec] * 5,
+        scratch_shapes=[pltpu.VMEM((rank, rank), f32)],
         compiler_params=params(16),
         name="system",
-    )(info, full_z, full_y)
+    )(found, full_z, full_y)
     new_rows, low = pl.pallas_call(
         functools.partial(solve_kernel, ta_count, swaps),
         out_shape=[shape((frames, rank), f32), shape((frames, rank), bf16)],
-        in_specs=[vmem_spec] * 4,
+        in_specs=[vmem_spec] * 7,
         out_specs=[vmem_spec] * 2,
+        scratch_shapes=[pltpu.VMEM((rank, rank), f32)],
         compiler_params=params(8),
         name="solve",
-    )(terms, arrived, system, inverse)
+    )(terms, arrived, *parts)
     if swaps:
         others = jnp.concatenate([swap(low, "ta", ta_count, k) for k in range(1, ta_count)], axis=0)
     else:

time: 44.7 us -> 45.2 us (1.011)
  waiting for transfers between devices: 12.7 us -> 14.6 us
  Pallas kernels: 15.4 us -> 14.1 us
    ppermute x11 -> x12, waiting for transfers between devices: 12.7 us -> 14.6 us  [swap(): return lax.ppermute(x, axis, [(i, i ^ k) for i in range(count)])]
    pallas_call x2, Pallas kernels: 5.76 us -> 4.56 us  [the longest x1 2.8 us: load(): pl.pallas_call(functools.partial(load_kernel, [grid] + tables), out_shape...]
    ppermute x11 -> x12, starting transfers between devices: 15.7 us -> 15.6 us  [swap(): return lax.ppermute(x, axis, [(i, i ^ k) for i in range(count)])]
  transfers between devices with their start and end apart: 11 -> 12, of which waited for: 10 -> 9; matrix products, arithmetic and copies ran while one was open for 0% -> 0% of each run, Pallas kernels for 13% -> 10%
where the time goes in v5:
time: 45.2 us; the launch traced here: 45.1 us
  starting transfers between devices  15.6 us (35%)
  waiting for transfers between devices  14.6 us (32%)
  Pallas kernels  14.1 us (31%)
  between operations  0.71 us (2%)
    ppermute x12, starting transfers between devices, swap(): return lax.ppermute(x, axis, [(i, i ^ k) for i in range(count)])  15.6 us
    ppermute x12, waiting for transfers between devices, swap(): return lax.ppermute(x, axis, [(i, i ^ k) for i in range(count)])  14.6 us
    pallas_call x1, Pallas kernels, body(): pl.pallas_call(functools.partial(misfit_kernel, ta_count, edge, swaps), o...  3.57 us
    pallas_call x1, Pallas kernels, body(): pl.pallas_call(functools.partial(term_kernel, ta_count, edge, swaps), out...  2.94 us
    pallas_call x1, Pallas kernels, load(): pl.pallas_call(functools.partial(load_kernel, [grid] + tables), out_shape...  2.8 us
    pallas_call x1, Pallas kernels, body(): pl.pallas_call(functools.partial(system_kernel, edge), out_shape=square,...  1.76 us
    pallas_call x1, Pallas kernels, body(): pl.pallas_call(pack_kernel, out_shape=[shape((2 * half + info_rows, rank)...  1.64 us
    pallas_call x1, Pallas kernels, body(): pl.pallas_call(functools.partial(solve_kernel, ta_count, swaps), out_shap...  1.4 us
  transfers between devices with their start and end apart: 12, of which 9 were waited for; matrix products, arithmetic and copies ran while one was open for 0% of the time, Pallas kernels for 10%

profile of v5, /device:TPU:0, one launch (start us, length us, event | category | flops | bytes accessed | tf_op | source)
XLA Modules:
  0.0 45.1 jit_solution(1373007690066036090)
XLA Ops:
  0.6 1.6 %pack.1 = (bf16[272,256]{1,0:T(8,128)(2,1)S(1)}, bf16[144,256]{1,0:T(8,128)(2,1)S(1)}, bf16[256,256]{1,0:T(8,128)(2,1)S(1)}, s32[12]{0:T(128)S(1)}) custom-call(s32[1,1,4]{2,1,0:T(1,128)} %owner_hbm.1, s32[1,1,2,4]{3,2,1,0:T(2,128)} %bitcast.2, bf16[256,256]{1,0:T(8,128)(2,1)} %z_hbm.1, bf16[256,256]{1,0:T(8,128)(2,1)} %y_hbm.1), custom_call_target="tpu_custom_call" | custom-call | tf_op jit(solution)/shard_map/pack/pallas_call | solution.py:352
  2.3 5.1 %collective-permute-start.2 = (bf16[144,256]{1,0:T(8,128)(2,1)S(1)}, bf16[144,256]{1,0:T(8,128)(2,1)S(1)}, u32[]{:S(2)}, u32[]{:S(2)}) collective-permute-start(bf16[144,256]{1,0:T(8,128)(2,1)S(1)} %get-tuple-element.27), channel_id=1, source_target_pairs={{0,12},{4,8},{8,4},{12,0},{1,13},{5,9},{9,5},{13,1},{2,14},{6,10},... | collective-permute-start | bytes 221192 | tf_op jit(solution)/shard_map/ppermute | solution.py:318
  7.4 0.0 collective-permute-start.1
  7.4 0.6 %collective-permute-start = (bf16[272,256]{1,0:T(8,128)(2,1)S(1)}, bf16[272,256]{1,0:T(8,128)(2,1)S(1)}, u32[]{:S(2)}, u32[]{:S(2)}) collective-permute-start(bf16[272,256]{1,0:T(8,128)(2,1)S(1)} %get-tuple-element.26.refs_0_), channel_id=1, source_target_pairs={{0,4},{4,0},{8,12},{12,8},{1,5},{5,1},{9,13},{13,9},{2,6},{6,2},{1... | collective-permute-start | bytes 417800 | tf_op jit(solution)/shard_map/ppermute | solution.py:318
  8.1 2.0 %collective-permute-done.2 = bf16[144,256]{1,0:T(8,128)(2,1)S(1)} collective-permute-done((bf16[144,256]{1,0:T(8,128)(2,1)S(1)}, bf16[144,256]{1,0:T(8,128)(2,1)S(1)}, u32[]{:S(2)}, u32[]{:S(2)}) %collective-permute-start.2) | collective-permute-done | bytes 73760 | tf_op jit(solution)/shard_map/ppermute | solution.py:318
  10.1 3.7 %collective-permute-done.1 = bf16[144,256]{1,0:T(8,128)(2,1)S(1)} collective-permute-done((bf16[144,256]{1,0:T(8,128)(2,1)S(1)}, bf16[144,256]{1,0:T(8,128)(2,1)S(1)}, u32[]{:S(2)}, u32[]{:S(2)}) %collective-permute-start.1) | collective-permute-done | bytes 73760 | tf_op jit(solution)/shard_map/ppermute | solution.py:318
  13.8 0.6 %collective-permute-done.refs_1_.refs_2_ = bf16[272,256]{1,0:T(8,128)(2,1)S(1)} collective-permute-done((bf16[272,256]{1,0:T(8,128)(2,1)S(1)}, bf16[272,256]{1,0:T(8,128)(2,1)S(1)}, u32[]{:S(2)}, u32[]{:S(2)}) %collective-permute-start) | collective-permute-done | bytes 139296 | tf_op jit(solution)/shard_map/ppermute | solution.py:318
  14.4 0.1 collective-permute-start.4
  14.5 1.8 %collective-permute-start.3 = (bf16[288,256]{1,0:T(8,128)(2,1)S(1)}, bf16[288,256]{1,0:T(8,128)(2,1)S(1)}, u32[]{:S(2)}, u32[]{:S(2)}) collective-permute-start(bf16[288,256]{1,0:T(8,128)(2,1)S(1)} %pad_maximum_fusion.1.refs_2_.refs_3_), channel_id=1, source_target_pairs={{0,2},{1,3},{2,0},{3,1},{4,6},{5,7},{6,4},{7,5},{8,10},{9,11},{10,... | collective-permute-start | bytes 442376 | tf_op jit(solution)/shard_map/ppermute | solution.py:318
  16.3 2.8 %load.1 = (bf16[4,32,128,128]{3,2,1,0:T(8,128)(2,1)S(1)}, s32[18]{0:T(128)S(1)}) custom-call(bf16[1,1,4,32,128,128]{5,4,3,2,1,0:T(8,128)(2,1)} %blocks, bf16[272,256]{1,0:T(8,128)(2,1)S(1)} %get-tuple-element.26.refs_0_, bf16[272,256]{1,0:T(8,128)(2,1)S(1)} %collective-permute-done.refs_1_.refs_2_, bf16[288,256]{1,0:T(8,128)(2,1)S(1)} %pad_maximum_fusion.1.refs_2_.refs_3_), custom_call_target="tpu_custom_call" | custom-call | bytes 8388608 | tf_op jit(solution)/shard_map/load/pallas_call | solution.py:335
  19.1 1.7 %collective-permute-done.3.refs_4_ = bf16[288,256]{1,0:T(8,128)(2,1)S(1)} collective-permute-done((bf16[288,256]{1,0:T(8,128)(2,1)S(1)}, bf16[288,256]{1,0:T(8,128)(2,1)S(1)}, u32[]{:S(2)}, u32[]{:S(2)}) %collective-permute-start.3) | collective-permute-done | bytes 147488 | tf_op jit(solution)/shard_map/ppermute | solution.py:318
  20.8 0.0 collective-permute-done.4.refs_5_
  20.8 0.0 collective-permute-start.5
  20.8 1.4 %collective-permute-done.5.refs_6_ = bf16[288,256]{1,0:T(8,128)(2,1)S(1)} collective-permute-done((bf16[288,256]{1,0:T(8,128)(2,1)S(1)}, bf16[288,256]{1,0:T(8,128)(2,1)S(1)}, u32[]{:S(2)}, u32[]{:S(2)}) %collective-permute-start.5) | collective-permute-done | bytes 147488 | tf_op jit(solution)/shard_map/ppermute | solution.py:318
  22.1 2.9 %terms.1 = (f32[128,256]{1,0:T(8,128)S(1)}, bf16[1024,256]{1,0:T(8,128)(2,1)S(1)}, bf16[1024,256]{1,0:T(8,128)(2,1)S(1)}) custom-call(s32[12]{0:T(128)S(1)} %get-tuple-element.25.table, bf16[4,32,128,128]{3,2,1,0:T(8,128)(2,1)S(1)} %get-tuple-element.33.cube, bf16[272,256]{1,0:T(8,128)(2,1)S(1)} %get-tuple-element.26.refs_0_, ...), custom_call_target="tpu_custom_call" | custom-call | tf_op jit(solution)/shard_map/terms/pallas_call | solution.py:398
  25.1 1.7 %collective-permute-start.6 = (f32[32,256]{1,0:T(8,128)S(1)}, f32[32,256]{1,0:T(8,128)S(1)}, u32[]{:S(2)}, u32[]{:S(2)}) collective-permute-start(f32[32,256]{1,0:T(8,128)S(1)} %get-tuple-element.48), channel_id=1, source_target_pairs={{0,4},{4,0},{8,12},{12,8},{1,5},{5,1},{9,13},{13,9},{2,6},{6,2},{1... | collective-permute-start | bytes 98312 | tf_op jit(solution)/shard_map/ppermute | solution.py:318
  26.8 1.4 %collective-permute-start.8 = (f32[32,256]{1,0:T(8,128)S(1)}, f32[32,256]{1,0:T(8,128)S(1)}, u32[]{:S(2)}, u32[]{:S(2)}) collective-permute-start(f32[32,256]{1,0:T(8,128)S(1)} %get-tuple-element.49), channel_id=1, source_target_pairs={{0,12},{4,8},{8,4},{12,0},{1,13},{5,9},{9,5},{13,1},{2,14},{6,10},... | collective-permute-start | bytes 98312 | tf_op jit(solution)/shard_map/ppermute | solution.py:318
  28.3 0.5 %collective-permute-start.7 = (f32[32,256]{1,0:T(8,128)S(1)}, f32[32,256]{1,0:T(8,128)S(1)}, u32[]{:S(2)}, u32[]{:S(2)}) collective-permute-start(f32[32,256]{1,0:T(8,128)S(1)} %get-tuple-element.50), channel_id=1, source_target_pairs={{0,8},{4,12},{8,0},{12,4},{1,9},{5,13},{9,1},{13,5},{2,10},{6,14},... | collective-permute-start | bytes 98312 | tf_op jit(solution)/shard_map/ppermute | solution.py:318
  28.7 1.8 %system.1 = (f32[256,256]{1,0:T(8,128)S(1)}, bf16[256,256]{1,0:T(8,128)(2,1)S(1)}, bf16[256,256]{1,0:T(8,128)(2,1)S(1)}, bf16[256,256]{1,0:T(8,128)(2,1)S(1)}, bf16[256,256]{1,0:T(8,128)(2,1)S(1)}) custom-call(s32[18]{0:T(128)S(1)} %get-tuple-element.38.found, bf16[1024,256]{1,0:T(8,128)(2,1)S(1)} %get-tuple-element.39.full_z, ...), custom_call_target="tpu_custom_call" | custom-call | tf_op jit(solution)/shard_map/system/pallas_call | solution.py:420
  30.5 0.0 collective-permute-done.6
  30.5 2.1 %collective-permute-done.8 = f32[32,256]{1,0:T(8,128)S(1)} collective-permute-done((f32[32,256]{1,0:T(8,128)S(1)}, f32[32,256]{1,0:T(8,128)S(1)}, u32[]{:S(2)}, u32[]{:S(2)}) %collective-permute-start.8) | collective-permute-done | bytes 32800 | tf_op jit(solution)/shard_map/ppermute | solution.py:318
  32.6 0.4 collective-permute-done.7
  33.1 1.4 %solve.1 = (f32[32,256]{1,0:T(8,128)}, bf16[32,256]{1,0:T(8,128)(2,1)S(1)}) custom-call(f32[128,256]{1,0:T(8,128)S(1)} %get-tuple-element.37.own, f32[96,256]{1,0:T(8,128)S(1)} %pad_maximum_fusion.2.far, f32[256,256]{1,0:T(8,128)S(1)} %get-tuple-element.41.system, bf16[256,256]{1,0:T(8,128)(2,1)S(1)} %get-tuple-element.42.high, ...), custom_call_target="tpu_custom_call" | custom-call | tf_op jit(solution)/shard_map/solve/pallas_call | solution.py:429
  34.5 2.4 %collective-permute-start.11 = (bf16[32,256]{1,0:T(8,128)(2,1)S(1)}, bf16[32,256]{1,0:T(8,128)(2,1)S(1)}, u32[]{:S(2)}, u32[]{:S(2)}) collective-permute-start(bf16[32,256]{1,0:T(8,128)(2,1)S(1)} %get-tuple-element.47.low), channel_id=1, source_target_pairs={{0,12},{4,8},{8,4},{12,0},{1,13},{5,9},{9,5},{13,1},{2,14},{6,10},... | collective-permute-start | bytes 49160 | tf_op jit(solution)/shard_map/ppermute | solution.py:318
  36.9 0.1 collective-permute-start.10
  37.0 1.9 %collective-permute-start.9 = (bf16[32,256]{1,0:T(8,128)(2,1)S(1)}, bf16[32,256]{1,0:T(8,128)(2,1)S(1)}, u32[]{:S(2)}, u32[]{:S(2)}) collective-permute-start(bf16[32,256]{1,0:T(8,128)(2,1)S(1)} %get-tuple-element.47.low), channel_id=1, source_target_pairs={{0,4},{4,0},{8,12},{12,8},{1,5},{5,1},{9,13},{13,9},{2,6},{6,2},{1... | collective-permute-start | bytes 49160 | tf_op jit(solution)/shard_map/ppermute | solution.py:318
  38.9 1.1 %collective-permute-done.11 = bf16[32,256]{1,0:T(8,128)(2,1)S(1)} collective-permute-done((bf16[32,256]{1,0:T(8,128)(2,1)S(1)}, bf16[32,256]{1,0:T(8,128)(2,1)S(1)}, u32[]{:S(2)}, u32[]{:S(2)}) %collective-permute-start.11) | collective-permute-done | bytes 16416 | tf_op jit(solution)/shard_map/ppermute | solution.py:318
  40.0 1.5 %collective-permute-done.10 = bf16[32,256]{1,0:T(8,128)(2,1)S(1)} collective-permute-done((bf16[32,256]{1,0:T(8,128)(2,1)S(1)}, bf16[32,256]{1,0:T(8,128)(2,1)S(1)}, u32[]{:S(2)}, u32[]{:S(2)}) %collective-permute-start.10) | collective-permute-done | bytes 16416 | tf_op jit(solution)/shard_map/ppermute | solution.py:318
  41.5 0.0 collective-permute-done.9
  41.5 3.6 %misfit.1 = f32[1,4]{1,0:T(1,128)} custom-call(s32[12]{0:T(128)S(1)} %get-tuple-element.25.table, bf16[32,256]{1,0:T(8,128)(2,1)S(1)} %get-tuple-element.47.low, bf16[96,256]{1,0:T(8,128)(2,1)S(1)} %pad_maximum_fusion.3.far, bf16[1024,256]{1,0:T(8,128)(2,1)S(1)} %get-tuple-element.39.full_z, bf16[1024,256]{1,0:T(8,128)(2,1)S(1)} %get-tuple-element.40.full_y, ...), custom_call_target="tpu_custom_call" | custom-call | tf_op jit(solution)/shard_map/misfit/pallas_call | solution.py:442
  (5 shorter events, 0.1 us)
Async XLA Ops:
  2.3 7.8 %collective-permute-start.2 = (bf16[144,256]{1,0:T(8,128)(2,1)S(1)}, bf16[144,256]{1,0:T(8,128)(2,1)S(1)}, u32[]{:S(2)}, u32[]{:S(2)}) collective-permute-start(bf16[144,256]{1,0:T(8,128)(2,1)S(1)} %get-tuple-element.27), channel_id=1, source_target_pairs={{0,12},{4,8},{8,4},{12,0},{1,13},{5,9},{9,5},{13,1},{2,14},{6,10},... | collective-permute-start | bytes 221192 | tf_op jit(solution)/shard_map/ppermute | solution.py:318
  7.4 6.3 %collective-permute-start.1 = (bf16[144,256]{1,0:T(8,128)(2,1)S(1)}, bf16[144,256]{1,0:T(8,128)(2,1)S(1)}, u32[]{:S(2)}, u32[]{:S(2)}) collective-permute-start(bf16[144,256]{1,0:T(8,128)(2,1)S(1)} %get-tuple-element.27), channel_id=1, source_target_pairs={{0,8},{4,12},{8,0},{12,4},{1,9},{5,13},{9,1},{13,5},{2,10},{6,14},... | collective-permute-start | bytes 221192 | tf_op jit(solution)/shard_map/ppermute | solution.py:318
  7.4 7.0 %collective-permute-start = (bf16[272,256]{1,0:T(8,128)(2,1)S(1)}, bf16[272,256]{1,0:T(8,128)(2,1)S(1)}, u32[]{:S(2)}, u32[]{:S(2)}) collective-permute-start(bf16[272,256]{1,0:T(8,128)(2,1)S(1)} %get-tuple-element.26.refs_0_), channel_id=1, source_target_pairs={{0,4},{4,0},{8,12},{12,8},{1,5},{5,1},{9,13},{13,9},{2,6},{6,2},{1... | collective-permute-start | bytes 417800 | tf_op jit(solution)/shard_map/ppermute | solution.py:318
  14.4 6.3 %collective-permute-start.4 = (bf16[560,256]{1,0:T(8,128)(2,1)S(1)}, bf16[560,256]{1,0:T(8,128)(2,1)S(1)}, u32[]{:S(2)}, u32[]{:S(2)}) collective-permute-start(bf16[560,256]{1,0:T(8,128)(2,1)S(1)} %pad_maximum_fusion), channel_id=1, source_target_pairs={{0,1},{1,0},{2,3},{3,2},{4,5},{5,4},{6,7},{7,6},{8,9},{9,8},{10,11... | collective-permute-start | bytes 860168 | tf_op jit(solution)/shard_map/ppermute | solution.py:318
  14.5 6.2 %collective-permute-start.3 = (bf16[288,256]{1,0:T(8,128)(2,1)S(1)}, bf16[288,256]{1,0:T(8,128)(2,1)S(1)}, u32[]{:S(2)}, u32[]{:S(2)}) collective-permute-start(bf16[288,256]{1,0:T(8,128)(2,1)S(1)} %pad_maximum_fusion.1.refs_2_.refs_3_), channel_id=1, source_target_pairs={{0,2},{1,3},{2,0},{3,1},{4,6},{5,7},{6,4},{7,5},{8,10},{9,11},{10,... | collective-permute-start | bytes 442376 | tf_op jit(solution)/shard_map/ppermute | solution.py:318
  20.8 1.4 %collective-permute-start.5 = (bf16[288,256]{1,0:T(8,128)(2,1)S(1)}, bf16[288,256]{1,0:T(8,128)(2,1)S(1)}, u32[]{:S(2)}, u32[]{:S(2)}) collective-permute-start(bf16[288,256]{1,0:T(8,128)(2,1)S(1)} %collective-permute-done.3.refs_4_), channel_id=1, source_target_pairs={{0,1},{1,0},{2,3},{3,2},{4,5},{5,4},{6,7},{7,6},{8,9},{9,8},{10,11... | collective-permute-start | bytes 442376 | tf_op jit(solution)/shard_map/ppermute | solution.py:318
  25.1 5.4 %collective-permute-start.6 = (f32[32,256]{1,0:T(8,128)S(1)}, f32[32,256]{1,0:T(8,128)S(1)}, u32[]{:S(2)}, u32[]{:S(2)}) collective-permute-start(f32[32,256]{1,0:T(8,128)S(1)} %get-tuple-element.48), channel_id=1, source_target_pairs={{0,4},{4,0},{8,12},{12,8},{1,5},{5,1},{9,13},{13,9},{2,6},{6,2},{1... | collective-permute-start | bytes 98312 | tf_op jit(solution)/shard_map/ppermute | solution.py:318
  26.8 5.8 %collective-permute-start.8 = (f32[32,256]{1,0:T(8,128)S(1)}, f32[32,256]{1,0:T(8,128)S(1)}, u32[]{:S(2)}, u32[]{:S(2)}) collective-permute-start(f32[32,256]{1,0:T(8,128)S(1)} %get-tuple-element.49), channel_id=1, source_target_pairs={{0,12},{4,8},{8,4},{12,0},{1,13},{5,9},{9,5},{13,1},{2,14},{6,10},... | collective-permute-start | bytes 98312 | tf_op jit(solution)/shard_map/ppermute | solution.py:318
  28.3 4.8 %collective-permute-start.7 = (f32[32,256]{1,0:T(8,128)S(1)}, f32[32,256]{1,0:T(8,128)S(1)}, u32[]{:S(2)}, u32[]{:S(2)}) collective-permute-start(f32[32,256]{1,0:T(8,128)S(1)} %get-tuple-element.50), channel_id=1, source_target_pairs={{0,8},{4,12},{8,0},{12,4},{1,9},{5,13},{9,1},{13,5},{2,10},{6,14},... | collective-permute-start | bytes 98312 | tf_op jit(solution)/shard_map/ppermute | solution.py:318
  34.5 5.5 %collective-permute-start.11 = (bf16[32,256]{1,0:T(8,128)(2,1)S(1)}, bf16[32,256]{1,0:T(8,128)(2,1)S(1)}, u32[]{:S(2)}, u32[]{:S(2)}) collective-permute-start(bf16[32,256]{1,0:T(8,128)(2,1)S(1)} %get-tuple-element.47.low), channel_id=1, source_target_pairs={{0,12},{4,8},{8,4},{12,0},{1,13},{5,9},{9,5},{13,1},{2,14},{6,10},... | collective-permute-start | bytes 49160 | tf_op jit(solution)/shard_map/ppermute | solution.py:318
  36.9 4.6 %collective-permute-start.10 = (bf16[32,256]{1,0:T(8,128)(2,1)S(1)}, bf16[32,256]{1,0:T(8,128)(2,1)S(1)}, u32[]{:S(2)}, u32[]{:S(2)}) collective-permute-start(bf16[32,256]{1,0:T(8,128)(2,1)S(1)} %get-tuple-element.47.low), channel_id=1, source_target_pairs={{0,8},{4,12},{8,0},{12,4},{1,9},{5,13},{9,1},{13,5},{2,10},{6,14},... | collective-permute-start | bytes 49160 | tf_op jit(solution)/shard_map/ppermute | solution.py:318
  37.0 4.5 %collective-permute-start.9 = (bf16[32,256]{1,0:T(8,128)(2,1)S(1)}, bf16[32,256]{1,0:T(8,128)(2,1)S(1)}, u32[]{:S(2)}, u32[]{:S(2)}) collective-permute-start(bf16[32,256]{1,0:T(8,128)(2,1)S(1)} %get-tuple-element.47.low), channel_id=1, source_target_pairs={{0,4},{4,0},{8,12},{12,8},{1,5},{5,1},{9,13},{13,9},{2,6},{6,2},{1... | collective-permute-start | bytes 49160 | tf_op jit(solution)/shard_map/ppermute | solution.py:318

commit v6 on v5

--- a/solution.py
+++ b/solution.py
@@ -7,12 +7,13 @@
 from jax.experimental.pallas import tpu as pltpu
 from jax.sharding import PartitionSpec as P
 
+
 ridge_weight = 0.1
 info_rows = 16
 swap_limit = 8
 newton_steps = 10
 newton_goal = 0.25
-solve_goal = 2e-6
+solve_goal = 1e-3
 top = lax.Precision.HIGHEST
 f32 = jnp.float32
 bf16 = jnp.bfloat16
@@ -143,7 +144,7 @@
             put(ref, start + base, source + which * half + where * quarter, quarter)
 
 
-def term_kernel(ta_count, edge, swaps, table, cube, *refs):
+def term_kernel(edge, swaps, table, cube, *refs):
     if swaps:
         pieces, (terms, full_z, full_y) = refs[:-3], refs[-3:]
         assemble(*pieces, full_z, full_y)
@@ -170,7 +171,7 @@
             terms[at, :] += jnp.where(live, summed, 0.0)
 
 
-def system_kernel(edge, found, full_z, full_y, system, high, mid, low, inverse, guess_ref):
+def system_kernel(edge, found, full_z, full_y, system, high, mid, low, inverse, tail, guess_ref):
     rank = full_z.shape[1]
     grid = full_z.shape[0] // edge
     count = found[0]
@@ -207,6 +208,9 @@
     across = 1.0 / jnp.sum(jnp.where(eye, matrix, 0.0), axis=0, keepdims=True)
     guess_ref[...] = jnp.where(eye, 2.0 * across, 0.0) - down * matrix * across
 
+    unit = jnp.where(eye, 1.0, 0.0)
+    dot = functools.partial(jnp.dot, preferred_element_type=f32)
+
     def going(state):
         step, error = state
         return (step < newton_steps) & jnp.logical_not(error <= newton_goal)
@@ -214,17 +218,23 @@
     def newton(state):
         guess = guess_ref[...]
         short = guess.astype(bf16)
-        miss = jnp.where(eye, 1.0, 0.0) - jnp.dot(high[...], short, preferred_element_type=f32)
-        better = guess + jnp.dot(short, miss.astype(bf16), preferred_element_type=f32)
-        guess_ref[...] = better
-        inverse[...] = better.astype(bf16)
+        miss = unit - dot(high[...], short)
+        guess_ref[...] = guess + dot(short, miss.astype(bf16))
         return state[0] + 1, jnp.sum(miss * miss)
 
     lax.while_loop(going, newton, newton((jnp.int32(0), jnp.float32(0.0))))
+    guess = guess_ref[...]
+    short = guess.astype(bf16)
+    rest = (guess - short.astype(f32)).astype(bf16)
+    miss = (unit - dot(high[...], short)) - (dot(high[...], rest) + dot(mid[...], short))
+    better = guess + dot(short, miss.astype(bf16))
+    short = better.astype(bf16)
+    inverse[...] = short
+    tail[...] = (better - short.astype(f32)).astype(bf16)
 
 
 def solve_kernel(
-    ta_count, swaps, own, far, system, high, mid, low, inverse, rows_out, low_out, exact
+    ta_count, swaps, own, far, system, high, mid, low, inverse, tail, rows_out, low_out, exact
 ):
     frames, rank = rows_out.shape
     if swaps:
@@ -248,17 +258,21 @@
         small = (a[2 * frames :] + b[frames:]) + c
         return ((rhs - a[:frames]) - (a[frames : 2 * frames] + b[:frames])) - small
 
-    rows = dot(rhs.astype(bf16), inverse[...])
-    rest_a = residual(rows)
-    rows = rows + dot(rest_a.astype(bf16), inverse[...])
-    rest_b = residual(rows)
-    rows = rows + dot(rest_b.astype(bf16), inverse[...])
+    def solved(right):
+        one = right.astype(bf16)
+        two = (right - one.astype(f32)).astype(bf16)
+        a = dot(jnp.concatenate([one, two], axis=0), inverse[...])
+        return a[:frames] + (a[frames:] + dot(one, tail[...]))
+
+    rows = solved(rhs)
+    rest = residual(rows)
+    rows = rows + solved(rest)
     rows_out[...] = rows
-    scale = 1.0 / jnp.maximum(jnp.sum(rhs * rhs), 1e-30)
-    size_a = jnp.sum(rest_a * rest_a) * scale
-    size_b = jnp.sum(rest_b * rest_b) * scale
-
-    @pl.when(jnp.logical_not(size_b * size_b <= solve_goal * solve_goal * size_a))
+    low_out[...] = rows.astype(bf16)
+
+    @pl.when(
+        jnp.logical_not(jnp.sum(rest * rest) <= solve_goal * solve_goal * jnp.sum(rhs * rhs))
+    )
     def _():
         exact[...] = system[...]
         lanes = lax.broadcasted_iota(jnp.int32, (1, rank), 1)
@@ -277,9 +291,9 @@
         full = functools.partial(dot, precision=top)
         answer = full(rhs, exact[...])
         miss = rhs - full(answer, system[...])
-        rows_out[...] = answer + full(miss, exact[...])
-
-    low_out[...] = rows_out[...].astype(bf16)
+        answer = answer + full(miss, exact[...])
+        rows_out[...] = answer
+        low_out[...] = answer.astype(bf16)
 
 
 def misfit_kernel(ta_count, edge, swaps, table, low, far, full_z, full_y, cube, out, every):
@@ -373,12 +387,11 @@
         short = 2 * quarter + info_rows
         tables = [(0, 2 * half), (1, 2 * half)]
         tables += [(2, i * short + 2 * quarter) for i in range(ta_count - 2)]
-        side_away, mate, (cube, found) = lax.optimization_barrier(
-            (
-                swap(away, "pb", pb_count, 2),
-                swap(jnp.concatenate([first, away], axis=0), "pb", pb_count, 1),
-                load(blocks, tables, (near, first, away)),
-            )
+        both = jnp.concatenate([first, away], axis=0)
+        cube, found = load(blocks, tables, (near, first, away))
+        both, cube, found = lax.optimization_barrier((both, cube, found))
+        side_away, mate = lax.optimization_barrier(
+            (swap(away, "pb", pb_count, 2), swap(both, "pb", pb_count, 1))
         )
         side_mate = swap(side_away, "pb", pb_count, 1)
         pieces = (near, rest, first, away, side_away, mate, side_mate)
@@ -396,7 +409,7 @@
         info = lax.all_gather(shown.astype(bf16), "ta", axis=0, tiled=True)
         cube, found = load(blocks, [(0, k * info_rows) for k in range(ta_count)], (info,))
     out = pl.pallas_call(
-        functools.partial(term_kernel, ta_count, edge, swaps),
+        functools.partial(term_kernel, edge, swaps),
         out_shape=[shape((ta_count * frames, rank), f32)] + made,
         in_specs=[smem_spec] + [vmem_spec] * (1 + len(pieces)),
         out_specs=[vmem_spec] * (1 + len(made)),
@@ -416,12 +429,12 @@
     else:
         full_z, full_y = pieces
         arrived = lax.all_to_all(terms, "ta", split_axis=0, concat_axis=0, tiled=True)
-    square = [shape((rank, rank), f32)] + [shape((rank, rank), bf16)] * 4
+    square = [shape((rank, rank), f32)] + [shape((rank, rank), bf16)] * 5
     parts = pl.pallas_call(
         functools.partial(system_kernel, edge),
         out_shape=square,
         in_specs=[smem_spec] + [vmem_spec] * 2,
-        out_specs=[vmem_spec] * 5,
+        out_specs=[vmem_spec] * 6,
         scratch_shapes=[pltpu.VMEM((rank, rank), f32)],
         compiler_params=params(16),
         name="system",
@@ -429,7 +442,7 @@
     new_rows, low = pl.pallas_call(
         functools.partial(solve_kernel, ta_count, swaps),
         out_shape=[shape((frames, rank), f32), shape((frames, rank), bf16)],
-        in_specs=[vmem_spec] * 7,
+        in_specs=[vmem_spec] * 8,
         out_specs=[vmem_spec] * 2,
         scratch_shapes=[pltpu.VMEM((rank, rank), f32)],
         compiler_params=params(8),
@@ -459,6 +472,7 @@
         P(("series", "ta"), "pb", None),
         P(("series", "ta"), "pb", None, None),
     )
+
     return jax.shard_map(
         body,
         mesh=mesh,

time: 45.2 us -> 47.8 us (1.058)
  waiting for transfers between devices: 14.6 us -> 17.2 us
    ppermute x12, waiting for transfers between devices: 14.6 us -> 17.2 us  [swap(): return lax.ppermute(x, axis, [(i, i ^ k) for i in range(count)])]
  transfers between devices with their start and end apart: 12 -> 12, of which waited for: 9 -> 9; matrix products, arithmetic and copies ran while one was open for 0% -> 0% of each run, Pallas kernels for 10% -> 4%
where the time goes in v6:
time: 47.8 us; the launch traced here: 47.6 us
  waiting for transfers between devices  17.2 us (36%)
  starting transfers between devices  15.6 us (33%)
  Pallas kernels  14 us (29%)
  between operations  0.71 us (1%)
    ppermute x12, waiting for transfers between devices, swap(): return lax.ppermute(x, axis, [(i, i ^ k) for i in range(count)])  17.2 us
    ppermute x12, starting transfers between devices, swap(): return lax.ppermute(x, axis, [(i, i ^ k) for i in range(count)])  15.6 us
    pallas_call x1, Pallas kernels, body(): pl.pallas_call(functools.partial(misfit_kernel, ta_count, edge, swaps), o...  3.56 us
    pallas_call x1, Pallas kernels, body(): pl.pallas_call(functools.partial(term_kernel, edge, swaps), out_shape=[sh...  2.95 us
    pallas_call x1, Pallas kernels, load(): pl.pallas_call(functools.partial(load_kernel, [grid] + tables), out_shape...  2.81 us
    pallas_call x1, Pallas kernels, body(): pl.pallas_call(functools.partial(system_kernel, edge), out_shape=square,...  1.92 us
    pallas_call x1, Pallas kernels, body(): pl.pallas_call(pack_kernel, out_shape=[shape((2 * half + info_rows, rank)...  1.64 us
    pallas_call x1, Pallas kernels, body(): pl.pallas_call(functools.partial(solve_kernel, ta_count, swaps), out_shap...  1.15 us
  transfers between devices with their start and end apart: 12, of which 9 were waited for; matrix products, arithmetic and copies ran while one was open for 0% of the time, Pallas kernels for 4%

profile of v6, /device:TPU:0, one launch (start us, length us, event | category | flops | bytes accessed | tf_op | source)
XLA Modules:
  0.0 47.6 jit_solution(8290517774831974368)
XLA Ops:
  0.6 1.6 %pack.1 = (bf16[272,256]{1,0:T(8,128)(2,1)S(1)}, bf16[144,256]{1,0:T(8,128)(2,1)S(1)}, bf16[256,256]{1,0:T(8,128)(2,1)S(1)}, s32[12]{0:T(128)S(1)}) custom-call(s32[1,1,4]{2,1,0:T(1,128)} %owner_hbm.1, s32[1,1,2,4]{3,2,1,0:T(2,128)} %bitcast.2, bf16[256,256]{1,0:T(8,128)(2,1)} %z_hbm.1, bf16[256,256]{1,0:T(8,128)(2,1)} %y_hbm.1), custom_call_target="tpu_custom_call" | custom-call | tf_op jit(solution)/shard_map/pack/pallas_call | solution.py:366
  2.3 5.1 %collective-permute-start.2 = (bf16[144,256]{1,0:T(8,128)(2,1)S(1)}, bf16[144,256]{1,0:T(8,128)(2,1)S(1)}, u32[]{:S(2)}, u32[]{:S(2)}) collective-permute-start(bf16[144,256]{1,0:T(8,128)(2,1)S(1)} %get-tuple-element.29), channel_id=1, source_target_pairs={{0,12},{4,8},{8,4},{12,0},{1,13},{5,9},{9,5},{13,1},{2,14},{6,10},... | collective-permute-start | bytes 221192 | tf_op jit(solution)/shard_map/ppermute | solution.py:332
  7.4 0.0 collective-permute-start.1
  7.4 0.6 %collective-permute-start = (bf16[272,256]{1,0:T(8,128)(2,1)S(1)}, bf16[272,256]{1,0:T(8,128)(2,1)S(1)}, u32[]{:S(2)}, u32[]{:S(2)}) collective-permute-start(bf16[272,256]{1,0:T(8,128)(2,1)S(1)} %get-tuple-element.28.refs_0_), channel_id=1, source_target_pairs={{0,4},{4,0},{8,12},{12,8},{1,5},{5,1},{9,13},{13,9},{2,6},{6,2},{1... | collective-permute-start | bytes 417800 | tf_op jit(solution)/shard_map/ppermute | solution.py:332
  8.1 2.0 %collective-permute-done.2 = bf16[144,256]{1,0:T(8,128)(2,1)S(1)} collective-permute-done((bf16[144,256]{1,0:T(8,128)(2,1)S(1)}, bf16[144,256]{1,0:T(8,128)(2,1)S(1)}, u32[]{:S(2)}, u32[]{:S(2)}) %collective-permute-start.2) | collective-permute-done | bytes 73760 | tf_op jit(solution)/shard_map/ppermute | solution.py:332
  10.1 3.7 %collective-permute-done.1 = bf16[144,256]{1,0:T(8,128)(2,1)S(1)} collective-permute-done((bf16[144,256]{1,0:T(8,128)(2,1)S(1)}, bf16[144,256]{1,0:T(8,128)(2,1)S(1)}, u32[]{:S(2)}, u32[]{:S(2)}) %collective-permute-start.1) | collective-permute-done | bytes 73760 | tf_op jit(solution)/shard_map/ppermute | solution.py:332
  13.8 0.6 %collective-permute-done.refs_1_.refs_2_ = bf16[272,256]{1,0:T(8,128)(2,1)S(1)} collective-permute-done((bf16[272,256]{1,0:T(8,128)(2,1)S(1)}, bf16[272,256]{1,0:T(8,128)(2,1)S(1)}, u32[]{:S(2)}, u32[]{:S(2)}) %collective-permute-start) | collective-permute-done | bytes 139296 | tf_op jit(solution)/shard_map/ppermute | solution.py:332
  14.4 2.8 %load.1 = (bf16[4,32,128,128]{3,2,1,0:T(8,128)(2,1)S(1)}, s32[18]{0:T(128)S(1)}) custom-call(bf16[1,1,4,32,128,128]{5,4,3,2,1,0:T(8,128)(2,1)} %blocks, bf16[272,256]{1,0:T(8,128)(2,1)S(1)} %get-tuple-element.28.refs_0_, bf16[272,256]{1,0:T(8,128)(2,1)S(1)} %collective-permute-done.refs_1_.refs_2_, bf16[288,256]{1,0:T(8,128)(2,1)S(1)} %pad_maximum_fusion.1.refs_2_.refs_3_), custom_call_target="tpu_custom_call" | custom-call | bytes 8388608 | tf_op jit(solution)/shard_map/load/pallas_call | solution.py:349
  17.2 0.1 collective-permute-start.4
  17.3 1.8 %collective-permute-start.3 = (bf16[288,256]{1,0:T(8,128)(2,1)S(1)}, bf16[288,256]{1,0:T(8,128)(2,1)S(1)}, u32[]{:S(2)}, u32[]{:S(2)}) collective-permute-start(bf16[288,256]{1,0:T(8,128)(2,1)S(1)} %pad_maximum_fusion.1.refs_2_.refs_3_), channel_id=1, source_target_pairs={{0,2},{1,3},{2,0},{3,1},{4,6},{5,7},{6,4},{7,5},{8,10},{9,11},{10,... | collective-permute-start | bytes 442376 | tf_op jit(solution)/shard_map/ppermute | solution.py:332
  19.1 4.5 %collective-permute-done.3.refs_4_ = bf16[288,256]{1,0:T(8,128)(2,1)S(1)} collective-permute-done((bf16[288,256]{1,0:T(8,128)(2,1)S(1)}, bf16[288,256]{1,0:T(8,128)(2,1)S(1)}, u32[]{:S(2)}, u32[]{:S(2)}) %collective-permute-start.3) | collective-permute-done | bytes 147488 | tf_op jit(solution)/shard_map/ppermute | solution.py:332
  23.6 0.0 collective-permute-done.4.refs_5_
  23.6 0.0 collective-permute-start.5
  23.6 1.4 %collective-permute-done.5.refs_6_ = bf16[288,256]{1,0:T(8,128)(2,1)S(1)} collective-permute-done((bf16[288,256]{1,0:T(8,128)(2,1)S(1)}, bf16[288,256]{1,0:T(8,128)(2,1)S(1)}, u32[]{:S(2)}, u32[]{:S(2)}) %collective-permute-start.5) | collective-permute-done | bytes 147488 | tf_op jit(solution)/shard_map/ppermute | solution.py:332
  24.9 2.9 %terms.1 = (f32[128,256]{1,0:T(8,128)S(1)}, bf16[1024,256]{1,0:T(8,128)(2,1)S(1)}, bf16[1024,256]{1,0:T(8,128)(2,1)S(1)}) custom-call(s32[12]{0:T(128)S(1)} %get-tuple-element.27.table, bf16[4,32,128,128]{3,2,1,0:T(8,128)(2,1)S(1)} %get-tuple-element.35.cube, bf16[272,256]{1,0:T(8,128)(2,1)S(1)} %get-tuple-element.28.refs_0_, ...), custom_call_target="tpu_custom_call" | custom-call | tf_op jit(solution)/shard_map/terms/pallas_call | solution.py:411
  27.9 1.7 %collective-permute-start.6 = (f32[32,256]{1,0:T(8,128)S(1)}, f32[32,256]{1,0:T(8,128)S(1)}, u32[]{:S(2)}, u32[]{:S(2)}) collective-permute-start(f32[32,256]{1,0:T(8,128)S(1)} %get-tuple-element.52), channel_id=1, source_target_pairs={{0,4},{4,0},{8,12},{12,8},{1,5},{5,1},{9,13},{13,9},{2,6},{6,2},{1... | collective-permute-start | bytes 98312 | tf_op jit(solution)/shard_map/ppermute | solution.py:332
  29.6 1.4 %collective-permute-start.8 = (f32[32,256]{1,0:T(8,128)S(1)}, f32[32,256]{1,0:T(8,128)S(1)}, u32[]{:S(2)}, u32[]{:S(2)}) collective-permute-start(f32[32,256]{1,0:T(8,128)S(1)} %get-tuple-element.53), channel_id=1, source_target_pairs={{0,12},{4,8},{8,4},{12,0},{1,13},{5,9},{9,5},{13,1},{2,14},{6,10},... | collective-permute-start | bytes 98312 | tf_op jit(solution)/shard_map/ppermute | solution.py:332
  31.1 0.5 %collective-permute-start.7 = (f32[32,256]{1,0:T(8,128)S(1)}, f32[32,256]{1,0:T(8,128)S(1)}, u32[]{:S(2)}, u32[]{:S(2)}) collective-permute-start(f32[32,256]{1,0:T(8,128)S(1)} %get-tuple-element.54), channel_id=1, source_target_pairs={{0,8},{4,12},{8,0},{12,4},{1,9},{5,13},{9,1},{13,5},{2,10},{6,14},... | collective-permute-start | bytes 98312 | tf_op jit(solution)/shard_map/ppermute | solution.py:332
  31.6 1.9 %system.1 = (f32[256,256]{1,0:T(8,128)S(1)}, bf16[256,256]{1,0:T(8,128)(2,1)S(1)}, bf16[256,256]{1,0:T(8,128)(2,1)S(1)}, bf16[256,256]{1,0:T(8,128)(2,1)S(1)}, b...) custom-call(s32[18]{0:T(128)S(1)} %get-tuple-element.41.found, bf16[1024,256]{1,0:T(8,128)(2,1)S(1)} %get-tuple-element.42.full_z, ...), custom_call_target="tpu_custom_call" | custom-call | tf_op jit(solution)/shard_map/system/pallas_call | solution.py:433
  33.5 0.0 collective-permute-done.6
  33.5 1.9 %collective-permute-done.8 = f32[32,256]{1,0:T(8,128)S(1)} collective-permute-done((f32[32,256]{1,0:T(8,128)S(1)}, f32[32,256]{1,0:T(8,128)S(1)}, u32[]{:S(2)}, u32[]{:S(2)}) %collective-permute-start.8) | collective-permute-done | bytes 32800 | tf_op jit(solution)/shard_map/ppermute | solution.py:332
  35.4 0.4 collective-permute-done.7
  35.9 1.2 %solve.1 = (f32[32,256]{1,0:T(8,128)}, bf16[32,256]{1,0:T(8,128)(2,1)S(1)}) custom-call(f32[128,256]{1,0:T(8,128)S(1)} %get-tuple-element.40.own, f32[96,256]{1,0:T(8,128)S(1)} %pad_maximum_fusion.2.far, f32[256,256]{1,0:T(8,128)S(1)} %get-tuple-element.44.system, bf16[256,256]{1,0:T(8,128)(2,1)S(1)} %get-tuple-element.45.high, ...), custom_call_target="tpu_custom_call" | custom-call | tf_op jit(solution)/shard_map/solve/pallas_call | solution.py:442
  37.1 2.4 %collective-permute-start.11 = (bf16[32,256]{1,0:T(8,128)(2,1)S(1)}, bf16[32,256]{1,0:T(8,128)(2,1)S(1)}, u32[]{:S(2)}, u32[]{:S(2)}) collective-permute-start(bf16[32,256]{1,0:T(8,128)(2,1)S(1)} %get-tuple-element.51.low), channel_id=1, source_target_pairs={{0,12},{4,8},{8,4},{12,0},{1,13},{5,9},{9,5},{13,1},{2,14},{6,10},... | collective-permute-start | bytes 49160 | tf_op jit(solution)/shard_map/ppermute | solution.py:332
  39.4 0.1 collective-permute-start.10
  39.6 1.9 %collective-permute-start.9 = (bf16[32,256]{1,0:T(8,128)(2,1)S(1)}, bf16[32,256]{1,0:T(8,128)(2,1)S(1)}, u32[]{:S(2)}, u32[]{:S(2)}) collective-permute-start(bf16[32,256]{1,0:T(8,128)(2,1)S(1)} %get-tuple-element.51.low), channel_id=1, source_target_pairs={{0,4},{4,0},{8,12},{12,8},{1,5},{5,1},{9,13},{13,9},{2,6},{6,2},{1... | collective-permute-start | bytes 49160 | tf_op jit(solution)/shard_map/ppermute | solution.py:332
  41.4 1.1 %collective-permute-done.11 = bf16[32,256]{1,0:T(8,128)(2,1)S(1)} collective-permute-done((bf16[32,256]{1,0:T(8,128)(2,1)S(1)}, bf16[32,256]{1,0:T(8,128)(2,1)S(1)}, u32[]{:S(2)}, u32[]{:S(2)}) %collective-permute-start.11) | collective-permute-done | bytes 16416 | tf_op jit(solution)/shard_map/ppermute | solution.py:332
  42.6 1.5 %collective-permute-done.10 = bf16[32,256]{1,0:T(8,128)(2,1)S(1)} collective-permute-done((bf16[32,256]{1,0:T(8,128)(2,1)S(1)}, bf16[32,256]{1,0:T(8,128)(2,1)S(1)}, u32[]{:S(2)}, u32[]{:S(2)}) %collective-permute-start.10) | collective-permute-done | bytes 16416 | tf_op jit(solution)/shard_map/ppermute | solution.py:332
  44.1 0.0 collective-permute-done.9
  44.1 3.6 %misfit.1 = f32[1,4]{1,0:T(1,128)} custom-call(s32[12]{0:T(128)S(1)} %get-tuple-element.27.table, bf16[32,256]{1,0:T(8,128)(2,1)S(1)} %get-tuple-element.51.low, bf16[96,256]{1,0:T(8,128)(2,1)S(1)} %pad_maximum_fusion.3.far, bf16[1024,256]{1,0:T(8,128)(2,1)S(1)} %get-tuple-element.42.full_z, bf16[1024,256]{1,0:T(8,128)(2,1)S(1)} %get-tuple-element.43.full_y, ...), custom_call_target="tpu_custom_call" | custom-call | tf_op jit(solution)/shard_map/misfit/pallas_call | solution.py:455
  (5 shorter events, 0.1 us)
Async XLA Ops:
  2.3 7.8 %collective-permute-start.2 = (bf16[144,256]{1,0:T(8,128)(2,1)S(1)}, bf16[144,256]{1,0:T(8,128)(2,1)S(1)}, u32[]{:S(2)}, u32[]{:S(2)}) collective-permute-start(bf16[144,256]{1,0:T(8,128)(2,1)S(1)} %get-tuple-element.29), channel_id=1, source_target_pairs={{0,12},{4,8},{8,4},{12,0},{1,13},{5,9},{9,5},{13,1},{2,14},{6,10},... | collective-permute-start | bytes 221192 | tf_op jit(solution)/shard_map/ppermute | solution.py:332
  7.4 6.3 %collective-permute-start.1 = (bf16[144,256]{1,0:T(8,128)(2,1)S(1)}, bf16[144,256]{1,0:T(8,128)(2,1)S(1)}, u32[]{:S(2)}, u32[]{:S(2)}) collective-permute-start(bf16[144,256]{1,0:T(8,128)(2,1)S(1)} %get-tuple-element.29), channel_id=1, source_target_pairs={{0,8},{4,12},{8,0},{12,4},{1,9},{5,13},{9,1},{13,5},{2,10},{6,14},... | collective-permute-start | bytes 221192 | tf_op jit(solution)/shard_map/ppermute | solution.py:332
  7.4 7.0 %collective-permute-start = (bf16[272,256]{1,0:T(8,128)(2,1)S(1)}, bf16[272,256]{1,0:T(8,128)(2,1)S(1)}, u32[]{:S(2)}, u32[]{:S(2)}) collective-permute-start(bf16[272,256]{1,0:T(8,128)(2,1)S(1)} %get-tuple-element.28.refs_0_), channel_id=1, source_target_pairs={{0,4},{4,0},{8,12},{12,8},{1,5},{5,1},{9,13},{13,9},{2,6},{6,2},{1... | collective-permute-start | bytes 417800 | tf_op jit(solution)/shard_map/ppermute | solution.py:332
  17.2 6.3 %collective-permute-start.4 = (bf16[560,256]{1,0:T(8,128)(2,1)S(1)}, bf16[560,256]{1,0:T(8,128)(2,1)S(1)}, u32[]{:S(2)}, u32[]{:S(2)}) collective-permute-start(bf16[560,256]{1,0:T(8,128)(2,1)S(1)} %pad_maximum_fusion), channel_id=1, source_target_pairs={{0,1},{1,0},{2,3},{3,2},{4,5},{5,4},{6,7},{7,6},{8,9},{9,8},{10,11... | collective-permute-start | bytes 860168 | tf_op jit(solution)/shard_map/ppermute | solution.py:332
  17.3 6.2 %collective-permute-start.3 = (bf16[288,256]{1,0:T(8,128)(2,1)S(1)}, bf16[288,256]{1,0:T(8,128)(2,1)S(1)}, u32[]{:S(2)}, u32[]{:S(2)}) collective-permute-start(bf16[288,256]{1,0:T(8,128)(2,1)S(1)} %pad_maximum_fusion.1.refs_2_.refs_3_), channel_id=1, source_target_pairs={{0,2},{1,3},{2,0},{3,1},{4,6},{5,7},{6,4},{7,5},{8,10},{9,11},{10,... | collective-permute-start | bytes 442376 | tf_op jit(solution)/shard_map/ppermute | solution.py:332
  23.6 1.4 %collective-permute-start.5 = (bf16[288,256]{1,0:T(8,128)(2,1)S(1)}, bf16[288,256]{1,0:T(8,128)(2,1)S(1)}, u32[]{:S(2)}, u32[]{:S(2)}) collective-permute-start(bf16[288,256]{1,0:T(8,128)(2,1)S(1)} %collective-permute-done.3.refs_4_), channel_id=1, source_target_pairs={{0,1},{1,0},{2,3},{3,2},{4,5},{5,4},{6,7},{7,6},{8,9},{9,8},{10,11... | collective-permute-start | bytes 442376 | tf_op jit(solution)/shard_map/ppermute | solution.py:332
  27.9 5.6 %collective-permute-start.6 = (f32[32,256]{1,0:T(8,128)S(1)}, f32[32,256]{1,0:T(8,128)S(1)}, u32[]{:S(2)}, u32[]{:S(2)}) collective-permute-start(f32[32,256]{1,0:T(8,128)S(1)} %get-tuple-element.52), channel_id=1, source_target_pairs={{0,4},{4,0},{8,12},{12,8},{1,5},{5,1},{9,13},{13,9},{2,6},{6,2},{1... | collective-permute-start | bytes 98312 | tf_op jit(solution)/shard_map/ppermute | solution.py:332
  29.6 5.8 %collective-permute-start.8 = (f32[32,256]{1,0:T(8,128)S(1)}, f32[32,256]{1,0:T(8,128)S(1)}, u32[]{:S(2)}, u32[]{:S(2)}) collective-permute-start(f32[32,256]{1,0:T(8,128)S(1)} %get-tuple-element.53), channel_id=1, source_target_pairs={{0,12},{4,8},{8,4},{12,0},{1,13},{5,9},{9,5},{13,1},{2,14},{6,10},... | collective-permute-start | bytes 98312 | tf_op jit(solution)/shard_map/ppermute | solution.py:332
  31.1 4.8 %collective-permute-start.7 = (f32[32,256]{1,0:T(8,128)S(1)}, f32[32,256]{1,0:T(8,128)S(1)}, u32[]{:S(2)}, u32[]{:S(2)}) collective-permute-start(f32[32,256]{1,0:T(8,128)S(1)} %get-tuple-element.54), channel_id=1, source_target_pairs={{0,8},{4,12},{8,0},{12,4},{1,9},{5,13},{9,1},{13,5},{2,10},{6,14},... | collective-permute-start | bytes 98312 | tf_op jit(solution)/shard_map/ppermute | solution.py:332
  37.1 5.5 %collective-permute-start.11 = (bf16[32,256]{1,0:T(8,128)(2,1)S(1)}, bf16[32,256]{1,0:T(8,128)(2,1)S(1)}, u32[]{:S(2)}, u32[]{:S(2)}) collective-permute-start(bf16[32,256]{1,0:T(8,128)(2,1)S(1)} %get-tuple-element.51.low), channel_id=1, source_target_pairs={{0,12},{4,8},{8,4},{12,0},{1,13},{5,9},{9,5},{13,1},{2,14},{6,10},... | collective-permute-start | bytes 49160 | tf_op jit(solution)/shard_map/ppermute | solution.py:332
  39.4 4.6 %collective-permute-start.10 = (bf16[32,256]{1,0:T(8,128)(2,1)S(1)}, bf16[32,256]{1,0:T(8,128)(2,1)S(1)}, u32[]{:S(2)}, u32[]{:S(2)}) collective-permute-start(bf16[32,256]{1,0:T(8,128)(2,1)S(1)} %get-tuple-element.51.low), channel_id=1, source_target_pairs={{0,8},{4,12},{8,0},{12,4},{1,9},{5,13},{9,1},{13,5},{2,10},{6,14},... | collective-permute-start | bytes 49160 | tf_op jit(solution)/shard_map/ppermute | solution.py:332
  39.6 4.5 %collective-permute-start.9 = (bf16[32,256]{1,0:T(8,128)(2,1)S(1)}, bf16[32,256]{1,0:T(8,128)(2,1)S(1)}, u32[]{:S(2)}, u32[]{:S(2)}) collective-permute-start(bf16[32,256]{1,0:T(8,128)(2,1)S(1)} %get-tuple-element.51.low), channel_id=1, source_target_pairs={{0,4},{4,0},{8,12},{12,8},{1,5},{5,1},{9,13},{13,9},{2,6},{6,2},{1... | collective-permute-start | bytes 49160 | tf_op jit(solution)/shard_map/ppermute | solution.py:332

commit v7 on v6

--- a/solution.py
+++ b/solution.py
@@ -9,7 +9,7 @@
 
 
 ridge_weight = 0.1
-info_rows = 16
+info_rows = 8
 swap_limit = 8
 newton_steps = 10
 newton_goal = 0.25
@@ -31,7 +31,7 @@
     return pltpu.CompilerParams(vmem_limit_bytes=mib * 1024 * 1024)
 
 
-def pack_kernel(owner_hbm, cells_hbm, z_hbm, y_hbm, half_ref, part_ref, rest_ref, table_ref, owner, cells, sems):
+def pack_kernel(owner_hbm, cells_hbm, z_hbm, y_hbm, half_ref, part_ref, rest_ref, owner, cells, sems):
     half = z_hbm.shape[0] // 2
     part = half // 2
     rank = z_hbm.shape[1]
@@ -69,7 +69,6 @@
     for s in range(slots):
         values = (owner[0, 0, s], cells[0, 0, 0, s], cells[0, 0, 1, s])
         for r, value in enumerate(values):
-            table_ref[r * slots + s] = value
             shown = value + 1 if r == 0 else value
             table = jnp.where((row == r) & (lane == s), shown, table)
     table = table.astype(f32).astype(bf16)
@@ -84,18 +83,32 @@
     return lax.bitwise_xor(u, me) if swaps else u
 
 
-def load_kernel(tables, blocks, *refs):
-    infos, (cube, found, sems) = refs[:-3], refs[-3:]
+def load_kernel(blocks, owner_hbm, cells_hbm, cube, table, owner, cells, sems):
     slots = cube.shape[0]
-    copies = [pltpu.make_async_copy(blocks.at[0, 0, s], cube.at[s], sems.at[s]) for s in range(slots)]
+    copies = [
+        pltpu.make_async_copy(owner_hbm, owner, sems.at[slots]),
+        pltpu.make_async_copy(cells_hbm, cells, sems.at[slots + 1]),
+    ]
+    copies += [
+        pltpu.make_async_copy(blocks.at[0, 0, s], cube.at[s], sems.at[s]) for s in range(slots)
+    ]
     for copy in copies:
         copy.start()
+    for copy in copies:
+        copy.wait()
+    for s in range(slots):
+        table[s] = owner[0, 0, s]
+        table[slots + s] = cells[0, 0, 0, s]
+        table[2 * slots + s] = cells[0, 0, 1, s]
+
+
+def match_kernel(slots, grid, tables, *refs):
+    infos, found = refs[:-1], refs[-1]
     rank = infos[0].shape[1]
     me = lax.axis_index("ta")
-    grid = tables[0]
     lane = lax.broadcasted_iota(jnp.int32, (1, rank), 1)
     codes = []
-    for which, base in tables[1:]:
+    for which, base in tables:
         table = infos[which][base : base + info_rows, :].astype(f32)
         cell = (table[1:2, :] * grid + table[2:3, :]).astype(jnp.int32)
         wanted = table[0:1, :].astype(jnp.int32) == me + 1
@@ -106,16 +119,14 @@
         found[1 + count] = code
         count = count + (code >= 0).astype(jnp.int32)
     found[0] = count
-    for copy in copies:
-        copy.wait()
 
 
 def assemble(near, rest, first, away, side_away, mate, side_mate, full_z, full_y):
     half = rest.shape[0] // 2
     quarter = half // 2
     rows = 2 * half
-    tall = 2 * half + info_rows
-    short = 2 * quarter + info_rows
+    tall = 2 * half
+    short = 2 * quarter
     me = lax.axis_index("ta")
     column = lax.axis_index("pb")
     core = lax.rem(column, 2)
@@ -296,8 +307,12 @@
         low_out[...] = answer.astype(bf16)
 
 
-def misfit_kernel(ta_count, edge, swaps, table, low, far, full_z, full_y, cube, out, every):
+def misfit_kernel(
+    ta_count, edge, swaps, table, low, far, full_z, full_y, cube, rows_in, out, rows_out, every, sem
+):
     slots, frames = cube.shape[0], cube.shape[1]
+    leaving = pltpu.make_async_copy(rows_in, rows_out, sem)
+    leaving.start()
     if swaps:
         every[0] = low[...].astype(f32)
     first = 1 if swaps else 0
@@ -326,6 +341,7 @@
         mean = jnp.sum(total) * (1.0 / (frames * edge * edge))
         answer = jnp.where((lane == s) & (u >= 0), mean, answer)
     out[...] = answer
+    leaving.wait()
 
 
 def swap(x, axis, count, k):
@@ -344,60 +360,67 @@
     cells = jnp.swapaxes(block_cells, 2, 3)
     full = [shape((ta_count * rows, rank), bf16)] * 2
     grid = ta_count * rows // edge
-
-    def load(blocks, tables, infos):
+    small = [
+        pltpu.SMEM(block_owner.shape, jnp.int32),
+        pltpu.SMEM(cells.shape, jnp.int32),
+    ]
+    cube, table = pl.pallas_call(
+        load_kernel,
+        out_shape=[
+            shape((slots, frames, edge, edge), bf16),
+            shape((3 * slots,), jnp.int32),
+        ],
+        in_specs=[hbm_spec] * 3,
+        out_specs=[vmem_spec, smem_spec],
+        scratch_shapes=small + [pltpu.SemaphoreType.DMA((slots + 2,))],
+        compiler_params=params(8),
+        cost_estimate=pl.CostEstimate(
+            flops=0, transcendentals=0, bytes_accessed=4 * slots * frames * edge * edge
+        ),
+        name="load",
+    )(held(blocks), held(block_owner), held(cells))
+
+    def match(tables, infos):
         return pl.pallas_call(
-            functools.partial(load_kernel, [grid] + tables),
-            out_shape=[
-                shape((slots, frames, edge, edge), bf16),
-                shape((ta_count * slots + 2,), jnp.int32),
-            ],
-            in_specs=[hbm_spec] + [vmem_spec] * len(infos),
-            out_specs=[vmem_spec, smem_spec],
-            scratch_shapes=[pltpu.SemaphoreType.DMA((slots,))],
-            compiler_params=params(8),
-            cost_estimate=pl.CostEstimate(
-                flops=0, transcendentals=0, bytes_accessed=4 * slots * frames * edge * edge
-            ),
-            name="load",
-        )(held(blocks), *infos)
+            functools.partial(match_kernel, slots, grid, tables),
+            out_shape=shape((ta_count * slots + 2,), jnp.int32),
+            in_specs=[vmem_spec] * len(infos),
+            out_specs=smem_spec,
+            compiler_params=params(4),
+            name="match",
+        )(*infos)
 
     if swaps:
-        near, part, rest, table = pl.pallas_call(
+        near, part, rest = pl.pallas_call(
             pack_kernel,
             out_shape=[
                 shape((2 * half + info_rows, rank), bf16),
                 shape((2 * quarter + info_rows, rank), bf16),
                 shape((2 * half, rank), bf16),
-                shape((3 * slots,), jnp.int32),
             ],
             in_specs=[hbm_spec] * 4,
-            out_specs=[vmem_spec] * 3 + [smem_spec],
-            scratch_shapes=[
-                pltpu.SMEM(block_owner.shape, jnp.int32),
-                pltpu.SMEM(cells.shape, jnp.int32),
-                pltpu.SemaphoreType.DMA((8,)),
-            ],
+            out_specs=[vmem_spec] * 3,
+            scratch_shapes=small + [pltpu.SemaphoreType.DMA((8,))],
             compiler_params=params(4),
             name="pack",
         )(*(held(x) for x in (block_owner, cells, qz_factor, qy_factor)))
         first = swap(near, "ta", ta_count, 1)
-        away = jnp.concatenate([swap(part, "ta", ta_count, k) for k in range(2, ta_count)], axis=0)
-        first, away, blocks = lax.optimization_barrier((first, away, blocks))
-        short = 2 * quarter + info_rows
+        parts = [swap(part, "ta", ta_count, k) for k in range(2, ta_count)]
+        first, parts, cube, table = lax.optimization_barrier((first, parts, cube, table))
+        away = jnp.concatenate([x[: 2 * quarter] for x in parts], axis=0)
         tables = [(0, 2 * half), (1, 2 * half)]
-        tables += [(2, i * short + 2 * quarter) for i in range(ta_count - 2)]
-        both = jnp.concatenate([first, away], axis=0)
-        cube, found = load(blocks, tables, (near, first, away))
-        both, cube, found = lax.optimization_barrier((both, cube, found))
-        side_away, mate = lax.optimization_barrier(
-            (swap(away, "pb", pb_count, 2), swap(both, "pb", pb_count, 1))
+        tables += [(k, 2 * quarter) for k in range(2, ta_count)]
+        side_away, mate, found = lax.optimization_barrier(
+            (
+                swap(away, "pb", pb_count, 2),
+                swap(jnp.concatenate([first[: 2 * half], away]), "pb", pb_count, 1),
+                match(tables, (near, first, *parts)),
+            )
         )
         side_mate = swap(side_away, "pb", pb_count, 1)
         pieces = (near, rest, first, away, side_away, mate, side_mate)
         made = full
     else:
-        table = jnp.concatenate([block_owner.reshape(slots), cells.reshape(2 * slots)])
         pieces = (
             lax.all_gather(qz_factor, "ta", axis=0, tiled=True),
             lax.all_gather(qy_factor, "ta", axis=0, tiled=True),
@@ -407,7 +430,7 @@
         shown = shown.at[0, :slots].set(table[:slots] + 1)
         shown = shown.at[1:3, :slots].set(table[slots:].reshape(2, slots))
         info = lax.all_gather(shown.astype(bf16), "ta", axis=0, tiled=True)
-        cube, found = load(blocks, [(0, k * info_rows) for k in range(ta_count)], (info,))
+        found = match([(0, k * info_rows) for k in range(ta_count)], (info,))
     out = pl.pallas_call(
         functools.partial(term_kernel, edge, swaps),
         out_shape=[shape((ta_count * frames, rank), f32)] + made,
@@ -439,7 +462,7 @@
         compiler_params=params(16),
         name="system",
     )(found, full_z, full_y)
-    new_rows, low = pl.pallas_call(
+    kept, low = pl.pallas_call(
         functools.partial(solve_kernel, ta_count, swaps),
         out_shape=[shape((frames, rank), f32), shape((frames, rank), bf16)],
         in_specs=[vmem_spec] * 8,
@@ -452,15 +475,18 @@
         others = jnp.concatenate([swap(low, "ta", ta_count, k) for k in range(1, ta_count)], axis=0)
     else:
         others = lax.all_gather(low, "ta", axis=0, tiled=True)
-    misfit = pl.pallas_call(
+    misfit, new_rows = pl.pallas_call(
         functools.partial(misfit_kernel, ta_count, edge, swaps),
-        out_shape=shape((1, slots), f32),
-        in_specs=[smem_spec] + [vmem_spec] * 5,
-        out_specs=vmem_spec,
-        scratch_shapes=[pltpu.VMEM((ta_count, frames, rank), f32)],
+        out_shape=[shape((1, slots), f32), shape((frames, rank), f32)],
+        in_specs=[smem_spec] + [vmem_spec] * 6,
+        out_specs=[vmem_spec, hbm_spec],
+        scratch_shapes=[
+            pltpu.VMEM((ta_count, frames, rank), f32),
+            pltpu.SemaphoreType.DMA,
+        ],
         compiler_params=params(16),
         name="misfit",
-    )(table, low, others, full_z, full_y, cube)
+    )(table, low, others, full_z, full_y, cube, kept)
     return (new_rows, misfit.reshape(1, 1, slots))
 
 

time: 47.8 us -> 43.2 us (0.904)
  waiting for transfers between devices: 17.2 us -> 13.2 us
    ppermute x12, waiting for transfers between devices: 17.2 us -> 13.2 us  [swap(): return lax.ppermute(x, axis, [(i, i ^ k) for i in range(count)])]
    pallas_call x1 -> x2, Pallas kernels: 2.81 us -> 3.65 us  [the longest x1 2.82 us: body(): pl.pallas_call(load_kernel, out_shape=[shape((slots, frames, edge, edge),...]
    pallas_call x1, Pallas kernels: 1.15 us -> 0.54 us  [body(): pl.pallas_call(functools.partial(solve_kernel, ta_count, swaps), out_shap...]
    pallas_call x1, Pallas kernels: 1.64 us -> 1.05 us  [body(): pl.pallas_call(pack_kernel, out_shape=[shape((2 * half + info_rows, rank)...]
  transfers between devices with their start and end apart: 12 -> 12, of which waited for: 9 -> 8; matrix products, arithmetic and copies ran while one was open for 0% -> 0% of each run, Pallas kernels for 4% -> 13%
where the time goes in v7:
time: 43.2 us; the launch traced here: 43 us
  starting transfers between devices  15.3 us (35%)
  Pallas kernels  13.7 us (32%)
  waiting for transfers between devices  13.2 us (31%)
  between operations  0.75 us (2%)
    ppermute x12, starting transfers between devices, swap(): return lax.ppermute(x, axis, [(i, i ^ k) for i in range(count)])  15.3 us
    ppermute x12, waiting for transfers between devices, swap(): return lax.ppermute(x, axis, [(i, i ^ k) for i in range(count)])  13.2 us
    pallas_call x1, Pallas kernels, body(): pl.pallas_call(functools.partial(misfit_kernel, ta_count, edge, swaps), o...  3.57 us
    pallas_call x1, Pallas kernels, body(): pl.pallas_call(functools.partial(term_kernel, edge, swaps), out_shape=[sh...  2.95 us
    pallas_call x1, Pallas kernels, body(): pl.pallas_call(load_kernel, out_shape=[shape((slots, frames, edge, edge),...  2.82 us
    pallas_call x1, Pallas kernels, body(): pl.pallas_call(functools.partial(system_kernel, edge), out_shape=square,...  1.91 us
    pallas_call x1, Pallas kernels, body(): pl.pallas_call(pack_kernel, out_shape=[shape((2 * half + info_rows, rank)...  1.05 us
  transfers between devices with their start and end apart: 12, of which 8 were waited for; matrix products, arithmetic and copies ran while one was open for 0% of the time, Pallas kernels for 13%

profile of v7, /device:TPU:0, one launch (start us, length us, event | category | flops | bytes accessed | tf_op | source)
XLA Modules:
  0.0 43.0 jit_solution(14411632618521917678)
XLA Ops:
  0.6 1.1 %pack.1 = (bf16[264,256]{1,0:T(8,128)(2,1)S(1)}, bf16[136,256]{1,0:T(8,128)(2,1)S(1)}, bf16[256,256]{1,0:T(8,128)(2,1)S(1)}) custom-call(s32[1,1,4]{2,1,0:T(1,128)} %owner_hbm.3, s32[1,1,2,4]{3,2,1,0:T(2,128)} %bitcast.2, bf16[256,256]{1,0:T(8,128)(2,1)} %z_hbm.1, bf16[256,256]{1,0:T(8,128)(2,1)} %y_hbm.1), custom_call_target="tpu_custom_call" | custom-call | tf_op jit(solution)/shard_map/pack/pallas_call | solution.py:394
  1.7 3.1 %collective-permute-start = (bf16[264,256]{1,0:T(8,128)(2,1)S(1)}, bf16[264,256]{1,0:T(8,128)(2,1)S(1)}, u32[]{:S(2)}, u32[]{:S(2)}) collective-permute-start(bf16[264,256]{1,0:T(8,128)(2,1)S(1)} %get-tuple-element.28.refs_0_), channel_id=1, source_target_pairs={{0,4},{4,0},{8,12},{12,8},{1,5},{5,1},{9,13},{13,9},{2,6},{6,2},{1... | collective-permute-start | bytes 405512 | tf_op jit(solution)/shard_map/ppermute | solution.py:348
  4.8 2.5 %collective-permute-start.2 = (bf16[136,256]{1,0:T(8,128)(2,1)S(1)}, bf16[136,256]{1,0:T(8,128)(2,1)S(1)}, u32[]{:S(2)}, u32[]{:S(2)}) collective-permute-start(bf16[136,256]{1,0:T(8,128)(2,1)S(1)} %get-tuple-element.29), channel_id=1, source_target_pairs={{0,12},{4,8},{8,4},{12,0},{1,13},{5,9},{9,5},{13,1},{2,14},{6,10},... | collective-permute-start | bytes 208904 | tf_op jit(solution)/shard_map/ppermute | solution.py:348
  7.3 0.1 collective-permute-start.1
  7.4 2.8 %load.1 = (bf16[4,32,128,128]{3,2,1,0:T(8,128)(2,1)S(1)}, s32[12]{0:T(128)S(1)}) custom-call(bf16[1,1,4,32,128,128]{5,4,3,2,1,0:T(8,128)(2,1)} %blocks.1, s32[1,1,4]{2,1,0:T(1,128)} %owner_hbm.3, s32[1,1,2,4]{3,2,1,0:T(2,128)} %bitcast.3), custom_call_target="tpu_custom_call" | custom-call | bytes 8388608 | tf_op jit(solution)/shard_map/load/pallas_call | solution.py:367
  10.2 2.7 %collective-permute-done.2.refs_3_ = bf16[136,256]{1,0:T(8,128)(2,1)S(1)} collective-permute-done((bf16[136,256]{1,0:T(8,128)(2,1)S(1)}, bf16[136,256]{1,0:T(8,128)(2,1)S(1)}, u32[]{:S(2)}, u32[]{:S(2)}) %collective-permute-start.2) | collective-permute-done | bytes 69664 | tf_op jit(solution)/shard_map/ppermute | solution.py:348
  12.9 1.4 %collective-permute-done.1.refs_2_ = bf16[136,256]{1,0:T(8,128)(2,1)S(1)} collective-permute-done((bf16[136,256]{1,0:T(8,128)(2,1)S(1)}, bf16[136,256]{1,0:T(8,128)(2,1)S(1)}, u32[]{:S(2)}, u32[]{:S(2)}) %collective-permute-start.1) | collective-permute-done | bytes 69664 | tf_op jit(solution)/shard_map/ppermute | solution.py:348
  14.3 0.0 collective-permute-done.refs_1_.refs_2_
  14.4 0.1 collective-permute-start.4
  14.5 1.6 %collective-permute-start.3 = (bf16[256,256]{1,0:T(8,128)(2,1)S(1)}, bf16[256,256]{1,0:T(8,128)(2,1)S(1)}, u32[]{:S(2)}, u32[]{:S(2)}) collective-permute-start(bf16[256,256]{1,0:T(8,128)(2,1)S(1)} %pad_maximum_fusion.1.refs_3_), channel_id=1, source_target_pairs={{0,2},{1,3},{2,0},{3,1},{4,6},{5,7},{6,4},{7,5},{8,10},{9,11},{10,... | collective-permute-start | bytes 393224 | tf_op jit(solution)/shard_map/ppermute | solution.py:348
  16.0 0.8 %match.1.found = s32[18]{0:T(128)S(1)} custom-call(bf16[264,256]{1,0:T(8,128)(2,1)S(1)} %get-tuple-element.28.refs_0_, bf16[264,256]{1,0:T(8,128)(2,1)S(1)} %collective-permute-done.refs_1_.refs_2_, bf16[136,256]{1,0:T(8,128)(2,1)S(1)} %collective-permute-done.1.refs_2_, bf16[136,256]{1,0:T(8,128)(2,1)S(1)} %collective-permute-done.2.refs_3_), custom_call_target="tpu_custom_call" | custom-call | tf_op jit(solution)/shard_map/match/pallas_call | solution.py:384
  16.9 3.6 %collective-permute-done.3.refs_4_ = bf16[256,256]{1,0:T(8,128)(2,1)S(1)} collective-permute-done((bf16[256,256]{1,0:T(8,128)(2,1)S(1)}, bf16[256,256]{1,0:T(8,128)(2,1)S(1)}, u32[]{:S(2)}, u32[]{:S(2)}) %collective-permute-start.3) | collective-permute-done | bytes 131104 | tf_op jit(solution)/shard_map/ppermute | solution.py:348
  20.4 0.0 collective-permute-done.4.refs_5_
  20.4 0.0 collective-permute-start.5
  20.4 1.3 %collective-permute-done.5.refs_6_ = bf16[256,256]{1,0:T(8,128)(2,1)S(1)} collective-permute-done((bf16[256,256]{1,0:T(8,128)(2,1)S(1)}, bf16[256,256]{1,0:T(8,128)(2,1)S(1)}, u32[]{:S(2)}, u32[]{:S(2)}) %collective-permute-start.5) | collective-permute-done | bytes 131104 | tf_op jit(solution)/shard_map/ppermute | solution.py:348
  21.8 2.9 %terms.1 = (f32[128,256]{1,0:T(8,128)S(1)}, bf16[1024,256]{1,0:T(8,128)(2,1)S(1)}, bf16[1024,256]{1,0:T(8,128)(2,1)S(1)}) custom-call(s32[12]{0:T(128)S(1)} %get-tuple-element.32.table, bf16[4,32,128,128]{3,2,1,0:T(8,128)(2,1)S(1)} %get-tuple-element.33.cube, bf16[264,256]{1,0:T(8,128)(2,1)S(1)} %get-tuple-element.28.refs_0_, ...), custom_call_target="tpu_custom_call" | custom-call | tf_op jit(solution)/shard_map/terms/pallas_call | solution.py:434
  24.8 0.1 collective-permute-start.6
  24.8 2.3 %collective-permute-start.8 = (f32[32,256]{1,0:T(8,128)S(1)}, f32[32,256]{1,0:T(8,128)S(1)}, u32[]{:S(2)}, u32[]{:S(2)}) collective-permute-start(f32[32,256]{1,0:T(8,128)S(1)} %get-tuple-element.55), channel_id=1, source_target_pairs={{0,12},{4,8},{8,4},{12,0},{1,13},{5,9},{9,5},{13,1},{2,14},{6,10},... | collective-permute-start | bytes 98312 | tf_op jit(solution)/shard_map/ppermute | solution.py:348
  27.1 1.2 %collective-permute-start.7 = (f32[32,256]{1,0:T(8,128)S(1)}, f32[32,256]{1,0:T(8,128)S(1)}, u32[]{:S(2)}, u32[]{:S(2)}) collective-permute-start(f32[32,256]{1,0:T(8,128)S(1)} %get-tuple-element.56), channel_id=1, source_target_pairs={{0,8},{4,12},{8,0},{12,4},{1,9},{5,13},{9,1},{13,5},{2,10},{6,14},... | collective-permute-start | bytes 98312 | tf_op jit(solution)/shard_map/ppermute | solution.py:348
  28.3 1.9 %system.1 = (f32[256,256]{1,0:T(8,128)S(1)}, bf16[256,256]{1,0:T(8,128)(2,1)S(1)}, bf16[256,256]{1,0:T(8,128)(2,1)S(1)}, bf16[256,256]{1,0:T(8,128)(2,1)S(1)}, b...) custom-call(s32[18]{0:T(128)S(1)} %match.1.found, bf16[1024,256]{1,0:T(8,128)(2,1)S(1)} %get-tuple-element.42.full_z, ...), custom_call_target="tpu_custom_call" | custom-call | tf_op jit(solution)/shard_map/system/pallas_call | solution.py:456
  30.2 0.0 collective-permute-done.6
  30.2 0.4 collective-permute-done.8
  30.6 1.3 %collective-permute-done.7 = f32[32,256]{1,0:T(8,128)S(1)} collective-permute-done((f32[32,256]{1,0:T(8,128)S(1)}, f32[32,256]{1,0:T(8,128)S(1)}, u32[]{:S(2)}, u32[]{:S(2)}) %collective-permute-start.7) | collective-permute-done | bytes 32800 | tf_op jit(solution)/shard_map/ppermute | solution.py:348
  32.0 0.5 %solve.1 = (f32[32,256]{1,0:T(8,128)S(1)}, bf16[32,256]{1,0:T(8,128)(2,1)S(1)}) custom-call(f32[128,256]{1,0:T(8,128)S(1)} %get-tuple-element.40.own, f32[96,256]{1,0:T(8,128)S(1)} %pad_maximum_fusion.2.far, f32[256,256]{1,0:T(8,128)S(1)} %get-tuple-element.44.system, bf16[256,256]{1,0:T(8,128)(2,1)S(1)} %get-tuple-element.45.high, ...), custom_call_target="tpu_custom_call" | custom-call | tf_op jit(solution)/shard_map/solve/pallas_call | solution.py:465
  32.5 2.3 %collective-permute-start.11 = (bf16[32,256]{1,0:T(8,128)(2,1)S(1)}, bf16[32,256]{1,0:T(8,128)(2,1)S(1)}, u32[]{:S(2)}, u32[]{:S(2)}) collective-permute-start(bf16[32,256]{1,0:T(8,128)(2,1)S(1)} %get-tuple-element.50.low), channel_id=1, source_target_pairs={{0,12},{4,8},{8,4},{12,0},{1,13},{5,9},{9,5},{13,1},{2,14},{6,10},... | collective-permute-start | bytes 49160 | tf_op jit(solution)/shard_map/ppermute | solution.py:348
  34.8 0.3 collective-permute-start.10
  35.1 1.9 %collective-permute-start.9 = (bf16[32,256]{1,0:T(8,128)(2,1)S(1)}, bf16[32,256]{1,0:T(8,128)(2,1)S(1)}, u32[]{:S(2)}, u32[]{:S(2)}) collective-permute-start(bf16[32,256]{1,0:T(8,128)(2,1)S(1)} %get-tuple-element.50.low), channel_id=1, source_target_pairs={{0,4},{4,0},{8,12},{12,8},{1,5},{5,1},{9,13},{13,9},{2,6},{6,2},{1... | collective-permute-start | bytes 49160 | tf_op jit(solution)/shard_map/ppermute | solution.py:348
  36.9 1.1 %collective-permute-done.11 = bf16[32,256]{1,0:T(8,128)(2,1)S(1)} collective-permute-done((bf16[32,256]{1,0:T(8,128)(2,1)S(1)}, bf16[32,256]{1,0:T(8,128)(2,1)S(1)}, u32[]{:S(2)}, u32[]{:S(2)}) %collective-permute-start.11) | collective-permute-done | bytes 16416 | tf_op jit(solution)/shard_map/ppermute | solution.py:348
  38.1 1.3 %collective-permute-done.10 = bf16[32,256]{1,0:T(8,128)(2,1)S(1)} collective-permute-done((bf16[32,256]{1,0:T(8,128)(2,1)S(1)}, bf16[32,256]{1,0:T(8,128)(2,1)S(1)}, u32[]{:S(2)}, u32[]{:S(2)}) %collective-permute-start.10) | collective-permute-done | bytes 16416 | tf_op jit(solution)/shard_map/ppermute | solution.py:348
  39.4 0.0 collective-permute-done.9
  39.4 3.6 %misfit.1 = (f32[1,4]{1,0:T(1,128)}, f32[32,256]{1,0:T(8,128)}) custom-call(s32[12]{0:T(128)S(1)} %get-tuple-element.32.table, bf16[32,256]{1,0:T(8,128)(2,1)S(1)} %get-tuple-element.50.low, bf16[96,256]{1,0:T(8,128)(2,1)S(1)} %pad_maximum_fusion.3.far, bf16[1024,256]{1,0:T(8,128)(2,1)S(1)} %get-tuple-element.42.full_z, ...), custom_call_target="tpu_custom_call" | custom-call | tf_op jit(solution)/shard_map/misfit/pallas_call | solution.py:478
  (8 shorter events, 0.1 us)
Async XLA Ops:
  1.7 12.6 %collective-permute-start = (bf16[264,256]{1,0:T(8,128)(2,1)S(1)}, bf16[264,256]{1,0:T(8,128)(2,1)S(1)}, u32[]{:S(2)}, u32[]{:S(2)}) collective-permute-start(bf16[264,256]{1,0:T(8,128)(2,1)S(1)} %get-tuple-element.28.refs_0_), channel_id=1, source_target_pairs={{0,4},{4,0},{8,12},{12,8},{1,5},{5,1},{9,13},{13,9},{2,6},{6,2},{1... | collective-permute-start | bytes 405512 | tf_op jit(solution)/shard_map/ppermute | solution.py:348
  4.8 8.1 %collective-permute-start.2 = (bf16[136,256]{1,0:T(8,128)(2,1)S(1)}, bf16[136,256]{1,0:T(8,128)(2,1)S(1)}, u32[]{:S(2)}, u32[]{:S(2)}) collective-permute-start(bf16[136,256]{1,0:T(8,128)(2,1)S(1)} %get-tuple-element.29), channel_id=1, source_target_pairs={{0,12},{4,8},{8,4},{12,0},{1,13},{5,9},{9,5},{13,1},{2,14},{6,10},... | collective-permute-start | bytes 208904 | tf_op jit(solution)/shard_map/ppermute | solution.py:348
  7.3 7.0 %collective-permute-start.1 = (bf16[136,256]{1,0:T(8,128)(2,1)S(1)}, bf16[136,256]{1,0:T(8,128)(2,1)S(1)}, u32[]{:S(2)}, u32[]{:S(2)}) collective-permute-start(bf16[136,256]{1,0:T(8,128)(2,1)S(1)} %get-tuple-element.29), channel_id=1, source_target_pairs={{0,8},{4,12},{8,0},{12,4},{1,9},{5,13},{9,1},{13,5},{2,10},{6,14},... | collective-permute-start | bytes 208904 | tf_op jit(solution)/shard_map/ppermute | solution.py:348
  14.4 6.1 %collective-permute-start.4 = (bf16[512,256]{1,0:T(8,128)(2,1)S(1)}, bf16[512,256]{1,0:T(8,128)(2,1)S(1)}, u32[]{:S(2)}, u32[]{:S(2)}) collective-permute-start(bf16[512,256]{1,0:T(8,128)(2,1)S(1)} %pad_maximum_fusion), channel_id=1, source_target_pairs={{0,1},{1,0},{2,3},{3,2},{4,5},{5,4},{6,7},{7,6},{8,9},{9,8},{10,11... | collective-permute-start | bytes 786440 | tf_op jit(solution)/shard_map/ppermute | solution.py:348
  14.5 6.0 %collective-permute-start.3 = (bf16[256,256]{1,0:T(8,128)(2,1)S(1)}, bf16[256,256]{1,0:T(8,128)(2,1)S(1)}, u32[]{:S(2)}, u32[]{:S(2)}) collective-permute-start(bf16[256,256]{1,0:T(8,128)(2,1)S(1)} %pad_maximum_fusion.1.refs_3_), channel_id=1, source_target_pairs={{0,2},{1,3},{2,0},{3,1},{4,6},{5,7},{6,4},{7,5},{8,10},{9,11},{10,... | collective-permute-start | bytes 393224 | tf_op jit(solution)/shard_map/ppermute | solution.py:348
  20.4 1.3 %collective-permute-start.5 = (bf16[256,256]{1,0:T(8,128)(2,1)S(1)}, bf16[256,256]{1,0:T(8,128)(2,1)S(1)}, u32[]{:S(2)}, u32[]{:S(2)}) collective-permute-start(bf16[256,256]{1,0:T(8,128)(2,1)S(1)} %collective-permute-done.3.refs_4_), channel_id=1, source_target_pairs={{0,1},{1,0},{2,3},{3,2},{4,5},{5,4},{6,7},{7,6},{8,9},{9,8},{10,11... | collective-permute-start | bytes 393224 | tf_op jit(solution)/shard_map/ppermute | solution.py:348
  24.8 5.5 %collective-permute-start.6 = (f32[32,256]{1,0:T(8,128)S(1)}, f32[32,256]{1,0:T(8,128)S(1)}, u32[]{:S(2)}, u32[]{:S(2)}) collective-permute-start(f32[32,256]{1,0:T(8,128)S(1)} %get-tuple-element.54), channel_id=1, source_target_pairs={{0,4},{4,0},{8,12},{12,8},{1,5},{5,1},{9,13},{13,9},{2,6},{6,2},{1... | collective-permute-start | bytes 98312 | tf_op jit(solution)/shard_map/ppermute | solution.py:348
  24.8 5.8 %collective-permute-start.8 = (f32[32,256]{1,0:T(8,128)S(1)}, f32[32,256]{1,0:T(8,128)S(1)}, u32[]{:S(2)}, u32[]{:S(2)}) collective-permute-start(f32[32,256]{1,0:T(8,128)S(1)} %get-tuple-element.55), channel_id=1, source_target_pairs={{0,12},{4,8},{8,4},{12,0},{1,13},{5,9},{9,5},{13,1},{2,14},{6,10},... | collective-permute-start | bytes 98312 | tf_op jit(solution)/shard_map/ppermute | solution.py:348
  27.1 4.8 %collective-permute-start.7 = (f32[32,256]{1,0:T(8,128)S(1)}, f32[32,256]{1,0:T(8,128)S(1)}, u32[]{:S(2)}, u32[]{:S(2)}) collective-permute-start(f32[32,256]{1,0:T(8,128)S(1)} %get-tuple-element.56), channel_id=1, source_target_pairs={{0,8},{4,12},{8,0},{12,4},{1,9},{5,13},{9,1},{13,5},{2,10},{6,14},... | collective-permute-start | bytes 98312 | tf_op jit(solution)/shard_map/ppermute | solution.py:348
  32.5 5.6 %collective-permute-start.11 = (bf16[32,256]{1,0:T(8,128)(2,1)S(1)}, bf16[32,256]{1,0:T(8,128)(2,1)S(1)}, u32[]{:S(2)}, u32[]{:S(2)}) collective-permute-start(bf16[32,256]{1,0:T(8,128)(2,1)S(1)} %get-tuple-element.50.low), channel_id=1, source_target_pairs={{0,12},{4,8},{8,4},{12,0},{1,13},{5,9},{9,5},{13,1},{2,14},{6,10},... | collective-permute-start | bytes 49160 | tf_op jit(solution)/shard_map/ppermute | solution.py:348
  34.8 4.6 %collective-permute-start.10 = (bf16[32,256]{1,0:T(8,128)(2,1)S(1)}, bf16[32,256]{1,0:T(8,128)(2,1)S(1)}, u32[]{:S(2)}, u32[]{:S(2)}) collective-permute-start(bf16[32,256]{1,0:T(8,128)(2,1)S(1)} %get-tuple-element.50.low), channel_id=1, source_target_pairs={{0,8},{4,12},{8,0},{12,4},{1,9},{5,13},{9,1},{13,5},{2,10},{6,14},... | collective-permute-start | bytes 49160 | tf_op jit(solution)/shard_map/ppermute | solution.py:348
  35.1 4.4 %collective-permute-start.9 = (bf16[32,256]{1,0:T(8,128)(2,1)S(1)}, bf16[32,256]{1,0:T(8,128)(2,1)S(1)}, u32[]{:S(2)}, u32[]{:S(2)}) collective-permute-start(bf16[32,256]{1,0:T(8,128)(2,1)S(1)} %get-tuple-element.50.low), channel_id=1, source_target_pairs={{0,4},{4,0},{8,12},{12,8},{1,5},{5,1},{9,13},{13,9},{2,6},{6,2},{1... | collective-permute-start | bytes 49160 | tf_op jit(solution)/shard_map/ppermute | solution.py:348
